TPU v7x, 1024 devices: a whole 8x8x8 slice. The times are simulated.
1024 devices in a mesh: wide: 32 (over x_hi, z), sec: 8 (over y), tile: 4 (over x_lo, core).
Axes of the slice: x: 8 (x_hi: 4, x_lo: 2; x = x_hi * 2 + x_lo), y: 8, z: 8, core: 2. Of those that a mesh axis runs over, the one named last changes fastest.
Arguments:
- velocity: float32 [3, 128, 64, 1024], P(None, 'wide', 'tile', 'sec'), may hold values from -0.4 to 0.4
- viscosity: float32 [128, 64, 1024], P('wide', 'tile', 'sec'), may hold values from 0.01 to 0.08
- counts: int32 [32, 8, 4], P('wide', 'sec', 'tile'), may hold values from 2 to 4, as said below
- destination: int32 [32, 8, 4, 4], P('wide', 'sec', 'tile'), may hold values from 0 to 3, as said below
- seeds: int32 [32, 8, 4, 4, 3, 128], P('wide', 'sec', 'tile'), may hold values from 0 to 127, as said below
- substeps: int32 [32, 8, 4, 4, 128], P('wide', 'sec', 'tile'), may hold values from 0 to 1
Outputs:
- new_velocity: float32 [3, 128, 64, 1024], P(None, 'wide', 'tile', 'sec')
- traced_blocks: float32 [32, 8, 4, 8, 3, 128], P('wide', 'sec', 'tile')
Inputs may be any that keep to these rules, and one draw needn't show every extreme that they name: Blocks 0 to counts - 1 of a device are live; some device has all 4 live. `destination`: among a device's live blocks at most 2 name any one tile, and exactly 2 name the tile that all devices with the same wide and sec index share. `seeds`: components 0, 1, 2 lie below 4, 16, 128.
All inputs are finite; a program needn't handle non-finite values.
Results may differ from a plain program's by a relative error of at most 0.0003.
Values sent between devices are 32-bit elements; how exact they have to be, the bound alone decides.
No kernel may reach another device: no remote copies, remote signals or barrier semaphores. Data moves between devices by JAX's collectives and lax.ppermute only.
A program may use at most 64 MiB of HBM per device.

v0:
```python
from functools import partial

import jax
import jax.numpy as jnp
from jax import lax
from jax.sharding import PartitionSpec as P

CAP = 2


flow_step = 0.2
trace_step = 1.25


def extended_2(block, sides, width):
    for axis, dim in sides:
        count = lax.axis_size(axis)
        forward = [(i, i + 1) for i in range(count - 1)]
        forward.append((count - 1, 0))
        backward = [(target, source) for source, target in forward]
        low = lax.ppermute(
            lax.slice_in_dim(block, block.shape[dim] - width, None, axis=dim), axis, forward
        )
        high = lax.ppermute(lax.slice_in_dim(block, 0, width, axis=dim), axis, backward)
        block = jnp.concatenate([low, block, high], axis=dim)
    return block


def neighbor(padded, dimension, offset):
    window = [slice(None), slice(1, -1), slice(1, -1), slice(1, -1)]
    length = padded.shape[dimension]
    window[dimension] = slice(1 + offset, length - 1 + offset)
    return padded[tuple(window)]


def advance(padded, viscous):
    centre = padded[:, 1:-1, 1:-1, 1:-1]
    spread = jnp.zeros_like(centre)
    laplace = jnp.zeros_like(centre)
    for component in range(3):
        dimension = component + 1
        upper_cell = neighbor(padded, dimension, 1)
        lower_cell = neighbor(padded, dimension, -1)
        flux_up = 0.25 * (centre + upper_cell) * (centre[component] + upper_cell[component])
        flux_down = 0.25 * (lower_cell + centre) * (lower_cell[component] + centre[component])
        spread = spread + (flux_up - flux_down)
        laplace = laplace + (upper_cell + lower_cell)
    laplace = laplace - 6.0 * centre
    return centre + flow_step * (viscous * laplace - spread)


def runge_kutta(offset, sampler):
    section_one = sampler(offset)
    section_two = sampler(0.5 * trace_step * section_one)
    section_three = sampler(0.5 * trace_step * section_two)
    section_four = sampler(trace_step * section_three)
    return trace_step / 6.0 * (section_one + 2.0 * section_two + 2.0 * section_three + section_four)


def march(offset, steps_float, sampler):
    moved_off = runge_kutta(offset, sampler)
    offset = jnp.where(0 < steps_float, moved_off, offset)
    return offset


def local_sampler(table, size_y, size_z, corner_base, box_offset, cells, offset):
    lowest = jnp.floor(offset)
    fraction = offset - lowest
    corner = cells + lowest.astype(jnp.int32) - corner_base
    linear_list = []
    weight_list = []
    for step_x in range(2):
        weight_x = fraction[0] if step_x else 1.0 - fraction[0]
        for step_y in range(2):
            weight_y = fraction[1] if step_y else 1.0 - fraction[1]
            for step_z in range(2):
                weight_z = fraction[2] if step_z else 1.0 - fraction[2]
                linear = (
                    ((corner[0] + step_x) * size_y + corner[1] + step_y) * size_z
                    + corner[2]
                    + step_z
                    + box_offset
                )
                linear_list.append(linear)
                weight_list.append(weight_x * weight_y * weight_z)
    linear_all = jnp.stack(linear_list)
    weight_all = jnp.stack(weight_list)
    point_total = offset.shape[1]
    values = jnp.take(table, linear_all.reshape(-1), axis=1).reshape(3, 8, point_total)
    return jnp.sum(values * weight_all[None], 1)


def wall_mask(field, depth, rows_y, tile_pos, total_y):
    global_rows = tile_pos * rows_y + jnp.arange(rows_y + 2 * depth, dtype=jnp.int32) - depth
    keeping = (global_rows >= 0) & (global_rows < total_y)
    return jnp.where(keeping[None, None, :, None], field, 0.0)


def shards(velocity, viscosity, counts, destination, seeds, substeps):
    rows_x = velocity.shape[1]
    rows_y = velocity.shape[2]
    rows_z = velocity.shape[3]
    tile_count = lax.axis_size("tile")
    tile_pos = lax.axis_index("tile")
    wide_pos = lax.axis_index("wide")
    sec_pos = lax.axis_index("sec")
    total_y = rows_y * tile_count
    padded = extended_2(velocity, (("wide", 1), ("sec", 3), ("tile", 2)), 1)
    padded = wall_mask(padded, 1, rows_y, tile_pos, total_y)
    fresh_vel = advance(padded, viscosity)
    extended = extended_2(fresh_vel, (("wide", 1), ("sec", 3), ("tile", 2)), 1)
    extended = wall_mask(extended, 1, rows_y, tile_pos, total_y)
    size_y = rows_y + 2
    size_z = rows_z + 2
    block_count = destination.shape[3]
    point_count = seeds.shape[5]
    is_live = jnp.arange(block_count, dtype=jnp.int32) < counts[0, 0, 0]
    target = destination[0, 0, 0]
    onehot = (
        (target[:, None] == jnp.arange(tile_count, dtype=jnp.int32)[None, :]) & is_live[:, None]
    ).astype(jnp.int32)
    order_rank = jnp.sum(onehot * (jnp.cumsum(onehot, 0) - onehot), 1)
    slot_count = CAP * tile_count
    slot_index = target * CAP + order_rank
    placing = (
        (slot_index[None, :] == jnp.arange(slot_count, dtype=jnp.int32)[:, None]) & is_live[None, :]
    ).astype(jnp.float32)
    anchor = jnp.stack(
        [
            jnp.full_like(target, wide_pos * rows_x),
            target * rows_y,
            jnp.full_like(target, sec_pos * rows_z),
        ],
        1,
    )
    start_cell = seeds[0, 0, 0] + anchor[:, :, None]
    steps_float = substeps[0, 0, 0].astype(jnp.float32)
    payload = jnp.concatenate([start_cell.astype(jnp.float32), steps_float[:, None, :]], 1)
    sending = jnp.dot(
        placing,
        payload.reshape(block_count, -1),
        precision=lax.Precision.HIGHEST,
        preferred_element_type=jnp.float32,
    )
    sending = sending.reshape(tile_count, CAP, 4, point_count)
    table = extended.reshape(3, -1)
    corner_base = jnp.stack([wide_pos * rows_x - 1, tile_pos * rows_y - 1, sec_pos * rows_z - 1])[
        :, None
    ]
    centre_cell = jnp.stack([wide_pos * rows_x, tile_pos * rows_y, sec_pos * rows_z]).astype(
        jnp.float32
    )[:, None]
    received = lax.all_to_all(sending, "tile", split_axis=0, concat_axis=0, tiled=True)
    source_count = received.shape[0]
    item_count = received.shape[1]
    gathered_cells = jnp.transpose(received[:, :, :3], (2, 0, 1, 3)).reshape(3, -1)
    steps_here = received[:, :, 3].reshape(-1)
    active = steps_here > 0.0
    safe_cells = jnp.where(active[None], gathered_cells, centre_cell).astype(jnp.int32)
    offset = jnp.zeros(safe_cells.shape, jnp.float32)
    moved_off = march(
        offset,
        steps_here,
        partial(local_sampler, table, size_y, size_z, corner_base, 0, safe_cells),
    )
    moved_off = jnp.where(active[None], moved_off, 0.0)
    arrived = jnp.transpose(
        moved_off.reshape(3, source_count, item_count, point_count), (1, 2, 0, 3)
    )
    result = arrived.reshape(slot_count, 3, point_count)
    return (fresh_vel, result[None, None, None])


def solution(mesh):
    in_specs = (
        P(None, "wide", "tile", "sec"),
        P("wide", "tile", "sec"),
        P("wide", "sec", "tile"),
        P("wide", "sec", "tile", None),
        P("wide", "sec", "tile", None, None, None),
        P("wide", "sec", "tile", None, None),
    )
    out_specs = (P(None, "wide", "tile", "sec"), P("wide", "sec", "tile", None, None, None))
    return jax.shard_map(shards, mesh=mesh, in_specs=in_specs, out_specs=out_specs, check_vma=False)
```

profile of v0, /device:TPU:1, one launch (start us, length us, event | category | flops | bytes accessed | tf_op | source)
XLA Modules:
  0.0 276.9 jit_solution(10569149950708730318)
XLA Ops:
  6.7 17.3 %all-to-all-start = ((f32[4,2,4,128]{3,2,1,0:T(4,128)}), f32[4,2,4,128]{3,2,1,0:T(4,128)S(1)}, u32[]{:S(2)}, u32[]{:S(2)}) async-start(f32[4,2,4,128]{3,2,1,0:T(4,128)} %copy.210), calls=%async_computation | async-start | bytes 32768 | tf_op jit(solution)/shard_map/all_to_all | solution.py:153
  24.8 7.6 %collective-permute-start.1 = (f32[3,1,16,128]{3,2,1,0:T(8,128)S(1)}, f32[3,1,16,128]{3,2,1,0:T(8,128)S(1)}, u32[]{:S(2)}, u32[]{:S(2)}) collective-permute-start(f32[3,1,16,128]{3,2,1,0:T(8,128)S(1)} %get-tuple-element.57), channel_id=1, source_target_pairs={{32,0},{64,32},{96,64},{128,96},{160,128},{192,160},{224,192},{256... | collective-permute-start | bytes 73736 | tf_op jit(solution)/shard_map/ppermute | solution.py:24
  34.8 6.3 %collective-permute-done = f32[3,1,16,128]{3,2,1,0:T(8,128)S(1)} collective-permute-done((f32[3,1,16,128]{3,2,1,0:T(8,128)S(1)}, f32[3,1,16,128]{3,2,1,0:T(8,128)S(1)}, u32[]{:S(2)}, u32[]{:S(2)}) %collective-permute-start) | collective-permute-done | bytes 24608 | tf_op jit(solution)/shard_map/ppermute | solution.py:21
  42.2 3.3 %collective-permute-start.2 = (f32[3,6,16,1]{3,2,1,0:T(8,128)S(1)}, f32[3,6,16,1]{3,2,1,0:T(8,128)S(1)}, u32[]{:S(2)}, u32[]{:S(2)}) collective-permute-start(f32[3,6,16,1]{3,2,1,0:T(8,128)S(1)} %get-tuple-element.53), channel_id=1, source_target_pairs={{0,4},{4,8},{8,12},{12,16},{16,20},{20,24},{24,28},{28,0},{1,5},{5... | collective-permute-start | bytes 3464 | tf_op jit(solution)/shard_map/ppermute | solution.py:21
  45.5 4.5 %collective-permute-start.3 = (f32[3,6,16,1]{3,2,1,0:T(8,128)S(1)}, f32[3,6,16,1]{3,2,1,0:T(8,128)S(1)}, u32[]{:S(2)}, u32[]{:S(2)}) collective-permute-start(f32[3,6,16,1]{3,2,1,0:T(8,128)S(1)} %get-tuple-element.54), channel_id=1, source_target_pairs={{4,0},{8,4},{12,8},{16,12},{20,16},{24,20},{28,24},{0,28},{5,1},{9... | collective-permute-start | bytes 3464 | tf_op jit(solution)/shard_map/ppermute | solution.py:24
  52.3 5.8 %collective-permute-start.4 = (f32[3,6,1,130]{3,2,1,0:T(1,128)S(1)}, f32[3,6,1,130]{3,2,1,0:T(1,128)S(1)}, u32[]{:S(2)}, u32[]{:S(2)}) collective-permute-start(f32[3,6,1,130]{3,2,1,0:T(1,128)S(1)} %get-tuple-element.49), channel_id=1, source_target_pairs={{0,1},{1,2},{2,3},{3,0},{4,5},{5,6},{6,7},{7,4},{8,9},{9,10},{10,1... | collective-permute-start | bytes 28088 | tf_op jit(solution)/shard_map/ppermute | solution.py:21
  60.1 3.1 %collective-permute-done.5 = f32[3,6,1,130]{3,2,1,0:T(1,128)S(1)} collective-permute-done((f32[3,6,1,130]{3,2,1,0:T(1,128)S(1)}, f32[3,6,1,130]{3,2,1,0:T(1,128)S(1)}, u32[]{:S(2)}, u32[]{:S(2)}) %collective-permute-start.5) | collective-permute-done | bytes 9392 | tf_op jit(solution)/shard_map/ppermute | solution.py:24
  66.6 7.6 %collective-permute-start.7 = (f32[3,1,16,128]{3,2,1,0:T(8,128)S(1)}, f32[3,1,16,128]{3,2,1,0:T(8,128)S(1)}, u32[]{:S(2)}, u32[]{:S(2)}) collective-permute-start(f32[3,1,16,128]{3,2,1,0:T(8,128)S(1)} %get-tuple-element.56), channel_id=1, source_target_pairs={{32,0},{64,32},{96,64},{128,96},{160,128},{192,160},{224,192},{256... | collective-permute-start | bytes 73736 | tf_op jit(solution)/shard_map/ppermute | solution.py:24
  75.2 3.2 %collective-permute-start.8 = (f32[3,6,16,1]{3,2,1,0:T(8,128)S(1)}, f32[3,6,16,1]{3,2,1,0:T(8,128)S(1)}, u32[]{:S(2)}, u32[]{:S(2)}) collective-permute-start(f32[3,6,16,1]{3,2,1,0:T(8,128)S(1)} %get-tuple-element.51), channel_id=1, source_target_pairs={{0,4},{4,8},{8,12},{12,16},{16,20},{20,24},{24,28},{28,0},{1,5},{5... | collective-permute-start | bytes 3464 | tf_op jit(solution)/shard_map/ppermute | solution.py:21
  78.4 4.0 %collective-permute-start.9 = (f32[3,6,16,1]{3,2,1,0:T(8,128)S(1)}, f32[3,6,16,1]{3,2,1,0:T(8,128)S(1)}, u32[]{:S(2)}, u32[]{:S(2)}) collective-permute-start(f32[3,6,16,1]{3,2,1,0:T(8,128)S(1)} %get-tuple-element.52), channel_id=1, source_target_pairs={{4,0},{8,4},{12,8},{16,12},{20,16},{24,20},{28,24},{0,28},{5,1},{9... | collective-permute-start | bytes 3464 | tf_op jit(solution)/shard_map/ppermute | solution.py:24
  91.7 2.9 %collective-permute-done.11 = f32[3,6,1,130]{3,2,1,0:T(1,128)S(1)} collective-permute-done((f32[3,6,1,130]{3,2,1,0:T(1,128)S(1)}, f32[3,6,1,130]{3,2,1,0:T(1,128)S(1)}, u32[]{:S(2)}, u32[]{:S(2)}) %collective-permute-start.11) | collective-permute-done | bytes 9392 | tf_op jit(solution)/shard_map/ppermute | solution.py:24
  95.2 4.6 %copy.213 = f32[3,14040]{0,1:T(8,128)} copy(f32[3,14040]{1,0:T(4,128)S(1)} %concatenate.34) | data formatting | bytes 336960 | tf_op jit(solution)/shard_map/concatenate | solution.py:25
  99.8 11.8 %broadcast_select_fusion = f32[3,14040]{0,1:T(8,128)} fusion(f32[3,14040]{0,1:T(8,128)} %copy.213, pred[14040]{0:T(1024)(128)(4,1)S(1)} %broadcast_in_dim.92), kind=kLoop, calls=%fused_computation.8 | loop fusion | flops 42120 | bytes 351000 | tf_op jit(solution)/shard_map/jit(_where)/select_n | solution.py:96
  111.5 30.9 %gather_fusion = f32[8192,3]{1,0:T(8,128)} fusion(f32[3,14040]{0,1:T(8,128)} %broadcast_select_fusion, s32[8192]{0:T(1024)S(1)} %fusion.12), kind=kCustom, calls=%fused_computation.clone | custom fusion | bytes 229376 | tf_op jit(solution)/shard_map/jit(_take)/gather | solution.py:89
  142.5 6.2 %broadcast_select_fusion.4 = f32[8192,3]{1,0:T(8,128)S(1)} fusion(f32[8192,3]{1,0:T(8,128)} %gather_fusion, pred[8192]{0:T(1024)(128)(4,1)S(1)} %compare_and_fusion.3), kind=kLoop, calls=%fused_computation.12 | loop fusion | flops 24576 | bytes 204800 | tf_op jit(solution)/shard_map/jit(_take)/select_n | solution.py:89
  150.6 30.9 %gather_fusion.1 = f32[8192,3]{1,0:T(8,128)} fusion(f32[3,14040]{0,1:T(8,128)} %broadcast_select_fusion, s32[8192]{0:T(1024)S(1)} %fusion.13), kind=kCustom, calls=%fused_computation.1.clone | custom fusion | bytes 229376 | tf_op jit(solution)/shard_map/jit(_take)/gather | solution.py:89
  181.6 7.5 %broadcast_select_fusion.3 = f32[8192,3]{1,0:T(8,128)} fusion(f32[8192,3]{1,0:T(8,128)} %gather_fusion.1, pred[8192]{0:T(1024)(128)(4,1)S(1)} %compare_and_fusion.2), kind=kLoop, calls=%fused_computation.11 | loop fusion | flops 24576 | bytes 204800 | tf_op jit(solution)/shard_map/jit(_take)/select_n | solution.py:89
  189.1 2.9 %multiply_reduce_fusion.2 = f32[3,1024]{0,1:T(8,128)S(1)} fusion(f32[3,8,1024]{0,2,1:T(8,128)} %bitcast.98, f32[8,1024]{1,0:T(8,128)S(1)} %stack.46), kind=kLoop, calls=%fused_computation.6 | loop fusion | flops 46080 | bytes 143360 | tf_op jit(solution)/shard_map/reduce_sum | solution.py:90
  192.5 30.9 %gather_fusion.2 = f32[8192,3]{1,0:T(8,128)} fusion(f32[3,14040]{0,1:T(8,128)} %broadcast_select_fusion, s32[8192]{0:T(1024)S(1)} %fusion.14), kind=kCustom, calls=%fused_computation.2.clone | custom fusion | bytes 229376 | tf_op jit(solution)/shard_map/jit(_take)/gather | solution.py:89
  223.4 7.5 %broadcast_select_fusion.2 = f32[8192,3]{1,0:T(8,128)} fusion(f32[8192,3]{1,0:T(8,128)} %gather_fusion.2, pred[8192]{0:T(1024)(128)(4,1)S(1)} %compare_and_fusion.1), kind=kLoop, calls=%fused_computation.10 | loop fusion | flops 24576 | bytes 204800 | tf_op jit(solution)/shard_map/jit(_take)/select_n | solution.py:89
  231.0 2.9 %multiply_reduce_fusion.1 = f32[3,1024]{0,1:T(8,128)S(1)} fusion(f32[3,8,1024]{0,2,1:T(8,128)} %bitcast.99, f32[8,1024]{1,0:T(8,128)S(1)} %stack.48), kind=kLoop, calls=%fused_computation.5 | loop fusion | flops 46080 | bytes 143360 | tf_op jit(solution)/shard_map/reduce_sum | solution.py:90
  234.4 30.9 %gather_fusion.3 = f32[8192,3]{1,0:T(8,128)} fusion(f32[3,14040]{0,1:T(8,128)} %broadcast_select_fusion, s32[8192]{0:T(1024)S(1)} %fusion.15), kind=kCustom, calls=%fused_computation.3.clone | custom fusion | bytes 229376 | tf_op jit(solution)/shard_map/jit(_take)/gather | solution.py:89
  265.3 7.5 %broadcast_select_fusion.1 = f32[8192,3]{1,0:T(8,128)} fusion(f32[8192,3]{1,0:T(8,128)} %gather_fusion.3, pred[8192]{0:T(1024)(128)(4,1)S(1)} %compare_and_fusion), kind=kLoop, calls=%fused_computation.9 | loop fusion | flops 24576 | bytes 204800 | tf_op jit(solution)/shard_map/jit(_take)/select_n | solution.py:89
  272.8 2.9 %multiply_reduce_fusion = f32[3,1024]{0,1:T(8,128)S(1)} fusion(f32[3,8,1024]{0,2,1:T(8,128)} %bitcast.100, f32[8,1024]{1,0:T(8,128)S(1)} %stack.50), kind=kLoop, calls=%fused_computation.4 | loop fusion | flops 46080 | bytes 143360 | tf_op jit(solution)/shard_map/reduce_sum | solution.py:90
  (99 shorter events, 32.0 us)
Async XLA Ops:
  6.7 28.1 %all-to-all-start = ((f32[4,2,4,128]{3,2,1,0:T(4,128)}), f32[4,2,4,128]{3,2,1,0:T(4,128)S(1)}, u32[]{:S(2)}, u32[]{:S(2)}) async-start(f32[4,2,4,128]{3,2,1,0:T(4,128)} %copy.210), calls=%async_computation | async-start | bytes 32768 | tf_op jit(solution)/shard_map/all_to_all | solution.py:153
  24.8 17.3 %collective-permute-start.1 = (f32[3,1,16,128]{3,2,1,0:T(8,128)S(1)}, f32[3,1,16,128]{3,2,1,0:T(8,128)S(1)}, u32[]{:S(2)}, u32[]{:S(2)}) collective-permute-start(f32[3,1,16,128]{3,2,1,0:T(8,128)S(1)} %get-tuple-element.57), channel_id=1, source_target_pairs={{32,0},{64,32},{96,64},{128,96},{160,128},{192,160},{224,192},{256... | collective-permute-start | bytes 73736 | tf_op jit(solution)/shard_map/ppermute | solution.py:24
  32.4 8.8 %collective-permute-start = (f32[3,1,16,128]{3,2,1,0:T(8,128)S(1)}, f32[3,1,16,128]{3,2,1,0:T(8,128)S(1)}, u32[]{:S(2)}, u32[]{:S(2)}) collective-permute-start(f32[3,1,16,128]{3,2,1,0:T(8,128)S(1)} %get-tuple-element.58), channel_id=1, source_target_pairs={{0,32},{32,64},{64,96},{96,128},{128,160},{160,192},{192,224},{224... | collective-permute-start | bytes 73736 | tf_op jit(solution)/shard_map/ppermute | solution.py:21
  42.2 8.4 %collective-permute-start.2 = (f32[3,6,16,1]{3,2,1,0:T(8,128)S(1)}, f32[3,6,16,1]{3,2,1,0:T(8,128)S(1)}, u32[]{:S(2)}, u32[]{:S(2)}) collective-permute-start(f32[3,6,16,1]{3,2,1,0:T(8,128)S(1)} %get-tuple-element.53), channel_id=1, source_target_pairs={{0,4},{4,8},{8,12},{12,16},{16,20},{20,24},{24,28},{28,0},{1,5},{5... | collective-permute-start | bytes 3464 | tf_op jit(solution)/shard_map/ppermute | solution.py:21
  45.5 6.6 %collective-permute-start.3 = (f32[3,6,16,1]{3,2,1,0:T(8,128)S(1)}, f32[3,6,16,1]{3,2,1,0:T(8,128)S(1)}, u32[]{:S(2)}, u32[]{:S(2)}) collective-permute-start(f32[3,6,16,1]{3,2,1,0:T(8,128)S(1)} %get-tuple-element.54), channel_id=1, source_target_pairs={{4,0},{8,4},{12,8},{16,12},{20,16},{24,20},{28,24},{0,28},{5,1},{9... | collective-permute-start | bytes 3464 | tf_op jit(solution)/shard_map/ppermute | solution.py:24
  52.3 7.8 %collective-permute-start.4 = (f32[3,6,1,130]{3,2,1,0:T(1,128)S(1)}, f32[3,6,1,130]{3,2,1,0:T(1,128)S(1)}, u32[]{:S(2)}, u32[]{:S(2)}) collective-permute-start(f32[3,6,1,130]{3,2,1,0:T(1,128)S(1)} %get-tuple-element.49), channel_id=1, source_target_pairs={{0,1},{1,2},{2,3},{3,0},{4,5},{5,6},{6,7},{7,4},{8,9},{9,10},{10,1... | collective-permute-start | bytes 28088 | tf_op jit(solution)/shard_map/ppermute | solution.py:21
  58.1 5.1 %collective-permute-start.5 = (f32[3,6,1,130]{3,2,1,0:T(1,128)S(1)}, f32[3,6,1,130]{3,2,1,0:T(1,128)S(1)}, u32[]{:S(2)}, u32[]{:S(2)}) collective-permute-start(f32[3,6,1,130]{3,2,1,0:T(1,128)S(1)} %get-tuple-element.50), channel_id=1, source_target_pairs={{1,0},{2,1},{3,2},{0,3},{5,4},{6,5},{7,6},{4,7},{9,8},{10,9},{11,1... | collective-permute-start | bytes 28088 | tf_op jit(solution)/shard_map/ppermute | solution.py:24
  64.6 35.2 %copy-start = (f32[3,4,16,128]{3,2,1,0:T(8,128)}, f32[3,4,16,128]{3,2,1,0:T(8,128)S(1)}, u32[]{:S(2)}) copy-start(f32[3,4,16,128]{3,2,1,0:T(8,128)S(1)} %multiply_add_fusion) | copy-start | bytes 294916
  64.6 9.6 %collective-permute-start.6 = (f32[3,1,16,128]{3,2,1,0:T(8,128)S(1)}, f32[3,1,16,128]{3,2,1,0:T(8,128)S(1)}, u32[]{:S(2)}, u32[]{:S(2)}) collective-permute-start(f32[3,1,16,128]{3,2,1,0:T(8,128)S(1)} %get-tuple-element.55), channel_id=1, source_target_pairs={{0,32},{32,64},{64,96},{96,128},{128,160},{160,192},{192,224},{224... | collective-permute-start | bytes 73736 | tf_op jit(solution)/shard_map/ppermute | solution.py:21
  66.6 8.5 %collective-permute-start.7 = (f32[3,1,16,128]{3,2,1,0:T(8,128)S(1)}, f32[3,1,16,128]{3,2,1,0:T(8,128)S(1)}, u32[]{:S(2)}, u32[]{:S(2)}) collective-permute-start(f32[3,1,16,128]{3,2,1,0:T(8,128)S(1)} %get-tuple-element.56), channel_id=1, source_target_pairs={{32,0},{64,32},{96,64},{128,96},{160,128},{192,160},{224,192},{256... | collective-permute-start | bytes 73736 | tf_op jit(solution)/shard_map/ppermute | solution.py:24
  75.2 9.7 %collective-permute-start.8 = (f32[3,6,16,1]{3,2,1,0:T(8,128)S(1)}, f32[3,6,16,1]{3,2,1,0:T(8,128)S(1)}, u32[]{:S(2)}, u32[]{:S(2)}) collective-permute-start(f32[3,6,16,1]{3,2,1,0:T(8,128)S(1)} %get-tuple-element.51), channel_id=1, source_target_pairs={{0,4},{4,8},{8,12},{12,16},{16,20},{20,24},{24,28},{28,0},{1,5},{5... | collective-permute-start | bytes 3464 | tf_op jit(solution)/shard_map/ppermute | solution.py:21
  78.4 8.3 %collective-permute-start.9 = (f32[3,6,16,1]{3,2,1,0:T(8,128)S(1)}, f32[3,6,16,1]{3,2,1,0:T(8,128)S(1)}, u32[]{:S(2)}, u32[]{:S(2)}) collective-permute-start(f32[3,6,16,1]{3,2,1,0:T(8,128)S(1)} %get-tuple-element.52), channel_id=1, source_target_pairs={{4,0},{8,4},{12,8},{16,12},{20,16},{24,20},{28,24},{0,28},{5,1},{9... | collective-permute-start | bytes 3464 | tf_op jit(solution)/shard_map/ppermute | solution.py:24
  86.9 4.8 %collective-permute-start.10 = (f32[3,6,1,130]{3,2,1,0:T(1,128)S(1)}, f32[3,6,1,130]{3,2,1,0:T(1,128)S(1)}, u32[]{:S(2)}, u32[]{:S(2)}) collective-permute-start(f32[3,6,1,130]{3,2,1,0:T(1,128)S(1)} %get-tuple-element.41), channel_id=1, source_target_pairs={{0,1},{1,2},{2,3},{3,0},{4,5},{5,6},{6,7},{7,4},{8,9},{9,10},{10,1... | collective-permute-start | bytes 28088 | tf_op jit(solution)/shard_map/ppermute | solution.py:21
  89.5 5.1 %collective-permute-start.11 = (f32[3,6,1,130]{3,2,1,0:T(1,128)S(1)}, f32[3,6,1,130]{3,2,1,0:T(1,128)S(1)}, u32[]{:S(2)}, u32[]{:S(2)}) collective-permute-start(f32[3,6,1,130]{3,2,1,0:T(1,128)S(1)} %get-tuple-element.42), channel_id=1, source_target_pairs={{1,0},{2,1},{3,2},{0,3},{5,4},{6,5},{7,6},{4,7},{9,8},{10,9},{11,1... | collective-permute-start | bytes 28088 | tf_op jit(solution)/shard_map/ppermute | solution.py:24
where the time goes:
time: 280 us; the launch traced here: 277 us
  local copies, waits for them, and re-layouts  133 us (48%)
  starting transfers between devices  63.9 us (23%)
  other arithmetic  58.2 us (21%)
  waiting for transfers between devices  19.4 us (7%)
    gather x4, local copies, waits for them, and re-layouts, local_sampler(): jnp.take(table, linear_all.reshape(-1), axis=1).reshape(3, 8, point_total)  124 us
    select_n x4, other arithmetic, local_sampler(): jnp.take(table, linear_all.reshape(-1), axis=1).reshape(3, 8, point_total)  28.6 us
    ppermute x6, starting transfers between devices, extended_2(): lax.ppermute(lax.slice_in_dim(block, 0, width, axis=dim), axis, backward)  27.7 us
    ppermute x6, starting transfers between devices, extended_2(): lax.ppermute(lax.slice_in_dim(block, block.shape[dim] - width, None, axis...  18.8 us
    all_to_all x1, starting transfers between devices, shards(): lax.all_to_all(sending, 'tile', split_axis=0, concat_axis=0, tiled=True)  17.3 us
    select_n x2, other arithmetic, wall_mask(): return jnp.where(keeping[None, None, :, None], field, 0.0)  12 us
    ppermute x6, waiting for transfers between devices, extended_2(): lax.ppermute(lax.slice_in_dim(block, 0, width, axis=dim), axis, backward)  10.2 us
    reduce_sum x4, other arithmetic, local_sampler(): return jnp.sum(values * weight_all[None], 1)  10.1 us
  transfers between devices with their start and end apart: 13, of which 8 were waited for; matrix products, arithmetic and copies ran while one was open for 1% of the time, Pallas kernels for 0%

commit v1 on v0

v1 whole, which is shorter than its diff:
```python
from functools import partial

import jax
import jax.numpy as jnp
from jax import lax
from jax.experimental import pallas as pl
from jax.experimental.pallas import tpu as pltpu
from jax.sharding import PartitionSpec as P

CAP = 2
CX, CY, CZ = 4, 16, 128
TILES = 4
BLOCKS = 4
LX = CX + 4
LY = 24
N_VEL = 3 * LX
N_ALL = N_VEL + CX + 2
PER = CZ // 4
N_Z = -(-N_ALL * 3 // PER)
ROWS = 64
PT_ROW = 56

flow_step = 0.2
trace_step = 1.25

VMEM = pl.BlockSpec(memory_space=pltpu.VMEM)
SMEM = pl.BlockSpec(memory_space=pltpu.SMEM)


def plane_ref(group, vel, visc, xlo, xhi):
    if group < N_VEL:
        comp, x = divmod(group, LX)
        if x < 2:
            return xlo.at[2 * comp + x]
        if x < 2 + CX:
            return vel.at[comp, x - 2]
        return xhi.at[2 * comp + x - 2 - CX]
    x = group - N_VEL
    if x == 0:
        return xlo.at[6]
    if x <= CX:
        return visc.at[x - 1]
    return xhi.at[6]


def halo_rows(group):
    if group < N_VEL:
        return 2 * group, 2
    return 2 * N_VEL + group - N_VEL, 1


def y_kernel(counts, dest, seeds, substeps, vel, visc, xlo, xhi, out):
    tile = lax.axis_index("tile")
    live = [b < counts[0] for b in range(BLOCKS)]
    ranks = []
    for b in range(BLOCKS):
        rank = jnp.int32(0)
        for a in range(b):
            rank = rank + jnp.where(dest[a] == dest[b], 1, 0)
        ranks.append(rank)
    payload = [
        jnp.concatenate([seeds[b], substeps[b : b + 1, :]], 0).astype(jnp.float32)
        for b in range(BLOCKS)
    ]
    for d in range(TILES):
        for r in range(CAP):
            slot = jnp.zeros((4, CZ), jnp.float32)
            for b in range(BLOCKS):
                chosen = live[b] & (dest[b] == d) & (ranks[b] == r)
                slot = jnp.where(chosen, payload[b], slot)
            out[d, PT_ROW + 4 * r : PT_ROW + 4 * r + 4, :] = slot

    @pl.when(tile < TILES - 1)
    def _():
        for g in range(N_ALL):
            row, n = halo_rows(g)
            out[tile + 1, row : row + n, :] = plane_ref(g, vel, visc, xlo, xhi)[CY - n : CY, :]

    @pl.when(tile > 0)
    def _():
        for g in range(N_ALL):
            row, n = halo_rows(g)
            out[tile - 1, row : row + n, :] = plane_ref(g, vel, visc, xlo, xhi)[0:n, :]


def z_kernel(vel, visc, xlo, xhi, yrecv, whole, zmsg):
    tile = lax.axis_index("tile")
    below = jnp.maximum(tile - 1, 0)
    above = jnp.minimum(tile + 1, TILES - 1)
    lane = lax.broadcasted_iota(jnp.int32, (8, CZ), 1)
    packs = [jnp.zeros((8, CZ), jnp.float32) for _ in range(N_Z)]
    for g in range(N_ALL):
        row, n = halo_rows(g)
        plane = plane_ref(g, vel, visc, xlo, xhi)
        high = jnp.where(tile < TILES - 1, yrecv[above, row : row + n, :], 0.0)
        low = jnp.where(tile > 0, yrecv[below, row : row + n, :], 0.0)
        edge = jnp.concatenate([high, jnp.zeros((8 - 2 * n, CZ), jnp.float32), low], 0)
        parts = [plane[0:8, :], plane[8:16, :], edge]
        for i, part in enumerate(parts):
            whole[g, 8 * i : 8 * i + 8, :] = part
            v, k = divmod(3 * g + i, PER)
            moved = pltpu.roll(part, (4 * k + 2) % CZ, 1)
            packs[v] = jnp.where((lane >= 4 * k) & (lane < 4 * k + 4), moved, packs[v])
    for v in range(N_Z):
        zmsg[v] = packs[v]


def trace_kernel(whole, zlo, zhi, yrecv, fresh, traced, wide, near, table):
    tile = lax.axis_index("tile")
    lane = lax.broadcasted_iota(jnp.int32, (LY, CZ), 1)
    row = lax.broadcasted_iota(jnp.int32, (LY, CZ), 0)
    low_lane = lax.broadcasted_iota(jnp.int32, (8, CZ), 1) % 4 < 2
    merged = [jnp.where(low_lane, zlo[v], zhi[v]) for v in range(N_Z)]
    for g in range(N_ALL):
        for i in range(3):
            v, k = divmod(3 * g + i, PER)
            wide[g, 8 * i : 8 * i + 8, :] = pltpu.roll(merged[v], (CZ - 2 - 4 * k) % CZ, 1)

    def up_z(a, b):
        ra, rb = pltpu.roll(a, CZ - 1, 1), pltpu.roll(b, CZ - 1, 1)
        return jnp.where(lane < CZ - 1, ra, rb), jnp.where(lane < CZ - 1, rb, ra)

    def down_z(a, b):
        ra, rb = pltpu.roll(a, 1, 1), pltpu.roll(b, 1, 1)
        return jnp.where(lane > 0, ra, rb), jnp.where(lane > 0, rb, ra)

    outside = ((tile == 0) & (row == LY - 1)) | ((tile == TILES - 1) & (row == CY))

    def flux(one, two, d):
        both = one[d] + two[d]
        return [0.25 * (one[i] + two[i]) * both for i in range(3)]

    def new_plane(x):
        fields = []
        cells = [[r[i * LX + x + 1] for i in range(3)] for r in (whole, wide)]
        ups = [up_z(cells[0][i], cells[1][i]) for i in range(3)]
        downs = [down_z(cells[0][i], cells[1][i]) for i in range(3)]
        for half, src in enumerate((whole, wide)):
            c = cells[half]
            spread = [0.0] * 3
            laplace = [0.0] * 3
            for d in range(3):
                if d == 0:
                    upper = [src[i * LX + x + 2] for i in range(3)]
                    lower = [src[i * LX + x] for i in range(3)]
                elif d == 1:
                    upper = [pltpu.roll(c[i], LY - 1, 0) for i in range(3)]
                    lower = [pltpu.roll(c[i], 1, 0) for i in range(3)]
                else:
                    upper = [ups[i][half] for i in range(3)]
                    lower = [downs[i][half] for i in range(3)]
                f_up, f_down = flux(c, upper, d), flux(lower, c, d)
                spread = [spread[i] + (f_up[i] - f_down[i]) for i in range(3)]
                laplace = [laplace[i] + (upper[i] + lower[i]) for i in range(3)]
            viscous = src[N_VEL + x]
            fields.append(
                [
                    c[i] + flow_step * (viscous * (laplace[i] - 6.0 * c[i]) - spread[i])
                    for i in range(3)
                ]
            )
        for i in range(3):
            if 1 <= x <= CX:
                fresh[i, x - 1] = fields[0][i][:CY]
            a, b = (jnp.where(outside, 0.0, fields[h][i]) for h in range(2))
            for dz, field in enumerate((down_z(a, b)[0], a, up_z(a, b)[0])):
                near[x, i, 0, dz] = pltpu.roll(field, 1, 0)[:CY]
                near[x, i, 1, dz] = field[:CY]
                near[x, i, 2, dz] = pltpu.roll(field, LY - 1, 0)[:CY]

    for x in range(CX + 2):
        new_plane(x)

    def sample(x, e):
        weights = [(jnp.maximum(-v, 0.0), 1.0 - jnp.abs(v), jnp.maximum(v, 0.0)) for v in e]
        total = [0.0] * 3
        for dx in range(3):
            plane = [0.0] * 3
            for dy in range(3):
                for i in range(3):
                    line = sum(weights[2][dz] * near[x + dx, i, dy, dz] for dz in range(3))
                    plane[i] = plane[i] + weights[1][dy] * line
            total = [total[i] + weights[0][dx] * plane[i] for i in range(3)]
        return total

    for x in range(CX):
        k1 = [near[x + 1, i, 1, 1] for i in range(3)]
        k2 = sample(x, [(0.5 * trace_step) * v for v in k1])
        k3 = sample(x, [(0.5 * trace_step) * v for v in k2])
        k4 = sample(x, [trace_step * v for v in k3])
        for i in range(3):
            moved = (trace_step / 6.0) * (k1[i] + 2.0 * k2[i] + 2.0 * k3[i] + k4[i])
            first = i * CX * CY + x * CY
            rest = moved
            for part in range(3):
                piece = rest.astype(jnp.bfloat16)
                table[part * 3 * CX * CY + first : part * 3 * CX * CY + first + CY, :] = piece
                rest = rest - piece.astype(jnp.float32)

    zs = lax.broadcasted_iota(jnp.int32, (CZ, CZ), 0)
    xys = lax.broadcasted_iota(jnp.int32, (CX * CY, CZ), 0)
    for s in range(TILES):
        for r in range(CAP):
            point = yrecv[s, PT_ROW + 4 * r : PT_ROW + 4 * r + 4, :].astype(jnp.int32)
            pick = jnp.where(zs == point[2:3], 1.0, 0.0).astype(jnp.bfloat16)
            got = jnp.dot(table[...], pick, preferred_element_type=jnp.float32)
            size = 3 * CX * CY
            got = got[:size] + got[size : 2 * size] + got[2 * size :]
            here = (xys == point[0:1] * CY + point[1:2]) & (point[3:4] > 0)
            for i in range(3):
                value = jnp.where(here, got[i * CX * CY : (i + 1) * CX * CY], 0.0)
                traced[s * CAP + r, i : i + 1, :] = jnp.sum(value, 0, keepdims=True)


def shards(velocity, viscosity, counts, destination, seeds, substeps):
    def ring(axis):
        n = lax.axis_size(axis)
        forward = [(i, (i + 1) % n) for i in range(n)]
        return forward, [(b, a) for a, b in forward]

    f32 = jnp.float32
    to_high = jnp.concatenate([velocity[:, CX - 2 :].reshape(6, CY, CZ), viscosity[CX - 1 :]], 0)
    to_low = jnp.concatenate([velocity[:, :2].reshape(6, CY, CZ), viscosity[:1]], 0)
    forward, backward = ring("wide")
    xlo = lax.ppermute(to_high, "wide", forward)
    xhi = lax.ppermute(to_low, "wide", backward)
    ymsg = pl.pallas_call(
        y_kernel,
        out_shape=jax.ShapeDtypeStruct((TILES, ROWS, CZ), f32),
        in_specs=[SMEM, SMEM] + [VMEM] * 6,
        out_specs=VMEM,
        name="pack_y",
    )(
        counts.reshape(1),
        destination.reshape(BLOCKS),
        seeds.reshape(BLOCKS, 3, CZ),
        substeps.reshape(BLOCKS, CZ),
        velocity,
        viscosity,
        xlo,
        xhi,
    )
    yrecv = lax.all_to_all(ymsg, "tile", split_axis=0, concat_axis=0, tiled=True)
    whole, zmsg = pl.pallas_call(
        z_kernel,
        out_shape=(
            jax.ShapeDtypeStruct((N_ALL, LY, CZ), f32),
            jax.ShapeDtypeStruct((N_Z, 8, CZ), f32),
        ),
        in_specs=[VMEM] * 5,
        out_specs=(VMEM, VMEM),
        name="pack_z",
    )(velocity, viscosity, xlo, xhi, yrecv)
    forward, backward = ring("sec")
    zlo = lax.ppermute(zmsg, "sec", forward)
    zhi = lax.ppermute(zmsg, "sec", backward)
    fresh, traced = pl.pallas_call(
        trace_kernel,
        out_shape=(
            jax.ShapeDtypeStruct((3, CX, CY, CZ), f32),
            jax.ShapeDtypeStruct((TILES * CAP, 3, CZ), f32),
        ),
        in_specs=[VMEM] * 4,
        out_specs=(VMEM, VMEM),
        scratch_shapes=[
            pltpu.VMEM((N_ALL, LY, CZ), f32),
            pltpu.VMEM((CX + 2, 3, 3, 3, CY, CZ), f32),
            pltpu.VMEM((9 * CX * CY, CZ), jnp.bfloat16),
        ],
        name="trace",
    )(whole, zlo, zhi, yrecv)
    return fresh, traced[None, None, None]


def solution(mesh):
    in_specs = (
        P(None, "wide", "tile", "sec"),
        P("wide", "tile", "sec"),
        P("wide", "sec", "tile"),
        P("wide", "sec", "tile", None),
        P("wide", "sec", "tile", None, None, None),
        P("wide", "sec", "tile", None, None),
    )
    out_specs = (P(None, "wide", "tile", "sec"), P("wide", "sec", "tile", None, None, None))
    return jax.shard_map(shards, mesh=mesh, in_specs=in_specs, out_specs=out_specs, check_vma=False)
```

time: 280 us -> 58.1 us (0.21)
  local copies, waits for them, and re-layouts: 133 us -> 4.69 us
  other arithmetic: 58.2 us -> 0.01 us
  starting transfers between devices: 63.9 us -> 30.8 us
  waiting for transfers between devices: 19.4 us -> 4.01 us
  blocking collectives: 0 us -> 9.57 us
  Pallas kernels: 0 us -> 7.16 us
    gather x4 -> x0, local copies, waits for them, and re-layouts: 124 us -> none  [local_sampler(): jnp.take(table, linear_all.reshape(-1), axis=1).reshape(3, 8, point_total)]
    select_n x6 -> x0, other arithmetic: 40.6 us -> none  [the longest x4 28.6 us: local_sampler(): jnp.take(table, linear_all.reshape(-1), axis=1).reshape(3, 8, point_total)]
    all_to_all x1 -> x0, starting transfers between devices: 17.3 us -> none  [shards(): lax.all_to_all(sending, 'tile', split_axis=0, concat_axis=0, tiled=True)]
    ppermute x12 -> x4, starting transfers between devices: 46.5 us -> 30.8 us  [the longest x1 17.2 us: shards(): xhi = lax.ppermute(to_low, 'wide', backward)]
    ppermute x12 -> x4, waiting for transfers between devices: 19.4 us -> 4.01 us  [the longest x1 3.91 us: shards(): zlo = lax.ppermute(zmsg, 'sec', forward)]
    reduce_sum x5 -> x0, other arithmetic: 10.9 us -> none  [the longest x4 10.1 us: local_sampler(): return jnp.sum(values * weight_all[None], 1)]
    all_to_all x0 -> x1, blocking collectives: none -> 9.57 us  [shards(): lax.all_to_all(ymsg, 'tile', split_axis=0, concat_axis=0, tiled=True)]
    pallas_call x0 -> x3, Pallas kernels: none -> 7.16 us  [the longest x1 3.59 us: shards(): pl.pallas_call(trace_kernel, out_shape=(jax.ShapeDtypeStruct((3, CX, CY,...]
  transfers between devices with their start and end apart: 13 -> 4, of which waited for: 8 -> 2; matrix products, arithmetic and copies ran while one was open for 1% -> 1% of each run, Pallas kernels for 0% -> 0%
where the time goes in v1:
time: 58.1 us; the launch traced here: 57.5 us
  starting transfers between devices  30.8 us (53%)
  blocking collectives  9.57 us (16%)
  Pallas kernels  7.16 us (12%)
  local copies, waits for them, and re-layouts  4.69 us (8%)
  waiting for transfers between devices  4.01 us (7%)
  between operations  1.36 us (2%)
    ppermute x1, starting transfers between devices, shards(): xhi = lax.ppermute(to_low, 'wide', backward)  17.2 us
    all_to_all x1, blocking collectives, shards(): lax.all_to_all(ymsg, 'tile', split_axis=0, concat_axis=0, tiled=True)  9.57 us
    ppermute x1, starting transfers between devices, shards(): zhi = lax.ppermute(zmsg, 'sec', backward)  5.88 us
    ppermute x1, starting transfers between devices, shards(): xlo = lax.ppermute(to_high, 'wide', forward)  5.73 us
    ppermute x1, waiting for transfers between devices, shards(): zlo = lax.ppermute(zmsg, 'sec', forward)  3.91 us
    pallas_call x1, Pallas kernels, shards(): pl.pallas_call(trace_kernel, out_shape=(jax.ShapeDtypeStruct((3, CX, CY,...  3.59 us
    unnamed x12, local copies, waits for them, and re-layouts  3.14 us
    ppermute x1, starting transfers between devices, shards(): zlo = lax.ppermute(zmsg, 'sec', forward)  1.92 us
  transfers between devices with their start and end apart: 4, of which 2 were waited for; matrix products, arithmetic and copies ran while one was open for 1% of the time, Pallas kernels for 0%

profile of v1, /device:TPU:1, one launch (start us, length us, event | category | flops | bytes accessed | tf_op | source)
XLA Modules:
  0.0 57.5 jit_solution(4966387879104535973)
XLA Ops:
  0.6 0.7 %fusion.1 = (f32[1,16,128]{2,1,0:T(8,128)S(1)}, f32[1,16,128]{2,1,0:T(8,128)S(1)}) fusion(f32[4,16,128]{2,1,0:T(8,128)} %visc.3), kind=kLoop, calls=%fused_computation.4 | loop fusion | bytes 32768 | tf_op jit(solution)/shard_map/slice | solution.py:223
  1.3 0.8 %fusion = (f32[3,2,16,128]{3,2,1,0:T(8,128)S(1)}, f32[3,2,16,128]{3,2,1,0:T(8,128)S(1)}) fusion(f32[3,4,16,128]{3,2,1,0:T(8,128)} %vel.3), kind=kLoop, calls=%fused_computation.3 | loop fusion | bytes 196608 | tf_op jit(solution)/shard_map/slice | solution.py:223
  2.2 5.7 %collective-permute-start = (f32[7,16,128]{2,1,0:T(8,128)S(1)}, f32[7,16,128]{2,1,0:T(8,128)S(1)}, u32[]{:S(2)}, u32[]{:S(2)}) collective-permute-start(f32[7,16,128]{2,1,0:T(8,128)S(1)} %pad_maximum_fusion), channel_id=1, source_target_pairs={{0,32},{32,64},{64,96},{96,128},{128,160},{160,192},{192,224},{224... | collective-permute-start | bytes 172040 | tf_op jit(solution)/shard_map/ppermute | solution.py:225
  7.9 0.0 copy-start.4
  7.9 17.2 %collective-permute-start.1 = (f32[7,16,128]{2,1,0:T(8,128)S(1)}, f32[7,16,128]{2,1,0:T(8,128)S(1)}, u32[]{:S(2)}, u32[]{:S(2)}) collective-permute-start(f32[7,16,128]{2,1,0:T(8,128)S(1)} %pad_maximum_fusion.1), channel_id=1, source_target_pairs={{32,0},{64,32},{96,64},{128,96},{160,128},{192,160},{224,192},{256... | collective-permute-start | bytes 172040 | tf_op jit(solution)/shard_map/ppermute | solution.py:226
  25.8 0.0 copy-done.4
  25.8 0.6 %copy.11 = s32[1,1,1,4,3,128]{5,4,3,2,1,0:T(4,128)} copy(s32[1,1,1,4,3,128]{5,3,4,2,1,0:T(4,128)S(1)} %copy-done.4) | data formatting | bytes 12288 | tf_op args[4]
  26.4 0.0 collective-permute-done.xlo
  26.4 0.0 copy-start
  26.4 0.1 collective-permute-done.1.xhi
  26.5 0.5 copy-done
  27.1 0.1 copy-done.1
  27.2 1.7 %pack_y.1 = f32[4,64,128]{2,1,0:T(8,128)} custom-call(s32[1]{0:T(128)} %bitcast.9.counts, s32[4]{0:T(128)} %bitcast.15, s32[4,3,128]{2,1,0:T(4,128)} %bitcast.12, s32[4,128]{1,0:T(4,128)} %bitcast.14, f32[3,4,16,128]{3,2,1,0:T(8,128)} %vel.3, f32[4,16,128]{2,1,0:T(8,128)} %visc.3, f32[7,16,128]{2,1,0:T(8,128)} %copy-done, f32[7,16,128]{2,1,0:T(8,128)} %copy-done.1), custom_call_target="tpu_custom_call" | custom-call | tf_op jit(solution)/shard_map/pack_y/pallas_call | solution.py:227
  28.8 9.6 %all_to_all.5.yrecv = f32[4,64,128]{2,1,0:T(8,128)} all-to-all(f32[4,64,128]{2,1,0:T(8,128)} %pack_y.1), channel_id=1, replica_groups=mesh['wide'=32,'sec'=8,'tile'=4] {'tile'}, dimensions={0} | all-to-all | bytes 262144 | tf_op jit(solution)/shard_map/all_to_all | solution.py:243
  38.4 1.9 %pack_z.1 = (f32[30,24,128]{2,1,0:T(8,128)}, f32[3,8,128]{2,1,0:T(8,128)}) custom-call(f32[3,4,16,128]{3,2,1,0:T(8,128)} %vel.3, f32[4,16,128]{2,1,0:T(8,128)} %visc.3, f32[7,16,128]{2,1,0:T(8,128)} %copy-done, f32[7,16,128]{2,1,0:T(8,128)} %copy-done.1, f32[4,64,128]{2,1,0:T(8,128)} %all_to_all.5.yrecv), custom_call_target="tpu_custom_call" | custom-call | tf_op jit(solution)/shard_map/pack_z/pallas_call | solution.py:244
  40.3 5.9 %collective-permute-start.3 = (f32[3,8,128]{2,1,0:T(8,128)}, f32[3,8,128]{2,1,0:T(8,128)S(1)}, u32[]{:S(2)}, u32[]{:S(2)}) collective-permute-start(f32[3,8,128]{2,1,0:T(8,128)} %get-tuple-element.7), channel_id=1, source_target_pairs={{4,0},{8,4},{12,8},{16,12},{20,16},{24,20},{28,24},{0,28},{5,1},{9... | collective-permute-start | bytes 36872 | tf_op jit(solution)/shard_map/ppermute | solution.py:256
  46.2 1.9 %collective-permute-start.2 = (f32[3,8,128]{2,1,0:T(8,128)}, f32[3,8,128]{2,1,0:T(8,128)S(1)}, u32[]{:S(2)}, u32[]{:S(2)}) collective-permute-start(f32[3,8,128]{2,1,0:T(8,128)} %get-tuple-element.7), channel_id=1, source_target_pairs={{0,4},{4,8},{8,12},{12,16},{16,20},{20,24},{24,28},{28,0},{1,5},{5... | collective-permute-start | bytes 36872 | tf_op jit(solution)/shard_map/ppermute | solution.py:255
  48.1 0.0 collective-permute-done.3.zhi
  48.1 0.0 copy-start.2
  48.1 3.9 %collective-permute-done.2.zlo = f32[3,8,128]{2,1,0:T(8,128)S(1)} collective-permute-done((f32[3,8,128]{2,1,0:T(8,128)}, f32[3,8,128]{2,1,0:T(8,128)S(1)}, u32[]{:S(2)}, u32[]{:S(2)}) %collective-permute-start.2) | collective-permute-done | bytes 12320 | tf_op jit(solution)/shard_map/ppermute | solution.py:255
  52.0 0.0 copy-done.2
  52.0 0.6 %copy-done.3 = f32[3,8,128]{2,1,0:T(8,128)} copy-done((f32[3,8,128]{2,1,0:T(8,128)}, f32[3,8,128]{2,1,0:T(8,128)S(1)}, u32[]{:S(2)}) %copy-start.3) | copy-done | bytes 12312
  52.6 3.6 %trace.1 = (f32[3,4,16,128]{3,2,1,0:T(8,128)}, f32[8,3,128]{2,1,0:T(4,128)}) custom-call(f32[30,24,128]{2,1,0:T(8,128)} %get-tuple-element.6.whole, f32[3,8,128]{2,1,0:T(8,128)} %copy-done.3, f32[3,8,128]{2,1,0:T(8,128)} %copy-done.2, f32[4,64,128]{2,1,0:T(8,128)} %all_to_all.5.yrecv), custom_call_target="tpu_custom_call" | custom-call | tf_op jit(solution)/shard_map/trace/pallas_call | solution.py:257
  56.2 1.3 %copy.9 = f32[1,1,1,8,3,128]{5,3,4,2,1,0:T(8,128)} copy(f32[1,1,1,8,3,128]{5,4,3,2,1,0:T(4,128)} %bitcast.13) | data formatting | bytes 24576
  (4 shorter events, 0.0 us)
Async XLA Ops:
  2.2 24.3 %collective-permute-start = (f32[7,16,128]{2,1,0:T(8,128)S(1)}, f32[7,16,128]{2,1,0:T(8,128)S(1)}, u32[]{:S(2)}, u32[]{:S(2)}) collective-permute-start(f32[7,16,128]{2,1,0:T(8,128)S(1)} %pad_maximum_fusion), channel_id=1, source_target_pairs={{0,32},{32,64},{64,96},{96,128},{128,160},{160,192},{192,224},{224... | collective-permute-start | bytes 172040 | tf_op jit(solution)/shard_map/ppermute | solution.py:225
  7.9 17.9 %copy-start.4 = (s32[1,1,1,4,3,128]{5,3,4,2,1,0:T(4,128)S(1)}, s32[1,1,1,4,3,128]{5,3,4,2,1,0:T(4,128)}, u32[]{:S(2)}) copy-start(s32[1,1,1,4,3,128]{5,3,4,2,1,0:T(4,128)} %param.10) | copy-start | bytes 18436
  7.9 18.6 %collective-permute-start.1 = (f32[7,16,128]{2,1,0:T(8,128)S(1)}, f32[7,16,128]{2,1,0:T(8,128)S(1)}, u32[]{:S(2)}, u32[]{:S(2)}) collective-permute-start(f32[7,16,128]{2,1,0:T(8,128)S(1)} %pad_maximum_fusion.1), channel_id=1, source_target_pairs={{32,0},{64,32},{96,64},{128,96},{160,128},{192,160},{224,192},{256... | collective-permute-start | bytes 172040 | tf_op jit(solution)/shard_map/ppermute | solution.py:226
  26.4 0.6 %copy-start = (f32[7,16,128]{2,1,0:T(8,128)}, f32[7,16,128]{2,1,0:T(8,128)S(1)}, u32[]{:S(2)}) copy-start(f32[7,16,128]{2,1,0:T(8,128)S(1)} %collective-permute-done.xlo) | copy-start | bytes 172036
  26.5 0.6 %copy-start.1 = (f32[7,16,128]{2,1,0:T(8,128)}, f32[7,16,128]{2,1,0:T(8,128)S(1)}, u32[]{:S(2)}) copy-start(f32[7,16,128]{2,1,0:T(8,128)S(1)} %collective-permute-done.1.xhi) | copy-start | bytes 172036
  40.3 7.8 %collective-permute-start.3 = (f32[3,8,128]{2,1,0:T(8,128)}, f32[3,8,128]{2,1,0:T(8,128)S(1)}, u32[]{:S(2)}, u32[]{:S(2)}) collective-permute-start(f32[3,8,128]{2,1,0:T(8,128)} %get-tuple-element.7), channel_id=1, source_target_pairs={{4,0},{8,4},{12,8},{16,12},{20,16},{24,20},{28,24},{0,28},{5,1},{9... | collective-permute-start | bytes 36872 | tf_op jit(solution)/shard_map/ppermute | solution.py:256
  46.2 5.9 %collective-permute-start.2 = (f32[3,8,128]{2,1,0:T(8,128)}, f32[3,8,128]{2,1,0:T(8,128)S(1)}, u32[]{:S(2)}, u32[]{:S(2)}) collective-permute-start(f32[3,8,128]{2,1,0:T(8,128)} %get-tuple-element.7), channel_id=1, source_target_pairs={{0,4},{4,8},{8,12},{12,16},{16,20},{20,24},{24,28},{28,0},{1,5},{5... | collective-permute-start | bytes 36872 | tf_op jit(solution)/shard_map/ppermute | solution.py:255
  48.1 3.9 %copy-start.2 = (f32[3,8,128]{2,1,0:T(8,128)}, f32[3,8,128]{2,1,0:T(8,128)S(1)}, u32[]{:S(2)}) copy-start(f32[3,8,128]{2,1,0:T(8,128)S(1)} %collective-permute-done.3.zhi) | copy-start | bytes 36868
  52.0 0.6 %copy-start.3 = (f32[3,8,128]{2,1,0:T(8,128)}, f32[3,8,128]{2,1,0:T(8,128)S(1)}, u32[]{:S(2)}) copy-start(f32[3,8,128]{2,1,0:T(8,128)S(1)} %collective-permute-done.2.zlo) | copy-start | bytes 36868

commit v2 on v1

v2 whole, which is shorter than its diff:
```python
from functools import partial

import jax
import jax.numpy as jnp
from jax import lax
from jax.experimental import pallas as pl
from jax.experimental.pallas import tpu as pltpu
from jax.sharding import PartitionSpec as P

CAP = 2
CX, CY, CZ = 4, 16, 128
TILES = 4
BLOCKS = 4
SLOTS = TILES * CAP
LX = CX + 4
LY = 24
N_VEL = 3 * LX
N_ALL = N_VEL + CX + 2
ROWS = 64
PT_ROW = 56
WIDTH = CZ // LX

flow_step = 0.2
trace_step = 1.25

VMEM = pl.BlockSpec(memory_space=pltpu.VMEM)
SMEM = pl.BlockSpec(memory_space=pltpu.SMEM)
f32 = jnp.float32


def call(kernel, name, out_shape, in_specs, scratch=(), flops=0, moved=0):
    return pl.pallas_call(
        kernel,
        out_shape=out_shape,
        in_specs=in_specs,
        out_specs=jax.tree.map(lambda _: VMEM, out_shape),
        scratch_shapes=list(scratch),
        compiler_params=pltpu.CompilerParams(vmem_limit_bytes=8 << 20),
        cost_estimate=pl.CostEstimate(flops=flops, bytes_accessed=moved, transcendentals=0),
        name=name,
    )


def shape(*dims):
    return jax.ShapeDtypeStruct(dims, f32)


def group_of(group):
    if group < N_VEL:
        return divmod(group, LX)
    return 3, group - N_VEL + 1


def plane_ref(group, vel, visc, xlo, xhi):
    comp, x = group_of(group)
    if x < 2:
        return xlo.at[2 * comp + x] if comp < 3 else xlo.at[6]
    if x < 2 + CX:
        return vel.at[comp, x - 2] if comp < 3 else visc.at[x - 2]
    return xhi.at[2 * comp + x - 2 - CX] if comp < 3 else xhi.at[6]


def inner(group):
    return 2 <= group_of(group)[1] < 2 + CX


def halo_rows(group):
    if group < N_VEL:
        return 2 * group, 2
    return 2 * N_VEL + group - N_VEL, 1


def x_kernel(vel, visc, to_high, to_low):
    for out, first, edge in ((to_high, CX - 2, CX - 1), (to_low, 0, 0)):
        for c in range(3):
            out[2 * c : 2 * c + 2] = vel[c, first : first + 2]
        out[6] = visc[edge]


def write_rows(groups, out, planes):
    tile = lax.axis_index("tile")

    @pl.when(tile < TILES - 1)
    def _():
        for g in groups:
            row, n = halo_rows(g)
            out[tile + 1, row : row + n, :] = planes(g)[CY - n : CY, :]

    @pl.when(tile > 0)
    def _():
        for g in groups:
            row, n = halo_rows(g)
            out[tile - 1, row : row + n, :] = planes(g)[0:n, :]


def points_kernel(counts, dest, seeds, substeps, vel, visc, out):
    live = [b < counts[0] for b in range(BLOCKS)]
    ranks = []
    for b in range(BLOCKS):
        rank = jnp.int32(0)
        for a in range(b):
            rank = rank + jnp.where(dest[a] == dest[b], 1, 0)
        ranks.append(rank)
    payload = [
        jnp.concatenate([seeds[c, b : b + 1, :] for c in range(3)] + [substeps[b : b + 1, :]], 0)
        for b in range(BLOCKS)
    ]
    for d in range(TILES):
        for r in range(CAP):
            slot = jnp.zeros((4, CZ), jnp.int32)
            for b in range(BLOCKS):
                chosen = live[b] & (dest[b] == d) & (ranks[b] == r)
                slot = jnp.where(chosen, payload[b], slot)
            out[d, PT_ROW + 4 * r : PT_ROW + 4 * r + 4, :] = slot.astype(f32)
    groups = [g for g in range(N_ALL) if inner(g)]
    write_rows(groups, out, lambda g: plane_ref(g, vel, visc, None, None))


def y_kernel(base, xlo, xhi, out):
    out[...] = base[...]
    groups = [g for g in range(N_ALL) if not inner(g)]
    write_rows(groups, out, lambda g: plane_ref(g, None, None, xlo, xhi))


def columns(part, group, lane, acc):
    comp, x = group_of(group)
    place = WIDTH * x + 4 * comp
    moved = pltpu.roll(part, (place + 2) % CZ, 1)
    return jnp.where((lane >= place) & (lane < place + 4), moved, acc)


def z_kernel(vel, visc, xlo, xhi, out):
    lane = lax.broadcasted_iota(jnp.int32, (CY, CZ), 1)
    acc = jnp.zeros((CY, CZ), f32)
    for g in range(N_ALL):
        acc = columns(plane_ref(g, vel, visc, xlo, xhi)[...], g, lane, acc)
    out[...] = acc


def edge_rows_kernel(yrecv, zpart, edges, zmsg):
    tile = lax.axis_index("tile")
    below = jnp.maximum(tile - 1, 0)
    above = jnp.minimum(tile + 1, TILES - 1)
    lane = lax.broadcasted_iota(jnp.int32, (8, CZ), 1)
    acc = jnp.zeros((8, CZ), f32)
    for g in range(N_ALL):
        row, n = halo_rows(g)
        high = jnp.where(tile < TILES - 1, yrecv[above, row : row + n, :], 0.0)
        low = jnp.where(tile > 0, yrecv[below, row : row + n, :], 0.0)
        edge = jnp.concatenate([high, jnp.zeros((8 - 2 * n, CZ), f32), low], 0)
        edges[g] = edge
        acc = columns(edge, g, lane, acc)
    zmsg[0:CY, :] = zpart[...]
    zmsg[CY:LY, :] = acc


def outside_walls():
    tile = lax.axis_index("tile")
    row = lax.broadcasted_iota(jnp.int32, (LY, CZ), 0)
    return ((tile == 0) & (row == LY - 1)) | ((tile == TILES - 1) & (row == CY))


def flux(one, two, d):
    both = one[d] + two[d]
    return [0.25 * (one[i] + two[i]) * both for i in range(3)]


def advance(c, viscous, sides):
    spread = [0.0] * 3
    laplace = [0.0] * 3
    for d, (lower, upper) in enumerate(sides):
        f_up, f_down = flux(c, upper, d), flux(lower, c, d)
        spread = [spread[i] + (f_up[i] - f_down[i]) for i in range(3)]
        laplace = [laplace[i] + (upper[i] + lower[i]) for i in range(3)]
    return [
        c[i] + flow_step * (viscous * (laplace[i] - 6.0 * c[i]) - spread[i]) for i in range(3)
    ]


def both_ways(fields, step, axis):
    n = fields[0].shape[axis]
    return (
        [pltpu.roll(v, step, axis) for v in fields],
        [pltpu.roll(v, n - step, axis) for v in fields],
    )


def runge_kutta(near):
    def sample(e):
        weights = [(jnp.maximum(-v, 0.0), 1.0 - jnp.abs(v), jnp.maximum(v, 0.0)) for v in e]
        total = [0.0] * 3
        for dx in range(3):
            plane = [0.0] * 3
            for dy in range(3):
                for i in range(3):
                    line = sum(weights[2][dz] * near(i, dx, dy, dz) for dz in range(3))
                    plane[i] = plane[i] + weights[1][dy] * line
            total = [total[i] + weights[0][dx] * plane[i] for i in range(3)]
        return total

    k1 = [near(i, 1, 1, 1) for i in range(3)]
    k2 = sample([(0.5 * trace_step) * v for v in k1])
    k3 = sample([(0.5 * trace_step) * v for v in k2])
    k4 = sample([trace_step * v for v in k3])
    return [
        (trace_step / 6.0) * (k1[i] + 2.0 * k2[i] + 2.0 * k3[i] + k4[i]) for i in range(3)
    ]


def points_of(yrecv, slot):
    s, r = divmod(slot, CAP)
    rows = yrecv[s, PT_ROW + 4 * r : PT_ROW + 4 * r + 4, :].astype(jnp.int32)
    return [rows[k : k + 1] for k in range(4)]


def at_edge(z):
    return (z < 2) | (z >= CZ - 2)


def lanes_of(table, index):
    return jnp.take_along_axis(table, index, axis=1, mode="promise_in_bounds")


def main_kernel(vel, visc, xlo, xhi, edges, yrecv, fresh, traced, strip, whole, near, table):
    lane = lax.broadcasted_iota(jnp.int32, (LY, CZ), 1)
    strips = [jnp.zeros((LY, CZ), f32) for _ in range(4)]
    for g in range(N_ALL):
        comp, x = group_of(g)
        whole[g, 0:CY, :] = plane_ref(g, vel, visc, xlo, xhi)[...]
        whole[g, CY:LY, :] = edges[g]
        plane = whole[g]
        place = WIDTH * x
        early = pltpu.roll(plane, (place + 2) % CZ, 1)
        late = pltpu.roll(plane, (place + 12) % CZ, 1)
        acc = jnp.where((lane >= place + 2) & (lane < place + 6), early, strips[comp])
        strips[comp] = jnp.where((lane >= place + 8) & (lane < place + 12), late, acc)
    for comp in range(4):
        strip[comp] = strips[comp]

    outside = outside_walls()
    for x in range(CX + 2):
        c = [whole[i * LX + x + 1] for i in range(3)]
        sides = [
            ([whole[i * LX + x] for i in range(3)], [whole[i * LX + x + 2] for i in range(3)]),
            both_ways(c, 1, 0),
            both_ways(c, 1, 1),
        ]
        new = advance(c, whole[N_VEL + x], sides)
        for i in range(3):
            if 1 <= x <= CX:
                fresh[i, x - 1] = new[i][:CY]
            a = jnp.where(outside, 0.0, new[i])
            for dz, field in enumerate((pltpu.roll(a, 1, 1), a, pltpu.roll(a, CZ - 1, 1))):
                near[x, i, 0, dz] = pltpu.roll(field, 1, 0)[:CY]
                near[x, i, 1, dz] = field[:CY]
                near[x, i, 2, dz] = pltpu.roll(field, LY - 1, 0)[:CY]

    for x in range(CX):
        moved = runge_kutta(lambda i, dx, dy, dz: near[x + dx, i, dy, dz])
        for i in range(3):
            table[i, x * CY : (x + 1) * CY, :] = moved[i]

    rows = lax.broadcasted_iota(jnp.int32, (CX * CY, CZ), 0)
    for slot in range(SLOTS):
        sx, sy, sz, steps = points_of(yrecv, slot)
        here = (rows == sx * CY + sy) & (steps > 0) & ~at_edge(sz)
        index = jnp.broadcast_to(sz, (8, CZ))
        for i in range(3):
            got = jnp.concatenate(
                [lanes_of(table[i, 8 * k : 8 * k + 8, :], index) for k in range(CX * CY // 8)], 0
            )
            traced[i, slot : slot + 1, :] = jnp.sum(jnp.where(here, got, 0.0), 0, keepdims=True)


def strip_kernel(strip, zlo, zhi, yrecv, fresh_in, traced_in, fresh, traced):
    lane = lax.broadcasted_iota(jnp.int32, (LY, CZ), 1)
    place = lane % WIDTH
    low, high = zlo[...], zhi[...]
    fields = []
    for comp in range(4):
        before = pltpu.roll(low, (CZ - 4 * comp) % CZ, 1)
        after = pltpu.roll(high, (CZ + 10 - 4 * comp) % CZ, 1)
        own = strip[comp]
        own = jnp.where(place < 2, before, own)
        fields.append(jnp.where((place == 12) | (place == 13), after, own))
    c = fields[:3]
    new = advance(c, fields[3], [both_ways(c, WIDTH, 1), both_ways(c, 1, 0), both_ways(c, 1, 1)])

    column = lax.broadcasted_iota(jnp.int32, (CY, CZ), 1)
    for i in range(3):
        part = new[i][:CY]
        for x in range(CX):
            first = WIDTH * (x + 2)
            left = pltpu.roll(part, (CZ - first - 2) % CZ, 1)
            right = pltpu.roll(part, (2 * CZ - 1 - first - 11) % CZ, 1)
            value = jnp.where(column == CZ - 1, right, fresh_in[i, x])
            fresh[i, x] = jnp.where(column == 0, left, value)

    outside = outside_walls()
    near = {}
    for i in range(3):
        a = jnp.where(outside, 0.0, new[i])
        for dz, field in enumerate((pltpu.roll(a, 1, 1), a, pltpu.roll(a, CZ - 1, 1))):
            shifts = (pltpu.roll(field, 1, 0), field, pltpu.roll(field, LY - 1, 0))
            for dy, shifted in enumerate(shifts):
                part = shifted[:CY]
                near[i, 0, dy, dz] = pltpu.roll(part, WIDTH, 1)
                near[i, 1, dy, dz] = part
                near[i, 2, dy, dz] = pltpu.roll(part, CZ - WIDTH, 1)
    moved = runge_kutta(lambda *key: near[key])

    rows = lax.broadcasted_iota(jnp.int32, (CY, CZ), 0)
    for slot in range(SLOTS):
        sx, sy, sz, steps = points_of(yrecv, slot)
        here = (rows == sy) & (steps > 0) & at_edge(sz)
        offset = jnp.where(sz < 2, sz + 2, sz - (CZ - 2) + 10)
        index = jnp.where(at_edge(sz), WIDTH * (sx + 2) + offset, 0)
        index = jnp.broadcast_to(index, (8, CZ))
        for i in range(3):
            got = jnp.concatenate([lanes_of(moved[i][8 * k : 8 * k + 8], index) for k in range(2)], 0)
            value = jnp.sum(jnp.where(here, got, 0.0), 0, keepdims=True)
            traced[i, slot : slot + 1, :] = traced_in[i, slot : slot + 1, :] + value


def shards(velocity, viscosity, counts, destination, seeds, substeps):
    def ring(axis):
        n = lax.axis_size(axis)
        forward = [(i, (i + 1) % n) for i in range(n)]
        return forward, [(b, a) for a, b in forward]

    message = shape(7, CY, CZ)
    to_high, to_low = call(x_kernel, "pack_x", (message, message), [VMEM] * 2)(velocity, viscosity)
    forward, backward = ring("wide")
    xlo = lax.ppermute(to_high, "wide", forward)
    xhi = lax.ppermute(to_low, "wide", backward)
    base = call(
        points_kernel,
        "points",
        shape(TILES, ROWS, CZ),
        [SMEM, SMEM] + [VMEM] * 4,
        flops=1 << 20,
        moved=1 << 20,
    )(
        counts.reshape(1),
        destination.reshape(BLOCKS),
        jnp.swapaxes(seeds.reshape(BLOCKS, 3, CZ), 0, 1),
        substeps.reshape(BLOCKS, CZ),
        velocity,
        viscosity,
    )
    ymsg = call(y_kernel, "pack_y", shape(TILES, ROWS, CZ), [VMEM] * 3)(base, xlo, xhi)
    yrecv = lax.all_to_all(ymsg, "tile", split_axis=0, concat_axis=0, tiled=True)
    zpart = call(z_kernel, "pack_z", shape(CY, CZ), [VMEM] * 4, flops=1 << 20, moved=1 << 20)(
        velocity, viscosity, xlo, xhi
    )
    edges, zmsg = call(
        edge_rows_kernel, "pack_edge", (shape(N_ALL, 8, CZ), shape(LY, CZ)), [VMEM] * 2
    )(yrecv, zpart)
    forward, backward = ring("sec")
    zlo = lax.ppermute(zmsg, "sec", forward)
    zhi = lax.ppermute(zmsg, "sec", backward)
    fresh, traced, strip = call(
        main_kernel,
        "trace",
        (shape(3, CX, CY, CZ), shape(3, SLOTS, CZ), shape(4, LY, CZ)),
        [VMEM] * 6,
        [
            pltpu.VMEM((N_ALL, LY, CZ), f32),
            pltpu.VMEM((CX + 2, 3, 3, 3, CY, CZ), f32),
            pltpu.VMEM((3, CX * CY, CZ), f32),
        ],
        flops=1 << 22,
        moved=1 << 23,
    )(velocity, viscosity, xlo, xhi, edges, yrecv)
    fresh, traced = call(
        strip_kernel,
        "strip",
        (shape(3, CX, CY, CZ), shape(3, SLOTS, CZ)),
        [VMEM] * 6,
    )(strip, zlo, zhi, yrecv, fresh, traced)
    return fresh, jnp.swapaxes(traced, 0, 1)[None, None, None]


def solution(mesh):
    in_specs = (
        P(None, "wide", "tile", "sec"),
        P("wide", "tile", "sec"),
        P("wide", "sec", "tile"),
        P("wide", "sec", "tile", None),
        P("wide", "sec", "tile", None, None, None),
        P("wide", "sec", "tile", None, None),
    )
    out_specs = (P(None, "wide", "tile", "sec"), P("wide", "sec", "tile", None, None, None))
    return jax.shard_map(shards, mesh=mesh, in_specs=in_specs, out_specs=out_specs, check_vma=False)
```

time: 58.1 us -> 49.8 us (0.86)
  blocking collectives: 9.57 us -> 0 us
  starting transfers between devices: 30.8 us -> 35.6 us
  Pallas kernels: 7.16 us -> 4.62 us
  local copies, waits for them, and re-layouts: 4.69 us -> 2.3 us
  waiting for transfers between devices: 4.01 us -> 5.43 us
    all_to_all x1 -> x0, blocking collectives: 9.57 us -> none  [shards(): lax.all_to_all(ymsg, 'tile', split_axis=0, concat_axis=0, tiled=True)]
    all_to_all x0 -> x1, starting transfers between devices: none -> 4.69 us  [shards(): lax.all_to_all(ymsg, 'tile', split_axis=0, concat_axis=0, tiled=True)]
    all_to_all x0 -> x1, waiting for transfers between devices: none -> 3.44 us  [shards(): lax.all_to_all(ymsg, 'tile', split_axis=0, concat_axis=0, tiled=True)]
    pallas_call x3 -> x7, Pallas kernels: 7.16 us -> 4.62 us  [the longest x1 1.73 us: shards(): call(main_kernel, 'trace', (shape(3, CX, CY, CZ), shape(3, SLOTS, CZ), sh...]
    ppermute x1, waiting for transfers between devices: 3.91 us -> 1.98 us  [shards(): zlo = lax.ppermute(zmsg, 'sec', forward)]
    slice x2 -> x0, local copies, waits for them, and re-layouts: 1.55 us -> none  [the longest x1 0.83 us: shards(): velocity[:, :2].reshape(6, CY, CZ)]
    unnamed x12 -> x14, local copies, waits for them, and re-layouts: 3.14 us -> 2.3 us
  transfers between devices with their start and end apart: 4 -> 5, of which waited for: 2 -> 2; matrix products, arithmetic and copies ran while one was open for 1% -> 0% of each run, Pallas kernels for 0% -> 5%
where the time goes in v2:
time: 49.8 us; the launch traced here: 49.3 us
  starting transfers between devices  35.6 us (71%)
  waiting for transfers between devices  5.43 us (11%)
  Pallas kernels  4.62 us (9%)
  local copies, waits for them, and re-layouts  2.3 us (5%)
  between operations  1.42 us (3%)
    ppermute x1, starting transfers between devices, shards(): xhi = lax.ppermute(to_low, 'wide', backward)  17.2 us
    ppermute x1, starting transfers between devices, shards(): zhi = lax.ppermute(zmsg, 'sec', backward)  5.89 us
    ppermute x1, starting transfers between devices, shards(): xlo = lax.ppermute(to_high, 'wide', forward)  5.86 us
    all_to_all x1, starting transfers between devices, shards(): lax.all_to_all(ymsg, 'tile', split_axis=0, concat_axis=0, tiled=True)  4.69 us
    all_to_all x1, waiting for transfers between devices, shards(): lax.all_to_all(ymsg, 'tile', split_axis=0, concat_axis=0, tiled=True)  3.44 us
    unnamed x14, local copies, waits for them, and re-layouts  2.3 us
    ppermute x1, waiting for transfers between devices, shards(): zlo = lax.ppermute(zmsg, 'sec', forward)  1.98 us
    ppermute x1, starting transfers between devices, shards(): zlo = lax.ppermute(zmsg, 'sec', forward)  1.92 us
  transfers between devices with their start and end apart: 5, of which 2 were waited for; matrix products, arithmetic and copies ran while one was open for 0% of the time, Pallas kernels for 5%

profile of v2, /device:TPU:1, one launch (start us, length us, event | category | flops | bytes accessed | tf_op | source)
XLA Modules:
  0.0 49.3 jit_solution(9573421310384625193)
XLA Ops:
  0.6 0.0 copy-start
  0.6 0.9 %copy-done = f32[3,4,16,128]{3,2,1,0:T(8,128)S(1)} copy-done((f32[3,4,16,128]{3,2,1,0:T(8,128)S(1)}, f32[3,4,16,128]{3,2,1,0:T(8,128)}, u32[]{:S(2)}) %copy-start) | copy-done | bytes 98328
  1.5 0.8 %copy-done.2 = f32[4,16,128]{2,1,0:T(8,128)S(1)} copy-done((f32[4,16,128]{2,1,0:T(8,128)S(1)}, f32[4,16,128]{2,1,0:T(8,128)}, u32[]{:S(2)}) %copy-start.2) | copy-done | bytes 32792
  2.3 0.0 copy-start.4
  2.3 5.9 %collective-permute-start = (f32[7,16,128]{2,1,0:T(8,128)S(1)}, f32[7,16,128]{2,1,0:T(8,128)S(1)}, u32[]{:S(2)}, u32[]{:S(2)}) collective-permute-start(f32[7,16,128]{2,1,0:T(8,128)S(1)} %get-tuple-element.11), channel_id=1, source_target_pairs={{0,32},{32,64},{64,96},{96,128},{128,160},{160,192},{192,224},{224... | collective-permute-start | bytes 172040 | tf_op jit(solution)/shard_map/ppermute | solution.py:334
  8.2 17.2 %collective-permute-start.1 = (f32[7,16,128]{2,1,0:T(8,128)S(1)}, f32[7,16,128]{2,1,0:T(8,128)S(1)}, u32[]{:S(2)}, u32[]{:S(2)}) collective-permute-start(f32[7,16,128]{2,1,0:T(8,128)S(1)} %get-tuple-element.12), channel_id=1, source_target_pairs={{32,0},{64,32},{96,64},{128,96},{160,128},{192,160},{224,192},{256... | collective-permute-start | bytes 172040 | tf_op jit(solution)/shard_map/ppermute | solution.py:335
  26.1 0.0 copy-start.5
  26.1 0.0 copy-start.6
  26.1 0.0 copy-done.1
  26.1 0.6 %copy-done.5 = s32[1,1,1,4,128]{4,3,2,1,0:T(4,128)S(1)} copy-done((s32[1,1,1,4,128]{4,3,2,1,0:T(4,128)S(1)}, s32[1,1,1,4,128]{4,3,2,1,0:T(4,128)}, u32[]{:S(2)}) %copy-start.5) | copy-done | bytes 2072
  26.7 0.6 %points.1.base = f32[4,64,128]{2,1,0:T(8,128)S(1)} custom-call(s32[1]{0:T(128)} %bitcast.9.counts, s32[4]{0:T(128)S(1)} %bitcast.12, s32[3,4,128]{2,1,0:T(4,128)S(1)} %bitcast.10, s32[4,128]{1,0:T(4,128)S(1)} %bitcast.11, f32[3,4,16,128]{3,2,1,0:T(8,128)S(1)} %copy-done.1, f32[4,16,128]{2,1,0:T(8,128)S(1)} %copy-done.3), custom_call_target="tpu_custom_call" | custom-call | flops 1048576 | bytes 1048576 | tf_op jit(solution)/shard_map/points/pallas_call | solution.py:336
  27.4 0.0 collective-permute-done.xlo
  27.4 0.0 collective-permute-done.1.xhi
  27.4 0.7 %pack_y.1 = f32[4,64,128]{2,1,0:T(8,128)} custom-call(f32[4,64,128]{2,1,0:T(8,128)S(1)} %points.1.base, f32[7,16,128]{2,1,0:T(8,128)S(1)} %collective-permute-done.xlo, f32[7,16,128]{2,1,0:T(8,128)S(1)} %collective-permute-done.1.xhi), custom_call_target="tpu_custom_call" | custom-call | tf_op jit(solution)/shard_map/pack_y/pallas_call | solution.py:351
  28.1 4.7 %all-to-all-start = ((f32[4,64,128]{2,1,0:T(8,128)}), f32[4,64,128]{2,1,0:T(8,128)S(1)}, u32[]{:S(2)}, u32[]{:S(2)}) async-start(f32[4,64,128]{2,1,0:T(8,128)} %pack_y.1), calls=%async_computation | async-start | bytes 262144 | tf_op jit(solution)/shard_map/all_to_all | solution.py:352
  32.7 0.1 pack_z.1.zpart
  32.9 3.4 %all-to-all-done.yrecv = f32[4,64,128]{2,1,0:T(8,128)S(1)} async-done(((f32[4,64,128]{2,1,0:T(8,128)}), f32[4,64,128]{2,1,0:T(8,128)S(1)}, u32[]{:S(2)}, u32[]{:S(2)}) %all-to-all-start) | async-done | bytes 131104 | tf_op jit(solution)/shard_map/all_to_all | solution.py:352
  36.3 0.1 pack_edge.1
  36.4 5.9 %collective-permute-start.3 = (f32[24,128]{1,0:T(8,128)S(1)}, f32[24,128]{1,0:T(8,128)S(1)}, u32[]{:S(2)}, u32[]{:S(2)}) collective-permute-start(f32[24,128]{1,0:T(8,128)S(1)} %get-tuple-element.15), channel_id=1, source_target_pairs={{4,0},{8,4},{12,8},{16,12},{20,16},{24,20},{28,24},{0,28},{5,1},{9... | collective-permute-start | bytes 36872 | tf_op jit(solution)/shard_map/ppermute | solution.py:361
  42.3 1.9 %collective-permute-start.2 = (f32[24,128]{1,0:T(8,128)S(1)}, f32[24,128]{1,0:T(8,128)S(1)}, u32[]{:S(2)}, u32[]{:S(2)}) collective-permute-start(f32[24,128]{1,0:T(8,128)S(1)} %get-tuple-element.15), channel_id=1, source_target_pairs={{0,4},{4,8},{8,12},{12,16},{16,20},{20,24},{24,28},{28,0},{1,5},{5... | collective-permute-start | bytes 36872 | tf_op jit(solution)/shard_map/ppermute | solution.py:360
  44.3 1.7 %trace.1 = (f32[3,4,16,128]{3,2,1,0:T(8,128)S(1)}, f32[3,8,128]{2,1,0:T(8,128)S(1)}, f32[4,24,128]{2,1,0:T(8,128)S(1)}) custom-call(f32[3,4,16,128]{3,2,1,0:T(8,128)S(1)} %copy-done.1, f32[4,16,128]{2,1,0:T(8,128)S(1)} %copy-done.3, f32[7,16,128]{2,1,0:T(8,128)S(1)} %collective-permute-done.xlo, f32[7,16,128]{2,1,0:T(8,128)S(1)} %collective-permute-done.1.xhi, ...), custom_call_target="tpu_custom_call" | custom-call | flops 4194304 | bytes 8388608 | tf_op jit(solution)/shard_map/trace/pallas_call | solution.py:362
  46.0 0.0 collective-permute-done.3.zhi
  46.0 2.0 %collective-permute-done.2.zlo = f32[24,128]{1,0:T(8,128)S(1)} collective-permute-done((f32[24,128]{1,0:T(8,128)S(1)}, f32[24,128]{1,0:T(8,128)S(1)}, u32[]{:S(2)}, u32[]{:S(2)}) %collective-permute-start.2) | collective-permute-done | bytes 12320 | tf_op jit(solution)/shard_map/ppermute | solution.py:360
  48.0 1.4 %strip.1 = (f32[3,4,16,128]{3,2,1,0:T(8,128)}, f32[3,8,128]{2,1,0:T(8,128)}) custom-call(f32[4,24,128]{2,1,0:T(8,128)S(1)} %get-tuple-element.14.strip, f32[24,128]{1,0:T(8,128)S(1)} %collective-permute-done.2.zlo, f32[24,128]{1,0:T(8,128)S(1)} %collective-permute-done.3.zhi, f32[4,64,128]{2,1,0:T(8,128)S(1)} %all-to-all-done.yrecv, ...), custom_call_target="tpu_custom_call" | custom-call | tf_op jit(solution)/shard_map/strip/pallas_call | solution.py:375
  (7 shorter events, 0.0 us)
Async XLA Ops:
  0.6 0.9 %copy-start = (f32[3,4,16,128]{3,2,1,0:T(8,128)S(1)}, f32[3,4,16,128]{3,2,1,0:T(8,128)}, u32[]{:S(2)}) copy-start(f32[3,4,16,128]{3,2,1,0:T(8,128)} %vel.7) | copy-start | bytes 294916
  1.5 0.8 %copy-start.2 = (f32[4,16,128]{2,1,0:T(8,128)S(1)}, f32[4,16,128]{2,1,0:T(8,128)}, u32[]{:S(2)}) copy-start(f32[4,16,128]{2,1,0:T(8,128)} %visc.7) | copy-start | bytes 98308
  2.3 23.8 %copy-start.1 = (f32[3,4,16,128]{3,2,1,0:T(8,128)S(1)}, f32[3,4,16,128]{3,2,1,0:T(8,128)}, u32[]{:S(2)}) copy-start(f32[3,4,16,128]{3,2,1,0:T(8,128)} %vel.7) | copy-start | bytes 294916
  2.3 23.8 %copy-start.3 = (f32[4,16,128]{2,1,0:T(8,128)S(1)}, f32[4,16,128]{2,1,0:T(8,128)}, u32[]{:S(2)}) copy-start(f32[4,16,128]{2,1,0:T(8,128)} %visc.7) | copy-start | bytes 98308
  2.3 23.8 %copy-start.4 = (s32[1,1,1,4,3,128]{5,3,4,2,1,0:T(4,128)S(1)}, s32[1,1,1,4,3,128]{5,3,4,2,1,0:T(4,128)}, u32[]{:S(2)}) copy-start(s32[1,1,1,4,3,128]{5,3,4,2,1,0:T(4,128)} %param.10) | copy-start | bytes 18436
  2.3 25.1 %collective-permute-start = (f32[7,16,128]{2,1,0:T(8,128)S(1)}, f32[7,16,128]{2,1,0:T(8,128)S(1)}, u32[]{:S(2)}, u32[]{:S(2)}) collective-permute-start(f32[7,16,128]{2,1,0:T(8,128)S(1)} %get-tuple-element.11), channel_id=1, source_target_pairs={{0,32},{32,64},{64,96},{96,128},{128,160},{160,192},{192,224},{224... | collective-permute-start | bytes 172040 | tf_op jit(solution)/shard_map/ppermute | solution.py:334
  8.2 19.2 %collective-permute-start.1 = (f32[7,16,128]{2,1,0:T(8,128)S(1)}, f32[7,16,128]{2,1,0:T(8,128)S(1)}, u32[]{:S(2)}, u32[]{:S(2)}) collective-permute-start(f32[7,16,128]{2,1,0:T(8,128)S(1)} %get-tuple-element.12), channel_id=1, source_target_pairs={{32,0},{64,32},{96,64},{128,96},{160,128},{192,160},{224,192},{256... | collective-permute-start | bytes 172040 | tf_op jit(solution)/shard_map/ppermute | solution.py:335
  26.1 0.7 %copy-start.5 = (s32[1,1,1,4,128]{4,3,2,1,0:T(4,128)S(1)}, s32[1,1,1,4,128]{4,3,2,1,0:T(4,128)}, u32[]{:S(2)}) copy-start(s32[1,1,1,4,128]{4,3,2,1,0:T(4,128)} %param.11) | copy-start | bytes 6148
  26.1 0.7 %copy-start.6 = (s32[1,1,1,4]{3,2,1,0:T(1,128)S(1)}, s32[1,1,1,4]{3,2,1,0:T(1,128)}, u32[]{:S(2)}) copy-start(s32[1,1,1,4]{3,2,1,0:T(1,128)} %param.9) | copy-start | bytes 52
  28.1 8.3 %all-to-all-start = ((f32[4,64,128]{2,1,0:T(8,128)}), f32[4,64,128]{2,1,0:T(8,128)S(1)}, u32[]{:S(2)}, u32[]{:S(2)}) async-start(f32[4,64,128]{2,1,0:T(8,128)} %pack_y.1), calls=%async_computation | async-start | bytes 262144 | tf_op jit(solution)/shard_map/all_to_all | solution.py:352
  36.4 9.6 %collective-permute-start.3 = (f32[24,128]{1,0:T(8,128)S(1)}, f32[24,128]{1,0:T(8,128)S(1)}, u32[]{:S(2)}, u32[]{:S(2)}) collective-permute-start(f32[24,128]{1,0:T(8,128)S(1)} %get-tuple-element.15), channel_id=1, source_target_pairs={{4,0},{8,4},{12,8},{16,12},{20,16},{24,20},{28,24},{0,28},{5,1},{9... | collective-permute-start | bytes 36872 | tf_op jit(solution)/shard_map/ppermute | solution.py:361
  42.3 5.7 %collective-permute-start.2 = (f32[24,128]{1,0:T(8,128)S(1)}, f32[24,128]{1,0:T(8,128)S(1)}, u32[]{:S(2)}, u32[]{:S(2)}) collective-permute-start(f32[24,128]{1,0:T(8,128)S(1)} %get-tuple-element.15), channel_id=1, source_target_pairs={{0,4},{4,8},{8,12},{12,16},{16,20},{20,24},{24,28},{28,0},{1,5},{5... | collective-permute-start | bytes 36872 | tf_op jit(solution)/shard_map/ppermute | solution.py:360

commit v3 on v2

--- a/solution.py
+++ b/solution.py
@@ -1,11 +1,10 @@
-from functools import partial
-
 import jax
 import jax.numpy as jnp
 from jax import lax
 from jax.experimental import pallas as pl
 from jax.experimental.pallas import tpu as pltpu
 from jax.sharding import PartitionSpec as P
+
 
 CAP = 2
 CX, CY, CZ = 4, 16, 128
@@ -16,8 +15,9 @@
 LY = 24
 N_VEL = 3 * LX
 N_ALL = N_VEL + CX + 2
+HALO_ROWS = 26
+PT_ROW = 56
 ROWS = 64
-PT_ROW = 56
 WIDTH = CZ // LX
 
 flow_step = 0.2
@@ -28,7 +28,7 @@
 f32 = jnp.float32
 
 
-def call(kernel, name, out_shape, in_specs, scratch=(), flops=0, moved=0):
+def call(kernel, out_shape, in_specs, scratch=(), flops=0, moved=0):
     return pl.pallas_call(
         kernel,
         out_shape=out_shape,
@@ -37,7 +37,6 @@
         scratch_shapes=list(scratch),
         compiler_params=pltpu.CompilerParams(vmem_limit_bytes=8 << 20),
         cost_estimate=pl.CostEstimate(flops=flops, bytes_accessed=moved, transcendentals=0),
-        name=name,
     )
 
 
@@ -51,12 +50,12 @@
     return 3, group - N_VEL + 1
 
 
-def plane_ref(group, vel, visc, xlo, xhi):
+def plane_ref(group, own, xlo, xhi):
     comp, x = group_of(group)
     if x < 2:
         return xlo.at[2 * comp + x] if comp < 3 else xlo.at[6]
     if x < 2 + CX:
-        return vel.at[comp, x - 2] if comp < 3 else visc.at[x - 2]
+        return own.at[CX * comp + x - 2]
     return xhi.at[2 * comp + x - 2 - CX] if comp < 3 else xhi.at[6]
 
 
@@ -65,36 +64,29 @@
 
 
 def halo_rows(group):
+    kind = [g for g in range(N_ALL) if inner(g) == inner(group)]
+    first = HALO_ROWS if inner(group) else 0
+    vels = [g for g in kind if g < N_VEL]
     if group < N_VEL:
-        return 2 * group, 2
-    return 2 * N_VEL + group - N_VEL, 1
-
-
-def x_kernel(vel, visc, to_high, to_low):
-    for out, first, edge in ((to_high, CX - 2, CX - 1), (to_low, 0, 0)):
-        for c in range(3):
-            out[2 * c : 2 * c + 2] = vel[c, first : first + 2]
-        out[6] = visc[edge]
-
-
-def write_rows(groups, out, planes):
+        return first + 2 * kind.index(group), 2
+    return first + len(vels) + kind.index(group), 1
+
+
+def next_tiles():
     tile = lax.axis_index("tile")
-
-    @pl.when(tile < TILES - 1)
-    def _():
-        for g in groups:
-            row, n = halo_rows(g)
-            out[tile + 1, row : row + n, :] = planes(g)[CY - n : CY, :]
-
-    @pl.when(tile > 0)
-    def _():
-        for g in groups:
-            row, n = halo_rows(g)
-            out[tile - 1, row : row + n, :] = planes(g)[0:n, :]
-
-
-def points_kernel(counts, dest, seeds, substeps, vel, visc, out):
-    live = [b < counts[0] for b in range(BLOCKS)]
+    return (tile + 1) % TILES, (tile + TILES - 1) % TILES
+
+
+def write_x(own, message, first, edge):
+    for c in range(3):
+        message[2 * c : 2 * c + 2] = own[CX * c + first : CX * c + first + 2]
+    message[6] = own[3 * CX + edge]
+
+
+def prepare_kernel(counts, dest, seeds, substeps, own, to_high, to_low, out):
+    write_x(own, to_high, CX - 2, CX - 1)
+    write_x(own, to_low, 0, 0)
+    live = [b < counts[0, 0, 0] for b in range(BLOCKS)]
     ranks = []
     for b in range(BLOCKS):
         rank = jnp.int32(0)
@@ -112,14 +104,24 @@
                 chosen = live[b] & (dest[b] == d) & (ranks[b] == r)
                 slot = jnp.where(chosen, payload[b], slot)
             out[d, PT_ROW + 4 * r : PT_ROW + 4 * r + 4, :] = slot.astype(f32)
-    groups = [g for g in range(N_ALL) if inner(g)]
-    write_rows(groups, out, lambda g: plane_ref(g, vel, visc, None, None))
+    up, down = next_tiles()
+    for g in range(N_ALL):
+        if inner(g):
+            row, n = halo_rows(g)
+            plane = plane_ref(g, own, None, None)
+            out[up, row : row + n, :] = plane[CY - n : CY, :]
+            out[down, row : row + n, :] = plane[0:n, :]
 
 
 def y_kernel(base, xlo, xhi, out):
     out[...] = base[...]
-    groups = [g for g in range(N_ALL) if not inner(g)]
-    write_rows(groups, out, lambda g: plane_ref(g, None, None, xlo, xhi))
+    up, down = next_tiles()
+    for g in range(N_ALL):
+        if not inner(g):
+            row, n = halo_rows(g)
+            plane = plane_ref(g, None, xlo, xhi)
+            out[up, row : row + n, :] = plane[CY - n : CY, :]
+            out[down, row : row + n, :] = plane[0:n, :]
 
 
 def columns(part, group, lane, acc):
@@ -129,11 +131,11 @@
     return jnp.where((lane >= place) & (lane < place + 4), moved, acc)
 
 
-def z_kernel(vel, visc, xlo, xhi, out):
+def z_kernel(own, xlo, xhi, out):
     lane = lax.broadcasted_iota(jnp.int32, (CY, CZ), 1)
     acc = jnp.zeros((CY, CZ), f32)
     for g in range(N_ALL):
-        acc = columns(plane_ref(g, vel, visc, xlo, xhi)[...], g, lane, acc)
+        acc = columns(plane_ref(g, own, xlo, xhi)[...], g, lane, acc)
     out[...] = acc
 
 
@@ -221,12 +223,12 @@
     return jnp.take_along_axis(table, index, axis=1, mode="promise_in_bounds")
 
 
-def main_kernel(vel, visc, xlo, xhi, edges, yrecv, fresh, traced, strip, whole, near, table):
+def main_kernel(own, xlo, xhi, edges, yrecv, fresh, traced, strip, whole, near, table):
     lane = lax.broadcasted_iota(jnp.int32, (LY, CZ), 1)
     strips = [jnp.zeros((LY, CZ), f32) for _ in range(4)]
     for g in range(N_ALL):
         comp, x = group_of(g)
-        whole[g, 0:CY, :] = plane_ref(g, vel, visc, xlo, xhi)[...]
+        whole[g, 0:CY, :] = plane_ref(g, own, xlo, xhi)[...]
         whole[g, CY:LY, :] = edges[g]
         plane = whole[g]
         place = WIDTH * x
@@ -329,41 +331,32 @@
         return forward, [(b, a) for a, b in forward]
 
     message = shape(7, CY, CZ)
-    to_high, to_low = call(x_kernel, "pack_x", (message, message), [VMEM] * 2)(velocity, viscosity)
+    own = jnp.concatenate([velocity.reshape(3 * CX, CY, CZ), viscosity], 0)
+    to_high, to_low, base = call(
+        prepare_kernel, (message, message, shape(TILES, ROWS, CZ)), [SMEM, SMEM] + [VMEM] * 3
+    )(
+        counts,
+        destination.reshape(BLOCKS),
+        jnp.swapaxes(seeds.reshape(BLOCKS, 3, CZ), 0, 1),
+        substeps.reshape(BLOCKS, CZ),
+        own,
+    )
     forward, backward = ring("wide")
     xlo = lax.ppermute(to_high, "wide", forward)
     xhi = lax.ppermute(to_low, "wide", backward)
-    base = call(
-        points_kernel,
-        "points",
-        shape(TILES, ROWS, CZ),
-        [SMEM, SMEM] + [VMEM] * 4,
-        flops=1 << 20,
-        moved=1 << 20,
-    )(
-        counts.reshape(1),
-        destination.reshape(BLOCKS),
-        jnp.swapaxes(seeds.reshape(BLOCKS, 3, CZ), 0, 1),
-        substeps.reshape(BLOCKS, CZ),
-        velocity,
-        viscosity,
-    )
-    ymsg = call(y_kernel, "pack_y", shape(TILES, ROWS, CZ), [VMEM] * 3)(base, xlo, xhi)
+    ymsg = call(y_kernel, shape(TILES, ROWS, CZ), [VMEM] * 3)(base, xlo, xhi)
     yrecv = lax.all_to_all(ymsg, "tile", split_axis=0, concat_axis=0, tiled=True)
-    zpart = call(z_kernel, "pack_z", shape(CY, CZ), [VMEM] * 4, flops=1 << 20, moved=1 << 20)(
-        velocity, viscosity, xlo, xhi
-    )
+    zpart = call(z_kernel, shape(CY, CZ), [VMEM] * 3, flops=1 << 20, moved=1 << 20)(own, xlo, xhi)
     edges, zmsg = call(
-        edge_rows_kernel, "pack_edge", (shape(N_ALL, 8, CZ), shape(LY, CZ)), [VMEM] * 2
+        edge_rows_kernel, (shape(N_ALL, 8, CZ), shape(LY, CZ)), [VMEM] * 2
     )(yrecv, zpart)
     forward, backward = ring("sec")
     zlo = lax.ppermute(zmsg, "sec", forward)
     zhi = lax.ppermute(zmsg, "sec", backward)
     fresh, traced, strip = call(
         main_kernel,
-        "trace",
         (shape(3, CX, CY, CZ), shape(3, SLOTS, CZ), shape(4, LY, CZ)),
-        [VMEM] * 6,
+        [VMEM] * 5,
         [
             pltpu.VMEM((N_ALL, LY, CZ), f32),
             pltpu.VMEM((CX + 2, 3, 3, 3, CY, CZ), f32),
@@ -371,12 +364,9 @@
         ],
         flops=1 << 22,
         moved=1 << 23,
-    )(velocity, viscosity, xlo, xhi, edges, yrecv)
+    )(own, xlo, xhi, edges, yrecv)
     fresh, traced = call(
-        strip_kernel,
-        "strip",
-        (shape(3, CX, CY, CZ), shape(3, SLOTS, CZ)),
-        [VMEM] * 6,
+        strip_kernel, (shape(3, CX, CY, CZ), shape(3, SLOTS, CZ)), [VMEM] * 6
     )(strip, zlo, zhi, yrecv, fresh, traced)
     return fresh, jnp.swapaxes(traced, 0, 1)[None, None, None]
 
@@ -391,4 +381,5 @@
         P("wide", "sec", "tile", None, None),
     )
     out_specs = (P(None, "wide", "tile", "sec"), P("wide", "sec", "tile", None, None, None))
+
     return jax.shard_map(shards, mesh=mesh, in_specs=in_specs, out_specs=out_specs, check_vma=False)

time: 49.8 us -> 50.8 us (1.020)
  local copies, waits for them, and re-layouts: 2.3 us -> 0.67 us
  waiting for transfers between devices: 5.43 us -> 6.77 us
  other arithmetic: 0 us -> 0.93 us
    unnamed x14 -> x6, local copies, waits for them, and re-layouts: 2.3 us -> 0.67 us
    ppermute x1, waiting for transfers between devices: 0.01 us -> 1.35 us  [shards(): xhi = lax.ppermute(to_low, 'wide', backward)]
    concatenate x0 -> x1, other arithmetic: none -> 0.93 us  [shards(): own = jnp.concatenate([velocity.reshape(3 * CX, CY, CZ), viscosity], 0)]
    all_to_all x1, starting transfers between devices: 4.69 us -> 5.31 us  [shards(): lax.all_to_all(ymsg, 'tile', split_axis=0, concat_axis=0, tiled=True)]
    pallas_call x7 -> x6, Pallas kernels: 4.62 us -> 4.62 us  [the longest x1 1.73 us: shards(): call(main_kernel, (shape(3, CX, CY, CZ), shape(3, SLOTS, CZ), shape(4, LY...]
  transfers between devices with their start and end apart: 5 -> 5, of which waited for: 2 -> 3; matrix products, arithmetic and copies ran while one was open for 0% -> 0% of each run, Pallas kernels for 5% -> 4%
where the time goes in v3:
time: 50.8 us; the launch traced here: 50.4 us
  starting transfers between devices  36.1 us (71%)
  waiting for transfers between devices  6.77 us (13%)
  Pallas kernels  4.62 us (9%)
  between operations  1.38 us (3%)
  other arithmetic  0.93 us (2%)
  local copies, waits for them, and re-layouts  0.67 us (1%)
    ppermute x1, starting transfers between devices, shards(): xhi = lax.ppermute(to_low, 'wide', backward)  17.2 us
    ppermute x1, starting transfers between devices, shards(): zhi = lax.ppermute(zmsg, 'sec', backward)  5.89 us
    ppermute x1, starting transfers between devices, shards(): xlo = lax.ppermute(to_high, 'wide', forward)  5.73 us
    all_to_all x1, starting transfers between devices, shards(): lax.all_to_all(ymsg, 'tile', split_axis=0, concat_axis=0, tiled=True)  5.31 us
    all_to_all x1, waiting for transfers between devices, shards(): lax.all_to_all(ymsg, 'tile', split_axis=0, concat_axis=0, tiled=True)  3.44 us
    ppermute x1, waiting for transfers between devices, shards(): zlo = lax.ppermute(zmsg, 'sec', forward)  1.98 us
    ppermute x1, starting transfers between devices, shards(): zlo = lax.ppermute(zmsg, 'sec', forward)  1.92 us
    pallas_call x1, Pallas kernels, shards(): call(main_kernel, (shape(3, CX, CY, CZ), shape(3, SLOTS, CZ), shape(4, LY...  1.73 us
  transfers between devices with their start and end apart: 5, of which 3 were waited for; matrix products, arithmetic and copies ran while one was open for 0% of the time, Pallas kernels for 4%

profile of v3, /device:TPU:1, one launch (start us, length us, event | category | flops | bytes accessed | tf_op | source)
XLA Modules:
  0.0 50.4 jit_solution(6906114682168978335)
XLA Ops:
  1.3 0.0 copy-start
  1.3 0.9 %pad_maximum_fusion.own = f32[16,16,128]{2,1,0:T(8,128)S(1)} fusion(f32[4,16,128]{2,1,0:T(8,128)} %param.7, f32[12,16,128]{2,1,0:T(8,128)} %bitcast.12), kind=kLoop, calls=%fused_computation | loop fusion | flops 32768 | bytes 262144 | tf_op jit(solution)/shard_map/concatenate | solution.py:334
  2.2 0.0 copy-start.1
  2.2 0.0 copy-start.2
  2.2 0.0 copy-done
  2.3 0.7 %copy-done.1 = s32[1,1,1,4,128]{4,3,2,1,0:T(4,128)S(1)} copy-done((s32[1,1,1,4,128]{4,3,2,1,0:T(4,128)S(1)}, s32[1,1,1,4,128]{4,3,2,1,0:T(4,128)}, u32[]{:S(2)}) %copy-start.1) | copy-done | bytes 2072
  2.9 0.0 copy-done.2
  2.9 0.6 %shard_map.77 = (f32[7,16,128]{2,1,0:T(8,128)S(1)}, f32[7,16,128]{2,1,0:T(8,128)S(1)}, f32[4,64,128]{2,1,0:T(8,128)S(1)}) custom-call(s32[1,1,1]{2,1,0:T(1,128)S(6)} %copy.8.counts, s32[4]{0:T(128)S(1)} %bitcast.11, s32[3,4,128]{2,1,0:T(4,128)S(1)} %bitcast.9, s32[4,128]{1,0:T(4,128)S(1)} %bitcast.10, f32[16,16,128]{2,1,0:T(8,128)S(1)} %pad_maximum_fusion.own), custom_call_target="tpu_custom_call" | custom-call | tf_op jit(solution)/shard_map/pallas_call | solution.py:335
  3.5 5.7 %collective-permute-start = (f32[7,16,128]{2,1,0:T(8,128)S(1)}, f32[7,16,128]{2,1,0:T(8,128)S(1)}, u32[]{:S(2)}, u32[]{:S(2)}) collective-permute-start(f32[7,16,128]{2,1,0:T(8,128)S(1)} %get-tuple-element.12), channel_id=1, source_target_pairs={{0,32},{32,64},{64,96},{96,128},{128,160},{160,192},{192,224},{224... | collective-permute-start | bytes 172040 | tf_op jit(solution)/shard_map/ppermute | solution.py:345
  9.3 17.2 %collective-permute-start.1 = (f32[7,16,128]{2,1,0:T(8,128)S(1)}, f32[7,16,128]{2,1,0:T(8,128)S(1)}, u32[]{:S(2)}, u32[]{:S(2)}) collective-permute-start(f32[7,16,128]{2,1,0:T(8,128)S(1)} %get-tuple-element.13), channel_id=1, source_target_pairs={{32,0},{64,32},{96,64},{128,96},{160,128},{192,160},{224,192},{256... | collective-permute-start | bytes 172040 | tf_op jit(solution)/shard_map/ppermute | solution.py:346
  26.5 0.0 collective-permute-done.xlo
  26.5 1.3 %collective-permute-done.1.xhi = f32[7,16,128]{2,1,0:T(8,128)S(1)} collective-permute-done((f32[7,16,128]{2,1,0:T(8,128)S(1)}, f32[7,16,128]{2,1,0:T(8,128)S(1)}, u32[]{:S(2)}, u32[]{:S(2)}) %collective-permute-start.1) | collective-permute-done | bytes 57376 | tf_op jit(solution)/shard_map/ppermute | solution.py:346
  27.9 0.7 %shard_map.78 = f32[4,64,128]{2,1,0:T(8,128)} custom-call(f32[4,64,128]{2,1,0:T(8,128)S(1)} %get-tuple-element.14.base, f32[7,16,128]{2,1,0:T(8,128)S(1)} %collective-permute-done.xlo, f32[7,16,128]{2,1,0:T(8,128)S(1)} %collective-permute-done.1.xhi), custom_call_target="tpu_custom_call" | custom-call | tf_op jit(solution)/shard_map/pallas_call | solution.py:347
  28.5 5.3 %all-to-all-start = ((f32[4,64,128]{2,1,0:T(8,128)}), f32[4,64,128]{2,1,0:T(8,128)S(1)}, u32[]{:S(2)}, u32[]{:S(2)}) async-start(f32[4,64,128]{2,1,0:T(8,128)} %shard_map.78), calls=%async_computation | async-start | bytes 262144 | tf_op jit(solution)/shard_map/all_to_all | solution.py:348
  33.8 0.1 shard_map.79.zpart
  34.0 3.4 %all-to-all-done.yrecv = f32[4,64,128]{2,1,0:T(8,128)S(1)} async-done(((f32[4,64,128]{2,1,0:T(8,128)}), f32[4,64,128]{2,1,0:T(8,128)S(1)}, u32[]{:S(2)}, u32[]{:S(2)}) %all-to-all-start) | async-done | bytes 131104 | tf_op jit(solution)/shard_map/all_to_all | solution.py:348
  37.4 0.1 shard_map.80
  37.5 5.9 %collective-permute-start.3 = (f32[24,128]{1,0:T(8,128)S(1)}, f32[24,128]{1,0:T(8,128)S(1)}, u32[]{:S(2)}, u32[]{:S(2)}) collective-permute-start(f32[24,128]{1,0:T(8,128)S(1)} %get-tuple-element.17), channel_id=1, source_target_pairs={{4,0},{8,4},{12,8},{16,12},{20,16},{24,20},{28,24},{0,28},{5,1},{9... | collective-permute-start | bytes 36872 | tf_op jit(solution)/shard_map/ppermute | solution.py:355
  43.4 1.9 %collective-permute-start.2 = (f32[24,128]{1,0:T(8,128)S(1)}, f32[24,128]{1,0:T(8,128)S(1)}, u32[]{:S(2)}, u32[]{:S(2)}) collective-permute-start(f32[24,128]{1,0:T(8,128)S(1)} %get-tuple-element.17), channel_id=1, source_target_pairs={{0,4},{4,8},{8,12},{12,16},{16,20},{20,24},{24,28},{28,0},{1,5},{5... | collective-permute-start | bytes 36872 | tf_op jit(solution)/shard_map/ppermute | solution.py:354
  45.3 1.7 %shard_map.81 = (f32[3,4,16,128]{3,2,1,0:T(8,128)S(1)}, f32[3,8,128]{2,1,0:T(8,128)S(1)}, f32[4,24,128]{2,1,0:T(8,128)S(1)}) custom-call(f32[16,16,128]{2,1,0:T(8,128)S(1)} %pad_maximum_fusion.own, f32[7,16,128]{2,1,0:T(8,128)S(1)} %collective-permute-done.xlo, f32[7,16,128]{2,1,0:T(8,128)S(1)} %collective-permute-done.1.xhi, ...), custom_call_target="tpu_custom_call" | custom-call | flops 4194304 | bytes 8388608 | tf_op jit(solution)/shard_map/pallas_call | solution.py:356
  47.1 0.0 collective-permute-done.3.zhi
  47.1 2.0 %collective-permute-done.2.zlo = f32[24,128]{1,0:T(8,128)S(1)} collective-permute-done((f32[24,128]{1,0:T(8,128)S(1)}, f32[24,128]{1,0:T(8,128)S(1)}, u32[]{:S(2)}, u32[]{:S(2)}) %collective-permute-start.2) | collective-permute-done | bytes 12320 | tf_op jit(solution)/shard_map/ppermute | solution.py:354
  49.1 1.4 %shard_map.82 = (f32[3,4,16,128]{3,2,1,0:T(8,128)}, f32[3,8,128]{2,1,0:T(8,128)}) custom-call(f32[4,24,128]{2,1,0:T(8,128)S(1)} %get-tuple-element.16.strip, f32[24,128]{1,0:T(8,128)S(1)} %collective-permute-done.2.zlo, f32[24,128]{1,0:T(8,128)S(1)} %collective-permute-done.3.zhi, f32[4,64,128]{2,1,0:T(8,128)S(1)} %all-to-all-done.yrecv, ...), custom_call_target="tpu_custom_call" | custom-call | tf_op jit(solution)/shard_map/pallas_call | solution.py:368
Async XLA Ops:
  1.3 1.0 %copy-start = (s32[1,1,1,4,3,128]{5,3,4,2,1,0:T(4,128)S(1)}, s32[1,1,1,4,3,128]{5,3,4,2,1,0:T(4,128)}, u32[]{:S(2)}) copy-start(s32[1,1,1,4,3,128]{5,3,4,2,1,0:T(4,128)} %param.10) | copy-start | bytes 18436
  2.2 0.7 %copy-start.1 = (s32[1,1,1,4,128]{4,3,2,1,0:T(4,128)S(1)}, s32[1,1,1,4,128]{4,3,2,1,0:T(4,128)}, u32[]{:S(2)}) copy-start(s32[1,1,1,4,128]{4,3,2,1,0:T(4,128)} %param.11) | copy-start | bytes 6148
  2.2 0.7 %copy-start.2 = (s32[1,1,1,4]{3,2,1,0:T(1,128)S(1)}, s32[1,1,1,4]{3,2,1,0:T(1,128)}, u32[]{:S(2)}) copy-start(s32[1,1,1,4]{3,2,1,0:T(1,128)} %param.9) | copy-start | bytes 52
  3.5 23.0 %collective-permute-start = (f32[7,16,128]{2,1,0:T(8,128)S(1)}, f32[7,16,128]{2,1,0:T(8,128)S(1)}, u32[]{:S(2)}, u32[]{:S(2)}) collective-permute-start(f32[7,16,128]{2,1,0:T(8,128)S(1)} %get-tuple-element.12), channel_id=1, source_target_pairs={{0,32},{32,64},{64,96},{96,128},{128,160},{160,192},{192,224},{224... | collective-permute-start | bytes 172040 | tf_op jit(solution)/shard_map/ppermute | solution.py:345
  9.3 18.6 %collective-permute-start.1 = (f32[7,16,128]{2,1,0:T(8,128)S(1)}, f32[7,16,128]{2,1,0:T(8,128)S(1)}, u32[]{:S(2)}, u32[]{:S(2)}) collective-permute-start(f32[7,16,128]{2,1,0:T(8,128)S(1)} %get-tuple-element.13), channel_id=1, source_target_pairs={{32,0},{64,32},{96,64},{128,96},{160,128},{192,160},{224,192},{256... | collective-permute-start | bytes 172040 | tf_op jit(solution)/shard_map/ppermute | solution.py:346
  28.5 8.9 %all-to-all-start = ((f32[4,64,128]{2,1,0:T(8,128)}), f32[4,64,128]{2,1,0:T(8,128)S(1)}, u32[]{:S(2)}, u32[]{:S(2)}) async-start(f32[4,64,128]{2,1,0:T(8,128)} %shard_map.78), calls=%async_computation | async-start | bytes 262144 | tf_op jit(solution)/shard_map/all_to_all | solution.py:348
  37.5 9.6 %collective-permute-start.3 = (f32[24,128]{1,0:T(8,128)S(1)}, f32[24,128]{1,0:T(8,128)S(1)}, u32[]{:S(2)}, u32[]{:S(2)}) collective-permute-start(f32[24,128]{1,0:T(8,128)S(1)} %get-tuple-element.17), channel_id=1, source_target_pairs={{4,0},{8,4},{12,8},{16,12},{20,16},{24,20},{28,24},{0,28},{5,1},{9... | collective-permute-start | bytes 36872 | tf_op jit(solution)/shard_map/ppermute | solution.py:355
  43.4 5.7 %collective-permute-start.2 = (f32[24,128]{1,0:T(8,128)S(1)}, f32[24,128]{1,0:T(8,128)S(1)}, u32[]{:S(2)}, u32[]{:S(2)}) collective-permute-start(f32[24,128]{1,0:T(8,128)S(1)} %get-tuple-element.17), channel_id=1, source_target_pairs={{0,4},{4,8},{8,12},{12,16},{16,20},{20,24},{24,28},{28,0},{1,5},{5... | collective-permute-start | bytes 36872 | tf_op jit(solution)/shard_map/ppermute | solution.py:354

commit v4 on v3

--- a/solution.py
+++ b/solution.py
@@ -50,13 +50,18 @@
     return 3, group - N_VEL + 1
 
 
-def plane_ref(group, own, xlo, xhi):
+def is_even(axis):
+    return lax.axis_index(axis) % 2 == 0
+
+
+def plane_rows(group, first, size, own, even_first, odd_first):
     comp, x = group_of(group)
-    if x < 2:
-        return xlo.at[2 * comp + x] if comp < 3 else xlo.at[6]
-    if x < 2 + CX:
-        return own.at[CX * comp + x - 2]
-    return xhi.at[2 * comp + x - 2 - CX] if comp < 3 else xhi.at[6]
+    rows = slice(first, first + size)
+    if 2 <= x < 2 + CX:
+        return own[CX * comp + x - 2, rows, :]
+    index = 6 if comp == 3 else 2 * comp + x % 2
+    first_is_odd = is_even("wide") if x < 2 else ~is_even("wide")
+    return jnp.where(first_is_odd, odd_first[index, rows, :], even_first[index, rows, :])
 
 
 def inner(group):
@@ -77,16 +82,19 @@
     return (tile + 1) % TILES, (tile + TILES - 1) % TILES
 
 
-def write_x(own, message, first, edge):
-    for c in range(3):
-        message[2 * c : 2 * c + 2] = own[CX * c + first : CX * c + first + 2]
-    message[6] = own[3 * CX + edge]
-
-
-def prepare_kernel(counts, dest, seeds, substeps, own, to_high, to_low, out):
-    write_x(own, to_high, CX - 2, CX - 1)
-    write_x(own, to_low, 0, 0)
-    live = [b < counts[0, 0, 0] for b in range(BLOCKS)]
+def x_kernel(own, odd_first, even_first):
+    even = is_even("wide")
+    for c in range(4):
+        for k in range(2 if c < 3 else 1):
+            high = own[CX * c + (CX - 2 + k if c < 3 else CX - 1)]
+            low = own[CX * c + k]
+            odd_first[2 * c + k] = jnp.where(even, low, high)
+            even_first[2 * c + k] = jnp.where(even, high, low)
+
+
+def points_kernel(dest, counts, seeds, substeps, own, out):
+    total = jnp.broadcast_to(counts[0], (4, CZ))
+    live = [b < total for b in range(BLOCKS)]
     ranks = []
     for b in range(BLOCKS):
         rank = jnp.int32(0)
@@ -108,20 +116,18 @@
     for g in range(N_ALL):
         if inner(g):
             row, n = halo_rows(g)
-            plane = plane_ref(g, own, None, None)
-            out[up, row : row + n, :] = plane[CY - n : CY, :]
-            out[down, row : row + n, :] = plane[0:n, :]
-
-
-def y_kernel(base, xlo, xhi, out):
+            out[up, row : row + n, :] = plane_rows(g, CY - n, n, own, None, None)
+            out[down, row : row + n, :] = plane_rows(g, 0, n, own, None, None)
+
+
+def y_kernel(base, even_first, odd_first, out):
     out[...] = base[...]
     up, down = next_tiles()
     for g in range(N_ALL):
         if not inner(g):
             row, n = halo_rows(g)
-            plane = plane_ref(g, None, xlo, xhi)
-            out[up, row : row + n, :] = plane[CY - n : CY, :]
-            out[down, row : row + n, :] = plane[0:n, :]
+            out[up, row : row + n, :] = plane_rows(g, CY - n, n, None, even_first, odd_first)
+            out[down, row : row + n, :] = plane_rows(g, 0, n, None, even_first, odd_first)
 
 
 def columns(part, group, lane, acc):
@@ -131,11 +137,11 @@
     return jnp.where((lane >= place) & (lane < place + 4), moved, acc)
 
 
-def z_kernel(own, xlo, xhi, out):
+def z_kernel(own, even_first, odd_first, out):
     lane = lax.broadcasted_iota(jnp.int32, (CY, CZ), 1)
     acc = jnp.zeros((CY, CZ), f32)
     for g in range(N_ALL):
-        acc = columns(plane_ref(g, own, xlo, xhi)[...], g, lane, acc)
+        acc = columns(plane_rows(g, 0, CY, own, even_first, odd_first), g, lane, acc)
     out[...] = acc
 
 
@@ -223,12 +229,12 @@
     return jnp.take_along_axis(table, index, axis=1, mode="promise_in_bounds")
 
 
-def main_kernel(own, xlo, xhi, edges, yrecv, fresh, traced, strip, whole, near, table):
+def main_kernel(own, even_first, odd_first, edges, yrecv, fresh, traced, strip, whole, near, table):
     lane = lax.broadcasted_iota(jnp.int32, (LY, CZ), 1)
     strips = [jnp.zeros((LY, CZ), f32) for _ in range(4)]
     for g in range(N_ALL):
         comp, x = group_of(g)
-        whole[g, 0:CY, :] = plane_ref(g, own, xlo, xhi)[...]
+        whole[g, 0:CY, :] = plane_rows(g, 0, CY, own, even_first, odd_first)
         whole[g, CY:LY, :] = edges[g]
         plane = whole[g]
         place = WIDTH * x
@@ -274,10 +280,12 @@
             traced[i, slot : slot + 1, :] = jnp.sum(jnp.where(here, got, 0.0), 0, keepdims=True)
 
 
-def strip_kernel(strip, zlo, zhi, yrecv, fresh_in, traced_in, fresh, traced):
+def strip_kernel(strip, even_first, odd_first, yrecv, fresh_in, traced_in, fresh, traced):
     lane = lax.broadcasted_iota(jnp.int32, (LY, CZ), 1)
     place = lane % WIDTH
-    low, high = zlo[...], zhi[...]
+    even = is_even("sec")
+    low = jnp.where(even, odd_first[...], even_first[...])
+    high = jnp.where(even, even_first[...], odd_first[...])
     fields = []
     for comp in range(4):
         before = pltpu.roll(low, (CZ - 4 * comp) % CZ, 1)
@@ -325,34 +333,35 @@
 
 
 def shards(velocity, viscosity, counts, destination, seeds, substeps):
-    def ring(axis):
+    def swap(value, axis, first):
         n = lax.axis_size(axis)
-        forward = [(i, (i + 1) % n) for i in range(n)]
-        return forward, [(b, a) for a, b in forward]
+        pairs = [(i, (i + 1) % n) for i in range(first, n, 2)]
+        return lax.ppermute(value, axis, pairs + [(b, a) for a, b in pairs])
 
     message = shape(7, CY, CZ)
     own = jnp.concatenate([velocity.reshape(3 * CX, CY, CZ), viscosity], 0)
-    to_high, to_low, base = call(
-        prepare_kernel, (message, message, shape(TILES, ROWS, CZ)), [SMEM, SMEM] + [VMEM] * 3
+    x_odd, x_even = call(x_kernel, (message, message), [VMEM])(own)
+    x_odd = swap(x_odd, "wide", 1)
+    x_even = swap(x_even, "wide", 0)
+    base = call(
+        points_kernel, shape(TILES, ROWS, CZ), [SMEM] + [VMEM] * 4, flops=1 << 20, moved=1 << 20
     )(
+        destination.reshape(BLOCKS),
         counts,
-        destination.reshape(BLOCKS),
         jnp.swapaxes(seeds.reshape(BLOCKS, 3, CZ), 0, 1),
         substeps.reshape(BLOCKS, CZ),
         own,
     )
-    forward, backward = ring("wide")
-    xlo = lax.ppermute(to_high, "wide", forward)
-    xhi = lax.ppermute(to_low, "wide", backward)
-    ymsg = call(y_kernel, shape(TILES, ROWS, CZ), [VMEM] * 3)(base, xlo, xhi)
+    ymsg = call(y_kernel, shape(TILES, ROWS, CZ), [VMEM] * 3)(base, x_even, x_odd)
     yrecv = lax.all_to_all(ymsg, "tile", split_axis=0, concat_axis=0, tiled=True)
-    zpart = call(z_kernel, shape(CY, CZ), [VMEM] * 3, flops=1 << 20, moved=1 << 20)(own, xlo, xhi)
+    zpart = call(z_kernel, shape(CY, CZ), [VMEM] * 3, flops=1 << 20, moved=1 << 20)(
+        own, x_even, x_odd
+    )
     edges, zmsg = call(
         edge_rows_kernel, (shape(N_ALL, 8, CZ), shape(LY, CZ)), [VMEM] * 2
     )(yrecv, zpart)
-    forward, backward = ring("sec")
-    zlo = lax.ppermute(zmsg, "sec", forward)
-    zhi = lax.ppermute(zmsg, "sec", backward)
+    z_odd = swap(zmsg, "sec", 1)
+    z_even = swap(zmsg, "sec", 0)
     fresh, traced, strip = call(
         main_kernel,
         (shape(3, CX, CY, CZ), shape(3, SLOTS, CZ), shape(4, LY, CZ)),
@@ -364,10 +373,10 @@
         ],
         flops=1 << 22,
         moved=1 << 23,
-    )(own, xlo, xhi, edges, yrecv)
+    )(own, x_even, x_odd, edges, yrecv)
     fresh, traced = call(
         strip_kernel, (shape(3, CX, CY, CZ), shape(3, SLOTS, CZ)), [VMEM] * 6
-    )(strip, zlo, zhi, yrecv, fresh, traced)
+    )(strip, z_even, z_odd, yrecv, fresh, traced)
     return fresh, jnp.swapaxes(traced, 0, 1)[None, None, None]
 
 

time: 50.8 us -> 48.2 us (0.949)
  waiting for transfers between devices: 6.77 us -> 4.21 us
    ppermute x4, waiting for transfers between devices: 3.33 us -> 0.78 us  [swap(): return lax.ppermute(value, axis, pairs + [(b, a) for a, b in pairs])]
    pallas_call x2 -> x3, Pallas kernels: 1.29 us -> 1.35 us  [the longest x1 0.69 us: shards(): call(y_kernel, shape(TILES, ROWS, CZ), [VMEM] * 3)(base, x_even, x_odd)]
  transfers between devices with their start and end apart: 5 -> 5, of which waited for: 3 -> 2; matrix products, arithmetic and copies ran while one was open for 0% -> 0% of each run, Pallas kernels for 4% -> 5%
where the time goes in v4:
time: 48.2 us; the launch traced here: 47.8 us
  starting transfers between devices  36 us (75%)
  Pallas kernels  4.66 us (10%)
  waiting for transfers between devices  4.21 us (9%)
  between operations  1.39 us (3%)
  other arithmetic  0.92 us (2%)
  local copies, waits for them, and re-layouts  0.67 us (1%)
    ppermute x4, starting transfers between devices, swap(): return lax.ppermute(value, axis, pairs + [(b, a) for a, b in pairs])  30.8 us
    all_to_all x1, starting transfers between devices, shards(): lax.all_to_all(ymsg, 'tile', split_axis=0, concat_axis=0, tiled=True)  5.22 us
    all_to_all x1, waiting for transfers between devices, shards(): lax.all_to_all(ymsg, 'tile', split_axis=0, concat_axis=0, tiled=True)  3.43 us
    pallas_call x1, Pallas kernels, shards(): call(main_kernel, (shape(3, CX, CY, CZ), shape(3, SLOTS, CZ), shape(4, LY...  1.73 us
    pallas_call x1, Pallas kernels, shards(): call(strip_kernel, (shape(3, CX, CY, CZ), shape(3, SLOTS, CZ)), [VMEM] * 6)  1.34 us
  transfers between devices with their start and end apart: 5, of which 2 were waited for; matrix products, arithmetic and copies ran while one was open for 0% of the time, Pallas kernels for 5%

profile of v4, /device:TPU:1, one launch (start us, length us, event | category | flops | bytes accessed | tf_op | source)
XLA Modules:
  0.0 47.8 jit_solution(17778701246747354996)
XLA Ops:
  0.6 0.9 %pad_maximum_fusion.own = f32[16,16,128]{2,1,0:T(8,128)S(1)} fusion(f32[4,16,128]{2,1,0:T(8,128)} %param.7, f32[12,16,128]{2,1,0:T(8,128)} %bitcast.12), kind=kLoop, calls=%fused_computation | loop fusion | flops 32768 | bytes 262144 | tf_op jit(solution)/shard_map/concatenate | solution.py:342
  1.6 0.0 copy-start
  1.6 5.7 %collective-permute-start = (f32[7,16,128]{2,1,0:T(8,128)S(1)}, f32[7,16,128]{2,1,0:T(8,128)S(1)}, u32[]{:S(2)}, u32[]{:S(2)}) collective-permute-start(f32[7,16,128]{2,1,0:T(8,128)S(1)} %get-tuple-element.11), channel_id=1, source_target_pairs={{0,32},{64,96},{128,160},{192,224},{256,288},{320,352},{384,416},{... | collective-permute-start | bytes 172040 | tf_op jit(solution)/shard_map/ppermute | solution.py:339
  7.3 17.2 %collective-permute-start.1 = (f32[7,16,128]{2,1,0:T(8,128)S(1)}, f32[7,16,128]{2,1,0:T(8,128)S(1)}, u32[]{:S(2)}, u32[]{:S(2)}) collective-permute-start(f32[7,16,128]{2,1,0:T(8,128)S(1)} %get-tuple-element.12), channel_id=1, source_target_pairs={{32,64},{96,128},{160,192},{224,256},{288,320},{352,384},{416,448}... | collective-permute-start | bytes 172040 | tf_op jit(solution)/shard_map/ppermute | solution.py:339
  25.2 0.0 copy-start.1
  25.2 0.0 copy-start.2
  25.2 0.0 copy-done
  25.2 0.7 %copy-done.1 = s32[1,1,1,4,128]{4,3,2,1,0:T(4,128)S(1)} copy-done((s32[1,1,1,4,128]{4,3,2,1,0:T(4,128)S(1)}, s32[1,1,1,4,128]{4,3,2,1,0:T(4,128)}, u32[]{:S(2)}) %copy-start.1) | copy-done | bytes 2072
  25.9 0.0 copy-done.2
  25.9 0.6 %shard_map.78.base = f32[4,64,128]{2,1,0:T(8,128)S(1)} custom-call(s32[4]{0:T(128)S(1)} %bitcast.11, s32[1,1,1]{2,1,0:T(1,128)S(6)} %copy.8.counts, s32[3,4,128]{2,1,0:T(4,128)S(1)} %bitcast.9, s32[4,128]{1,0:T(4,128)S(1)} %bitcast.10, f32[16,16,128]{2,1,0:T(8,128)S(1)} %pad_maximum_fusion.own), custom_call_target="tpu_custom_call" | custom-call | flops 1048576 | bytes 1048576 | tf_op jit(solution)/shard_map/pallas_call | solution.py:346
  26.5 0.0 collective-permute-done.even_first
  26.6 0.0 collective-permute-done.1.odd_first
  26.6 0.7 %shard_map.79 = f32[4,64,128]{2,1,0:T(8,128)} custom-call(f32[4,64,128]{2,1,0:T(8,128)S(1)} %shard_map.78.base, f32[7,16,128]{2,1,0:T(8,128)S(1)} %collective-permute-done.even_first, f32[7,16,128]{2,1,0:T(8,128)S(1)} %collective-permute-done.1.odd_first), custom_call_target="tpu_custom_call" | custom-call | tf_op jit(solution)/shard_map/pallas_call | solution.py:355
  27.3 5.2 %all-to-all-start = ((f32[4,64,128]{2,1,0:T(8,128)}), f32[4,64,128]{2,1,0:T(8,128)S(1)}, u32[]{:S(2)}, u32[]{:S(2)}) async-start(f32[4,64,128]{2,1,0:T(8,128)} %shard_map.79), calls=%async_computation | async-start | bytes 262144 | tf_op jit(solution)/shard_map/all_to_all | solution.py:356
  32.5 0.1 shard_map.80.zpart
  32.6 3.4 %all-to-all-done.yrecv = f32[4,64,128]{2,1,0:T(8,128)S(1)} async-done(((f32[4,64,128]{2,1,0:T(8,128)}), f32[4,64,128]{2,1,0:T(8,128)S(1)}, u32[]{:S(2)}, u32[]{:S(2)}) %all-to-all-start) | async-done | bytes 131104 | tf_op jit(solution)/shard_map/all_to_all | solution.py:356
  36.0 0.1 shard_map.81
  36.2 5.9 %collective-permute-start.3 = (f32[24,128]{1,0:T(8,128)S(1)}, f32[24,128]{1,0:T(8,128)S(1)}, u32[]{:S(2)}, u32[]{:S(2)}) collective-permute-start(f32[24,128]{1,0:T(8,128)S(1)} %get-tuple-element.15), channel_id=1, source_target_pairs={{4,8},{12,16},{20,24},{28,0},{8,4},{16,12},{24,20},{0,28},{5,9},{1... | collective-permute-start | bytes 36872 | tf_op jit(solution)/shard_map/ppermute | solution.py:339
  42.0 1.9 %collective-permute-start.2 = (f32[24,128]{1,0:T(8,128)S(1)}, f32[24,128]{1,0:T(8,128)S(1)}, u32[]{:S(2)}, u32[]{:S(2)}) collective-permute-start(f32[24,128]{1,0:T(8,128)S(1)} %get-tuple-element.15), channel_id=1, source_target_pairs={{0,4},{8,12},{16,20},{24,28},{4,0},{12,8},{20,16},{28,24},{1,5},{9... | collective-permute-start | bytes 36872 | tf_op jit(solution)/shard_map/ppermute | solution.py:339
  44.0 1.7 %shard_map.82 = (f32[3,4,16,128]{3,2,1,0:T(8,128)S(1)}, f32[3,8,128]{2,1,0:T(8,128)S(1)}, f32[4,24,128]{2,1,0:T(8,128)S(1)}) custom-call(f32[16,16,128]{2,1,0:T(8,128)S(1)} %pad_maximum_fusion.own, f32[7,16,128]{2,1,0:T(8,128)S(1)} %collective-permute-done.even_first, f32[7,16,128]{2,1,0:T(8,128)S(1)} %collective-permute-done.1.odd_first, ...), custom_call_target="tpu_custom_call" | custom-call | flops 4194304 | bytes 8388608 | tf_op jit(solution)/shard_map/pallas_call | solution.py:365
  45.7 0.0 collective-permute-done.3.odd_first
  45.7 0.8 %collective-permute-done.2.even_first = f32[24,128]{1,0:T(8,128)S(1)} collective-permute-done((f32[24,128]{1,0:T(8,128)S(1)}, f32[24,128]{1,0:T(8,128)S(1)}, u32[]{:S(2)}, u32[]{:S(2)}) %collective-permute-start.2) | collective-permute-done | bytes 12320 | tf_op jit(solution)/shard_map/ppermute | solution.py:339
  46.5 1.3 %shard_map.83 = (f32[3,4,16,128]{3,2,1,0:T(8,128)}, f32[3,8,128]{2,1,0:T(8,128)}) custom-call(f32[4,24,128]{2,1,0:T(8,128)S(1)} %get-tuple-element.14.strip, f32[24,128]{1,0:T(8,128)S(1)} %collective-permute-done.2.even_first, f32[24,128]{1,0:T(8,128)S(1)} %collective-permute-done.3.odd_first, f32[4,64,128]{2,1,0:T(8,128)S(1)} %all-to-all-done.yrecv, ...), custom_call_target="tpu_custom_call" | custom-call | tf_op jit(solution)/shard_map/pallas_call | solution.py:377
  (1 shorter events, 0.0 us)
Async XLA Ops:
  1.6 23.7 %copy-start = (s32[1,1,1,4,3,128]{5,3,4,2,1,0:T(4,128)S(1)}, s32[1,1,1,4,3,128]{5,3,4,2,1,0:T(4,128)}, u32[]{:S(2)}) copy-start(s32[1,1,1,4,3,128]{5,3,4,2,1,0:T(4,128)} %param.10) | copy-start | bytes 18436
  1.6 24.9 %collective-permute-start = (f32[7,16,128]{2,1,0:T(8,128)S(1)}, f32[7,16,128]{2,1,0:T(8,128)S(1)}, u32[]{:S(2)}, u32[]{:S(2)}) collective-permute-start(f32[7,16,128]{2,1,0:T(8,128)S(1)} %get-tuple-element.11), channel_id=1, source_target_pairs={{0,32},{64,96},{128,160},{192,224},{256,288},{320,352},{384,416},{... | collective-permute-start | bytes 172040 | tf_op jit(solution)/shard_map/ppermute | solution.py:339
  7.3 19.2 %collective-permute-start.1 = (f32[7,16,128]{2,1,0:T(8,128)S(1)}, f32[7,16,128]{2,1,0:T(8,128)S(1)}, u32[]{:S(2)}, u32[]{:S(2)}) collective-permute-start(f32[7,16,128]{2,1,0:T(8,128)S(1)} %get-tuple-element.12), channel_id=1, source_target_pairs={{32,64},{96,128},{160,192},{224,256},{288,320},{352,384},{416,448}... | collective-permute-start | bytes 172040 | tf_op jit(solution)/shard_map/ppermute | solution.py:339
  25.2 0.7 %copy-start.1 = (s32[1,1,1,4,128]{4,3,2,1,0:T(4,128)S(1)}, s32[1,1,1,4,128]{4,3,2,1,0:T(4,128)}, u32[]{:S(2)}) copy-start(s32[1,1,1,4,128]{4,3,2,1,0:T(4,128)} %param.11) | copy-start | bytes 6148
  25.2 0.7 %copy-start.2 = (s32[1,1,1,4]{3,2,1,0:T(1,128)S(1)}, s32[1,1,1,4]{3,2,1,0:T(1,128)}, u32[]{:S(2)}) copy-start(s32[1,1,1,4]{3,2,1,0:T(1,128)} %param.9) | copy-start | bytes 52
  27.3 8.8 %all-to-all-start = ((f32[4,64,128]{2,1,0:T(8,128)}), f32[4,64,128]{2,1,0:T(8,128)S(1)}, u32[]{:S(2)}, u32[]{:S(2)}) async-start(f32[4,64,128]{2,1,0:T(8,128)} %shard_map.79), calls=%async_computation | async-start | bytes 262144 | tf_op jit(solution)/shard_map/all_to_all | solution.py:356
  36.2 9.5 %collective-permute-start.3 = (f32[24,128]{1,0:T(8,128)S(1)}, f32[24,128]{1,0:T(8,128)S(1)}, u32[]{:S(2)}, u32[]{:S(2)}) collective-permute-start(f32[24,128]{1,0:T(8,128)S(1)} %get-tuple-element.15), channel_id=1, source_target_pairs={{4,8},{12,16},{20,24},{28,0},{8,4},{16,12},{24,20},{0,28},{5,9},{1... | collective-permute-start | bytes 36872 | tf_op jit(solution)/shard_map/ppermute | solution.py:339
  42.0 4.4 %collective-permute-start.2 = (f32[24,128]{1,0:T(8,128)S(1)}, f32[24,128]{1,0:T(8,128)S(1)}, u32[]{:S(2)}, u32[]{:S(2)}) collective-permute-start(f32[24,128]{1,0:T(8,128)S(1)} %get-tuple-element.15), channel_id=1, source_target_pairs={{0,4},{8,12},{16,20},{24,28},{4,0},{12,8},{20,16},{28,24},{1,5},{9... | collective-permute-start | bytes 36872 | tf_op jit(solution)/shard_map/ppermute | solution.py:339

commit v5 on v4

--- a/solution.py
+++ b/solution.py
@@ -19,6 +19,7 @@
 PT_ROW = 56
 ROWS = 64
 WIDTH = CZ // LX
+RUN = 8
 
 flow_step = 0.2
 trace_step = 1.25
@@ -54,14 +55,19 @@
     return lax.axis_index(axis) % 2 == 0
 
 
-def plane_rows(group, first, size, own, even_first, odd_first):
+def of_even_pair(axis, early, late):
+    return jnp.where(lax.axis_index(axis) % RUN < RUN // 2, early, late)
+
+
+def plane_rows(group, first, size, own, early, late, odd):
     comp, x = group_of(group)
     rows = slice(first, first + size)
     if 2 <= x < 2 + CX:
         return own[CX * comp + x - 2, rows, :]
     index = 6 if comp == 3 else 2 * comp + x % 2
-    first_is_odd = is_even("wide") if x < 2 else ~is_even("wide")
-    return jnp.where(first_is_odd, odd_first[index, rows, :], even_first[index, rows, :])
+    from_odd = is_even("wide") if x < 2 else ~is_even("wide")
+    even = of_even_pair("wide", early[index, rows, :], late[index, rows, :])
+    return jnp.where(from_odd, odd[index, rows, :], even)
 
 
 def inner(group):
@@ -116,18 +122,18 @@
     for g in range(N_ALL):
         if inner(g):
             row, n = halo_rows(g)
-            out[up, row : row + n, :] = plane_rows(g, CY - n, n, own, None, None)
-            out[down, row : row + n, :] = plane_rows(g, 0, n, own, None, None)
-
-
-def y_kernel(base, even_first, odd_first, out):
+            out[up, row : row + n, :] = plane_rows(g, CY - n, n, own, None, None, None)
+            out[down, row : row + n, :] = plane_rows(g, 0, n, own, None, None, None)
+
+
+def y_kernel(base, early, late, odd, out):
     out[...] = base[...]
     up, down = next_tiles()
     for g in range(N_ALL):
         if not inner(g):
             row, n = halo_rows(g)
-            out[up, row : row + n, :] = plane_rows(g, CY - n, n, None, even_first, odd_first)
-            out[down, row : row + n, :] = plane_rows(g, 0, n, None, even_first, odd_first)
+            out[up, row : row + n, :] = plane_rows(g, CY - n, n, None, early, late, odd)
+            out[down, row : row + n, :] = plane_rows(g, 0, n, None, early, late, odd)
 
 
 def columns(part, group, lane, acc):
@@ -137,11 +143,11 @@
     return jnp.where((lane >= place) & (lane < place + 4), moved, acc)
 
 
-def z_kernel(own, even_first, odd_first, out):
+def z_kernel(own, early, late, odd, out):
     lane = lax.broadcasted_iota(jnp.int32, (CY, CZ), 1)
     acc = jnp.zeros((CY, CZ), f32)
     for g in range(N_ALL):
-        acc = columns(plane_rows(g, 0, CY, own, even_first, odd_first), g, lane, acc)
+        acc = columns(plane_rows(g, 0, CY, own, early, late, odd), g, lane, acc)
     out[...] = acc
 
 
@@ -229,19 +235,19 @@
     return jnp.take_along_axis(table, index, axis=1, mode="promise_in_bounds")
 
 
-def main_kernel(own, even_first, odd_first, edges, yrecv, fresh, traced, strip, whole, near, table):
+def main_kernel(own, early, late, odd, edges, yrecv, fresh, traced, strip, whole, near, table):
     lane = lax.broadcasted_iota(jnp.int32, (LY, CZ), 1)
     strips = [jnp.zeros((LY, CZ), f32) for _ in range(4)]
     for g in range(N_ALL):
         comp, x = group_of(g)
-        whole[g, 0:CY, :] = plane_rows(g, 0, CY, own, even_first, odd_first)
+        whole[g, 0:CY, :] = plane_rows(g, 0, CY, own, early, late, odd)
         whole[g, CY:LY, :] = edges[g]
         plane = whole[g]
         place = WIDTH * x
-        early = pltpu.roll(plane, (place + 2) % CZ, 1)
-        late = pltpu.roll(plane, (place + 12) % CZ, 1)
-        acc = jnp.where((lane >= place + 2) & (lane < place + 6), early, strips[comp])
-        strips[comp] = jnp.where((lane >= place + 8) & (lane < place + 12), late, acc)
+        start_columns = pltpu.roll(plane, (place + 2) % CZ, 1)
+        end_columns = pltpu.roll(plane, (place + 12) % CZ, 1)
+        acc = jnp.where((lane >= place + 2) & (lane < place + 6), start_columns, strips[comp])
+        strips[comp] = jnp.where((lane >= place + 8) & (lane < place + 12), end_columns, acc)
     for comp in range(4):
         strip[comp] = strips[comp]
 
@@ -280,12 +286,13 @@
             traced[i, slot : slot + 1, :] = jnp.sum(jnp.where(here, got, 0.0), 0, keepdims=True)
 
 
-def strip_kernel(strip, even_first, odd_first, yrecv, fresh_in, traced_in, fresh, traced):
+def strip_kernel(strip, early, late, odd, yrecv, fresh_in, traced_in, fresh, traced):
     lane = lax.broadcasted_iota(jnp.int32, (LY, CZ), 1)
     place = lane % WIDTH
     even = is_even("sec")
-    low = jnp.where(even, odd_first[...], even_first[...])
-    high = jnp.where(even, even_first[...], odd_first[...])
+    from_odd, from_even = odd[...], of_even_pair("sec", early[...], late[...])
+    low = jnp.where(even, from_odd, from_even)
+    high = jnp.where(even, from_even, from_odd)
     fields = []
     for comp in range(4):
         before = pltpu.roll(low, (CZ - 4 * comp) % CZ, 1)
@@ -333,16 +340,21 @@
 
 
 def shards(velocity, viscosity, counts, destination, seeds, substeps):
-    def swap(value, axis, first):
+    def swap(value, axis, kept):
         n = lax.axis_size(axis)
-        pairs = [(i, (i + 1) % n) for i in range(first, n, 2)]
+        pairs = [(i, (i + 1) % n) for i in range(n) if kept(i)]
         return lax.ppermute(value, axis, pairs + [(b, a) for a, b in pairs])
+
+    def exchange(even, odd, axis):
+        early = swap(even, axis, lambda i: i % 2 == 0 and i % RUN < RUN // 2)
+        odd = swap(odd, axis, lambda i: i % 2 == 1)
+        late = swap(even, axis, lambda i: i % 2 == 0 and i % RUN >= RUN // 2)
+        return early, late, odd
 
     message = shape(7, CY, CZ)
     own = jnp.concatenate([velocity.reshape(3 * CX, CY, CZ), viscosity], 0)
     x_odd, x_even = call(x_kernel, (message, message), [VMEM])(own)
-    x_odd = swap(x_odd, "wide", 1)
-    x_even = swap(x_even, "wide", 0)
+    from_x = exchange(x_even, x_odd, "wide")
     base = call(
         points_kernel, shape(TILES, ROWS, CZ), [SMEM] + [VMEM] * 4, flops=1 << 20, moved=1 << 20
     )(
@@ -352,20 +364,17 @@
         substeps.reshape(BLOCKS, CZ),
         own,
     )
-    ymsg = call(y_kernel, shape(TILES, ROWS, CZ), [VMEM] * 3)(base, x_even, x_odd)
+    ymsg = call(y_kernel, shape(TILES, ROWS, CZ), [VMEM] * 4)(base, *from_x)
     yrecv = lax.all_to_all(ymsg, "tile", split_axis=0, concat_axis=0, tiled=True)
-    zpart = call(z_kernel, shape(CY, CZ), [VMEM] * 3, flops=1 << 20, moved=1 << 20)(
-        own, x_even, x_odd
-    )
+    zpart = call(z_kernel, shape(CY, CZ), [VMEM] * 4, flops=1 << 20, moved=1 << 20)(own, *from_x)
     edges, zmsg = call(
         edge_rows_kernel, (shape(N_ALL, 8, CZ), shape(LY, CZ)), [VMEM] * 2
     )(yrecv, zpart)
-    z_odd = swap(zmsg, "sec", 1)
-    z_even = swap(zmsg, "sec", 0)
+    from_z = exchange(zmsg, zmsg, "sec")
     fresh, traced, strip = call(
         main_kernel,
         (shape(3, CX, CY, CZ), shape(3, SLOTS, CZ), shape(4, LY, CZ)),
-        [VMEM] * 5,
+        [VMEM] * 6,
         [
             pltpu.VMEM((N_ALL, LY, CZ), f32),
             pltpu.VMEM((CX + 2, 3, 3, 3, CY, CZ), f32),
@@ -373,10 +382,10 @@
         ],
         flops=1 << 22,
         moved=1 << 23,
-    )(own, x_even, x_odd, edges, yrecv)
+    )(own, *from_x, edges, yrecv)
     fresh, traced = call(
-        strip_kernel, (shape(3, CX, CY, CZ), shape(3, SLOTS, CZ)), [VMEM] * 6
-    )(strip, z_even, z_odd, yrecv, fresh, traced)
+        strip_kernel, (shape(3, CX, CY, CZ), shape(3, SLOTS, CZ)), [VMEM] * 7
+    )(strip, *from_z, yrecv, fresh, traced)
     return fresh, jnp.swapaxes(traced, 0, 1)[None, None, None]
 
 

time: 48.2 us -> 50.8 us (1.054)
  starting transfers between devices: 36 us -> 37.5 us
  waiting for transfers between devices: 4.21 us -> 5.21 us
    ppermute x4 -> x6, starting transfers between devices: 30.8 us -> 32.1 us  [swap(): return lax.ppermute(value, axis, pairs + [(b, a) for a, b in pairs])]
    ppermute x4 -> x6, waiting for transfers between devices: 0.78 us -> 1.78 us  [swap(): return lax.ppermute(value, axis, pairs + [(b, a) for a, b in pairs])]
  transfers between devices with their start and end apart: 5 -> 7, of which waited for: 2 -> 3; matrix products, arithmetic and copies ran while one was open for 0% -> 0% of each run, Pallas kernels for 5% -> 5%
where the time goes in v5:
time: 50.8 us; the launch traced here: 50.3 us
  starting transfers between devices  37.5 us (74%)
  waiting for transfers between devices  5.21 us (10%)
  Pallas kernels  4.64 us (9%)
  between operations  1.42 us (3%)
  other arithmetic  0.92 us (2%)
  local copies, waits for them, and re-layouts  0.67 us (1%)
    ppermute x6, starting transfers between devices, swap(): return lax.ppermute(value, axis, pairs + [(b, a) for a, b in pairs])  32.1 us
    all_to_all x1, starting transfers between devices, shards(): lax.all_to_all(ymsg, 'tile', split_axis=0, concat_axis=0, tiled=True)  5.39 us
    all_to_all x1, waiting for transfers between devices, shards(): lax.all_to_all(ymsg, 'tile', split_axis=0, concat_axis=0, tiled=True)  3.43 us
    ppermute x6, waiting for transfers between devices, swap(): return lax.ppermute(value, axis, pairs + [(b, a) for a, b in pairs])  1.78 us
    pallas_call x1, Pallas kernels, shards(): call(main_kernel, (shape(3, CX, CY, CZ), shape(3, SLOTS, CZ), shape(4, LY...  1.71 us
    pallas_call x1, Pallas kernels, shards(): call(strip_kernel, (shape(3, CX, CY, CZ), shape(3, SLOTS, CZ)), [VMEM] * 7)  1.34 us
  transfers between devices with their start and end apart: 7, of which 3 were waited for; matrix products, arithmetic and copies ran while one was open for 0% of the time, Pallas kernels for 5%

profile of v5, /device:TPU:1, one launch (start us, length us, event | category | flops | bytes accessed | tf_op | source)
XLA Modules:
  0.0 50.3 jit_solution(15722655521013588861)
XLA Ops:
  0.6 0.9 %pad_maximum_fusion.own = f32[16,16,128]{2,1,0:T(8,128)S(1)} fusion(f32[4,16,128]{2,1,0:T(8,128)} %param.7, f32[12,16,128]{2,1,0:T(8,128)} %bitcast.12), kind=kLoop, calls=%fused_computation | loop fusion | flops 32768 | bytes 262144 | tf_op jit(solution)/shard_map/concatenate | solution.py:355
  1.6 0.0 copy-start
  1.6 21.0 %collective-permute-start.2 = (f32[7,16,128]{2,1,0:T(8,128)S(1)}, f32[7,16,128]{2,1,0:T(8,128)S(1)}, u32[]{:S(2)}, u32[]{:S(2)}) collective-permute-start(f32[7,16,128]{2,1,0:T(8,128)S(1)} %get-tuple-element.12), channel_id=1, source_target_pairs={{32,64},{96,128},{160,192},{224,256},{288,320},{352,384},{416,448}... | collective-permute-start | bytes 172040 | tf_op jit(solution)/shard_map/ppermute | solution.py:346
  22.6 0.7 %collective-permute-start.1 = (f32[7,16,128]{2,1,0:T(8,128)S(1)}, f32[7,16,128]{2,1,0:T(8,128)S(1)}, u32[]{:S(2)}, u32[]{:S(2)}) collective-permute-start(f32[7,16,128]{2,1,0:T(8,128)S(1)} %get-tuple-element.11), channel_id=1, source_target_pairs={{128,160},{192,224},{384,416},{448,480},{640,672},{704,736},{896,9... | collective-permute-start | bytes 172040 | tf_op jit(solution)/shard_map/ppermute | solution.py:346
  23.3 1.9 %collective-permute-start = (f32[7,16,128]{2,1,0:T(8,128)S(1)}, f32[7,16,128]{2,1,0:T(8,128)S(1)}, u32[]{:S(2)}, u32[]{:S(2)}) collective-permute-start(f32[7,16,128]{2,1,0:T(8,128)S(1)} %get-tuple-element.11), channel_id=1, source_target_pairs={{0,32},{64,96},{256,288},{320,352},{512,544},{576,608},{768,800},{... | collective-permute-start | bytes 172040 | tf_op jit(solution)/shard_map/ppermute | solution.py:346
  25.9 0.0 copy-start.1
  25.9 0.0 copy-start.2
  25.9 0.7 %copy-done.1 = s32[1,1,1,4,128]{4,3,2,1,0:T(4,128)S(1)} copy-done((s32[1,1,1,4,128]{4,3,2,1,0:T(4,128)S(1)}, s32[1,1,1,4,128]{4,3,2,1,0:T(4,128)}, u32[]{:S(2)}) %copy-start.1) | copy-done | bytes 2072
  26.6 0.6 %shard_map.78.base = f32[4,64,128]{2,1,0:T(8,128)S(1)} custom-call(s32[4]{0:T(128)S(1)} %bitcast.11, s32[1,1,1]{2,1,0:T(1,128)S(6)} %copy.8.counts, s32[3,4,128]{2,1,0:T(4,128)S(1)} %bitcast.9, s32[4,128]{1,0:T(4,128)S(1)} %bitcast.10, f32[16,16,128]{2,1,0:T(8,128)S(1)} %pad_maximum_fusion.own), custom_call_target="tpu_custom_call" | custom-call | flops 1048576 | bytes 1048576 | tf_op jit(solution)/shard_map/pallas_call | solution.py:358
  27.2 0.0 collective-permute-done.2.odd
  27.2 0.0 collective-permute-done.1.late
  27.2 1.0 %collective-permute-done.early = f32[7,16,128]{2,1,0:T(8,128)S(1)} collective-permute-done((f32[7,16,128]{2,1,0:T(8,128)S(1)}, f32[7,16,128]{2,1,0:T(8,128)S(1)}, u32[]{:S(2)}, u32[]{:S(2)}) %collective-permute-start) | collective-permute-done | bytes 57376 | tf_op jit(solution)/shard_map/ppermute | solution.py:346
  28.2 0.7 %shard_map.79 = f32[4,64,128]{2,1,0:T(8,128)} custom-call(f32[4,64,128]{2,1,0:T(8,128)S(1)} %shard_map.78.base, f32[7,16,128]{2,1,0:T(8,128)S(1)} %collective-permute-done.early, f32[7,16,128]{2,1,0:T(8,128)S(1)} %collective-permute-done.1.late, f32[7,16,128]{2,1,0:T(8,128)S(1)} %collective-permute-done.2.odd), custom_call_target="tpu_custom_call" | custom-call | tf_op jit(solution)/shard_map/pallas_call | solution.py:367
  28.9 5.4 %all-to-all-start = ((f32[4,64,128]{2,1,0:T(8,128)}), f32[4,64,128]{2,1,0:T(8,128)S(1)}, u32[]{:S(2)}, u32[]{:S(2)}) async-start(f32[4,64,128]{2,1,0:T(8,128)} %shard_map.79), calls=%async_computation | async-start | bytes 262144 | tf_op jit(solution)/shard_map/all_to_all | solution.py:368
  34.3 0.1 shard_map.80.zpart
  34.4 3.4 %all-to-all-done.yrecv = f32[4,64,128]{2,1,0:T(8,128)S(1)} async-done(((f32[4,64,128]{2,1,0:T(8,128)}), f32[4,64,128]{2,1,0:T(8,128)S(1)}, u32[]{:S(2)}, u32[]{:S(2)}) %all-to-all-start) | async-done | bytes 131104 | tf_op jit(solution)/shard_map/all_to_all | solution.py:368
  37.9 0.1 shard_map.81
  38.0 5.9 %collective-permute-start.5 = (f32[24,128]{1,0:T(8,128)S(1)}, f32[24,128]{1,0:T(8,128)S(1)}, u32[]{:S(2)}, u32[]{:S(2)}) collective-permute-start(f32[24,128]{1,0:T(8,128)S(1)} %get-tuple-element.15), channel_id=1, source_target_pairs={{4,8},{12,16},{20,24},{28,0},{8,4},{16,12},{24,20},{0,28},{5,9},{1... | collective-permute-start | bytes 36872 | tf_op jit(solution)/shard_map/ppermute | solution.py:346
  43.9 0.7 %collective-permute-start.4 = (f32[24,128]{1,0:T(8,128)S(1)}, f32[24,128]{1,0:T(8,128)S(1)}, u32[]{:S(2)}, u32[]{:S(2)}) collective-permute-start(f32[24,128]{1,0:T(8,128)S(1)} %get-tuple-element.15), channel_id=1, source_target_pairs={{16,20},{24,28},{20,16},{28,24},{17,21},{25,29},{21,17},{29,25},{1... | collective-permute-start | bytes 36872 | tf_op jit(solution)/shard_map/ppermute | solution.py:346
  44.6 1.9 %collective-permute-start.3 = (f32[24,128]{1,0:T(8,128)S(1)}, f32[24,128]{1,0:T(8,128)S(1)}, u32[]{:S(2)}, u32[]{:S(2)}) collective-permute-start(f32[24,128]{1,0:T(8,128)S(1)} %get-tuple-element.15), channel_id=1, source_target_pairs={{0,4},{8,12},{4,0},{12,8},{1,5},{9,13},{5,1},{13,9},{2,6},{10,14},... | collective-permute-start | bytes 36872 | tf_op jit(solution)/shard_map/ppermute | solution.py:346
  46.5 1.7 %shard_map.82 = (f32[3,4,16,128]{3,2,1,0:T(8,128)S(1)}, f32[3,8,128]{2,1,0:T(8,128)S(1)}, f32[4,24,128]{2,1,0:T(8,128)S(1)}) custom-call(f32[16,16,128]{2,1,0:T(8,128)S(1)} %pad_maximum_fusion.own, f32[7,16,128]{2,1,0:T(8,128)S(1)} %collective-permute-done.early, f32[7,16,128]{2,1,0:T(8,128)S(1)} %collective-permute-done.1.late, ...), custom_call_target="tpu_custom_call" | custom-call | flops 4194304 | bytes 8388608 | tf_op jit(solution)/shard_map/pallas_call | solution.py:374
  48.2 0.0 collective-permute-done.4.late
  48.2 0.8 %collective-permute-done.3.early = f32[24,128]{1,0:T(8,128)S(1)} collective-permute-done((f32[24,128]{1,0:T(8,128)S(1)}, f32[24,128]{1,0:T(8,128)S(1)}, u32[]{:S(2)}, u32[]{:S(2)}) %collective-permute-start.3) | collective-permute-done | bytes 12320 | tf_op jit(solution)/shard_map/ppermute | solution.py:346
  49.0 1.3 %shard_map.83 = (f32[3,4,16,128]{3,2,1,0:T(8,128)}, f32[3,8,128]{2,1,0:T(8,128)}) custom-call(f32[4,24,128]{2,1,0:T(8,128)S(1)} %get-tuple-element.14.strip, f32[24,128]{1,0:T(8,128)S(1)} %collective-permute-done.3.early, f32[24,128]{1,0:T(8,128)S(1)} %collective-permute-done.4.late, f32[24,128]{1,0:T(8,128)S(1)} %collective-permute-done.5.odd, ...), custom_call_target="tpu_custom_call" | custom-call | tf_op jit(solution)/shard_map/pallas_call | solution.py:386
  (4 shorter events, 0.0 us)
Async XLA Ops:
  1.6 24.3 %copy-start = (s32[1,1,1,4,3,128]{5,3,4,2,1,0:T(4,128)S(1)}, s32[1,1,1,4,3,128]{5,3,4,2,1,0:T(4,128)}, u32[]{:S(2)}) copy-start(s32[1,1,1,4,3,128]{5,3,4,2,1,0:T(4,128)} %param.10) | copy-start | bytes 18436
  1.6 25.6 %collective-permute-start.2 = (f32[7,16,128]{2,1,0:T(8,128)S(1)}, f32[7,16,128]{2,1,0:T(8,128)S(1)}, u32[]{:S(2)}, u32[]{:S(2)}) collective-permute-start(f32[7,16,128]{2,1,0:T(8,128)S(1)} %get-tuple-element.12), channel_id=1, source_target_pairs={{32,64},{96,128},{160,192},{224,256},{288,320},{352,384},{416,448}... | collective-permute-start | bytes 172040 | tf_op jit(solution)/shard_map/ppermute | solution.py:346
  22.6 4.6 %collective-permute-start.1 = (f32[7,16,128]{2,1,0:T(8,128)S(1)}, f32[7,16,128]{2,1,0:T(8,128)S(1)}, u32[]{:S(2)}, u32[]{:S(2)}) collective-permute-start(f32[7,16,128]{2,1,0:T(8,128)S(1)} %get-tuple-element.11), channel_id=1, source_target_pairs={{128,160},{192,224},{384,416},{448,480},{640,672},{704,736},{896,9... | collective-permute-start | bytes 172040 | tf_op jit(solution)/shard_map/ppermute | solution.py:346
  23.3 4.9 %collective-permute-start = (f32[7,16,128]{2,1,0:T(8,128)S(1)}, f32[7,16,128]{2,1,0:T(8,128)S(1)}, u32[]{:S(2)}, u32[]{:S(2)}) collective-permute-start(f32[7,16,128]{2,1,0:T(8,128)S(1)} %get-tuple-element.11), channel_id=1, source_target_pairs={{0,32},{64,96},{256,288},{320,352},{512,544},{576,608},{768,800},{... | collective-permute-start | bytes 172040 | tf_op jit(solution)/shard_map/ppermute | solution.py:346
  25.9 0.7 %copy-start.1 = (s32[1,1,1,4,128]{4,3,2,1,0:T(4,128)S(1)}, s32[1,1,1,4,128]{4,3,2,1,0:T(4,128)}, u32[]{:S(2)}) copy-start(s32[1,1,1,4,128]{4,3,2,1,0:T(4,128)} %param.11) | copy-start | bytes 6148
  25.9 0.7 %copy-start.2 = (s32[1,1,1,4]{3,2,1,0:T(1,128)S(1)}, s32[1,1,1,4]{3,2,1,0:T(1,128)}, u32[]{:S(2)}) copy-start(s32[1,1,1,4]{3,2,1,0:T(1,128)} %param.9) | copy-start | bytes 52
  28.9 9.0 %all-to-all-start = ((f32[4,64,128]{2,1,0:T(8,128)}), f32[4,64,128]{2,1,0:T(8,128)S(1)}, u32[]{:S(2)}, u32[]{:S(2)}) async-start(f32[4,64,128]{2,1,0:T(8,128)} %shard_map.79), calls=%async_computation | async-start | bytes 262144 | tf_op jit(solution)/shard_map/all_to_all | solution.py:368
  38.0 10.2 %collective-permute-start.5 = (f32[24,128]{1,0:T(8,128)S(1)}, f32[24,128]{1,0:T(8,128)S(1)}, u32[]{:S(2)}, u32[]{:S(2)}) collective-permute-start(f32[24,128]{1,0:T(8,128)S(1)} %get-tuple-element.15), channel_id=1, source_target_pairs={{4,8},{12,16},{20,24},{28,0},{8,4},{16,12},{24,20},{0,28},{5,9},{1... | collective-permute-start | bytes 36872 | tf_op jit(solution)/shard_map/ppermute | solution.py:346
  43.9 4.3 %collective-permute-start.4 = (f32[24,128]{1,0:T(8,128)S(1)}, f32[24,128]{1,0:T(8,128)S(1)}, u32[]{:S(2)}, u32[]{:S(2)}) collective-permute-start(f32[24,128]{1,0:T(8,128)S(1)} %get-tuple-element.15), channel_id=1, source_target_pairs={{16,20},{24,28},{20,16},{28,24},{17,21},{25,29},{21,17},{29,25},{1... | collective-permute-start | bytes 36872 | tf_op jit(solution)/shard_map/ppermute | solution.py:346
  44.6 4.4 %collective-permute-start.3 = (f32[24,128]{1,0:T(8,128)S(1)}, f32[24,128]{1,0:T(8,128)S(1)}, u32[]{:S(2)}, u32[]{:S(2)}) collective-permute-start(f32[24,128]{1,0:T(8,128)S(1)} %get-tuple-element.15), channel_id=1, source_target_pairs={{0,4},{8,12},{4,0},{12,8},{1,5},{9,13},{5,1},{13,9},{2,6},{10,14},... | collective-permute-start | bytes 36872 | tf_op jit(solution)/shard_map/ppermute | solution.py:346

commit v6 on v5

--- a/solution.py
+++ b/solution.py
@@ -286,11 +286,11 @@
             traced[i, slot : slot + 1, :] = jnp.sum(jnp.where(here, got, 0.0), 0, keepdims=True)
 
 
-def strip_kernel(strip, early, late, odd, yrecv, fresh_in, traced_in, fresh, traced):
+def strip_kernel(strip, from_even_pair, from_odd_pair, yrecv, fresh_in, traced_in, fresh, traced):
     lane = lax.broadcasted_iota(jnp.int32, (LY, CZ), 1)
     place = lane % WIDTH
     even = is_even("sec")
-    from_odd, from_even = odd[...], of_even_pair("sec", early[...], late[...])
+    from_even, from_odd = from_even_pair[...], from_odd_pair[...]
     low = jnp.where(even, from_odd, from_even)
     high = jnp.where(even, from_even, from_odd)
     fields = []
@@ -345,16 +345,20 @@
         pairs = [(i, (i + 1) % n) for i in range(n) if kept(i)]
         return lax.ppermute(value, axis, pairs + [(b, a) for a, b in pairs])
 
-    def exchange(even, odd, axis):
-        early = swap(even, axis, lambda i: i % 2 == 0 and i % RUN < RUN // 2)
-        odd = swap(odd, axis, lambda i: i % 2 == 1)
-        late = swap(even, axis, lambda i: i % 2 == 0 and i % RUN >= RUN // 2)
+    def exchange_x(even, odd):
+        early = swap(even, "wide", lambda i: i % 2 == 0 and i % RUN < RUN // 2)
+        odd = swap(odd, "wide", lambda i: i % 2 == 1)
+        late = swap(even, "wide", lambda i: i % 2 == 0 and i % RUN >= RUN // 2)
         return early, late, odd
+
+    def exchange_z(message):
+        even = swap(message, "sec", lambda i: i % 2 == 0)
+        return even, swap(message, "sec", lambda i: i % 2 == 1)
 
     message = shape(7, CY, CZ)
     own = jnp.concatenate([velocity.reshape(3 * CX, CY, CZ), viscosity], 0)
     x_odd, x_even = call(x_kernel, (message, message), [VMEM])(own)
-    from_x = exchange(x_even, x_odd, "wide")
+    from_x = exchange_x(x_even, x_odd)
     base = call(
         points_kernel, shape(TILES, ROWS, CZ), [SMEM] + [VMEM] * 4, flops=1 << 20, moved=1 << 20
     )(
@@ -370,7 +374,7 @@
     edges, zmsg = call(
         edge_rows_kernel, (shape(N_ALL, 8, CZ), shape(LY, CZ)), [VMEM] * 2
     )(yrecv, zpart)
-    from_z = exchange(zmsg, zmsg, "sec")
+    from_z = exchange_z(zmsg)
     fresh, traced, strip = call(
         main_kernel,
         (shape(3, CX, CY, CZ), shape(3, SLOTS, CZ), shape(4, LY, CZ)),
@@ -384,7 +388,7 @@
         moved=1 << 23,
     )(own, *from_x, edges, yrecv)
     fresh, traced = call(
-        strip_kernel, (shape(3, CX, CY, CZ), shape(3, SLOTS, CZ)), [VMEM] * 7
+        strip_kernel, (shape(3, CX, CY, CZ), shape(3, SLOTS, CZ)), [VMEM] * 6
     )(strip, *from_z, yrecv, fresh, traced)
     return fresh, jnp.swapaxes(traced, 0, 1)[None, None, None]
 

time: 50.8 us -> 50.1 us (0.986)
  starting transfers between devices: 37.5 us -> 36.8 us
    ppermute x6 -> x5, starting transfers between devices: 32.1 us -> 31.4 us  [swap(): return lax.ppermute(value, axis, pairs + [(b, a) for a, b in pairs])]
    ppermute x6 -> x5, waiting for transfers between devices: 1.78 us -> 1.79 us  [swap(): return lax.ppermute(value, axis, pairs + [(b, a) for a, b in pairs])]
  transfers between devices with their start and end apart: 7 -> 6, of which waited for: 3 -> 3; matrix products, arithmetic and copies ran while one was open for 0% -> 0% of each run, Pallas kernels for 5% -> 5%
where the time goes in v6:
time: 50.1 us; the launch traced here: 49.7 us
  starting transfers between devices  36.8 us (73%)
  waiting for transfers between devices  5.22 us (10%)
  Pallas kernels  4.64 us (9%)
  between operations  1.4 us (3%)
  other arithmetic  0.92 us (2%)
  local copies, waits for them, and re-layouts  0.67 us (1%)
    ppermute x5, starting transfers between devices, swap(): return lax.ppermute(value, axis, pairs + [(b, a) for a, b in pairs])  31.4 us
    all_to_all x1, starting transfers between devices, shards(): lax.all_to_all(ymsg, 'tile', split_axis=0, concat_axis=0, tiled=True)  5.39 us
    all_to_all x1, waiting for transfers between devices, shards(): lax.all_to_all(ymsg, 'tile', split_axis=0, concat_axis=0, tiled=True)  3.43 us
    ppermute x5, waiting for transfers between devices, swap(): return lax.ppermute(value, axis, pairs + [(b, a) for a, b in pairs])  1.79 us
    pallas_call x1, Pallas kernels, shards(): call(main_kernel, (shape(3, CX, CY, CZ), shape(3, SLOTS, CZ), shape(4, LY...  1.71 us
    pallas_call x1, Pallas kernels, shards(): call(strip_kernel, (shape(3, CX, CY, CZ), shape(3, SLOTS, CZ)), [VMEM] * 6)  1.34 us
  transfers between devices with their start and end apart: 6, of which 3 were waited for; matrix products, arithmetic and copies ran while one was open for 0% of the time, Pallas kernels for 5%

profile of v6, /device:TPU:1, one launch (start us, length us, event | category | flops | bytes accessed | tf_op | source)
XLA Modules:
  0.0 49.7 jit_solution(496568167070468759)
XLA Ops:
  0.6 0.9 %pad_maximum_fusion.own = f32[16,16,128]{2,1,0:T(8,128)S(1)} fusion(f32[4,16,128]{2,1,0:T(8,128)} %param.7, f32[12,16,128]{2,1,0:T(8,128)} %bitcast.12), kind=kLoop, calls=%fused_computation | loop fusion | flops 32768 | bytes 262144 | tf_op jit(solution)/shard_map/concatenate | solution.py:359
  1.6 0.0 copy-start
  1.6 21.0 %collective-permute-start.2 = (f32[7,16,128]{2,1,0:T(8,128)S(1)}, f32[7,16,128]{2,1,0:T(8,128)S(1)}, u32[]{:S(2)}, u32[]{:S(2)}) collective-permute-start(f32[7,16,128]{2,1,0:T(8,128)S(1)} %get-tuple-element.12), channel_id=1, source_target_pairs={{32,64},{96,128},{160,192},{224,256},{288,320},{352,384},{416,448}... | collective-permute-start | bytes 172040 | tf_op jit(solution)/shard_map/ppermute | solution.py:346
  22.6 0.7 %collective-permute-start.1 = (f32[7,16,128]{2,1,0:T(8,128)S(1)}, f32[7,16,128]{2,1,0:T(8,128)S(1)}, u32[]{:S(2)}, u32[]{:S(2)}) collective-permute-start(f32[7,16,128]{2,1,0:T(8,128)S(1)} %get-tuple-element.11), channel_id=1, source_target_pairs={{128,160},{192,224},{384,416},{448,480},{640,672},{704,736},{896,9... | collective-permute-start | bytes 172040 | tf_op jit(solution)/shard_map/ppermute | solution.py:346
  23.3 1.9 %collective-permute-start = (f32[7,16,128]{2,1,0:T(8,128)S(1)}, f32[7,16,128]{2,1,0:T(8,128)S(1)}, u32[]{:S(2)}, u32[]{:S(2)}) collective-permute-start(f32[7,16,128]{2,1,0:T(8,128)S(1)} %get-tuple-element.11), channel_id=1, source_target_pairs={{0,32},{64,96},{256,288},{320,352},{512,544},{576,608},{768,800},{... | collective-permute-start | bytes 172040 | tf_op jit(solution)/shard_map/ppermute | solution.py:346
  25.9 0.0 copy-start.1
  25.9 0.0 copy-start.2
  25.9 0.7 %copy-done.1 = s32[1,1,1,4,128]{4,3,2,1,0:T(4,128)S(1)} copy-done((s32[1,1,1,4,128]{4,3,2,1,0:T(4,128)S(1)}, s32[1,1,1,4,128]{4,3,2,1,0:T(4,128)}, u32[]{:S(2)}) %copy-start.1) | copy-done | bytes 2072
  26.6 0.0 copy-done.2
  26.6 0.6 %shard_map.78.base = f32[4,64,128]{2,1,0:T(8,128)S(1)} custom-call(s32[4]{0:T(128)S(1)} %bitcast.11, s32[1,1,1]{2,1,0:T(1,128)S(6)} %copy.8.counts, s32[3,4,128]{2,1,0:T(4,128)S(1)} %bitcast.9, s32[4,128]{1,0:T(4,128)S(1)} %bitcast.10, f32[16,16,128]{2,1,0:T(8,128)S(1)} %pad_maximum_fusion.own), custom_call_target="tpu_custom_call" | custom-call | flops 1048576 | bytes 1048576 | tf_op jit(solution)/shard_map/pallas_call | solution.py:362
  27.2 0.0 collective-permute-done.2.odd
  27.2 0.0 collective-permute-done.1.late
  27.2 1.0 %collective-permute-done.early = f32[7,16,128]{2,1,0:T(8,128)S(1)} collective-permute-done((f32[7,16,128]{2,1,0:T(8,128)S(1)}, f32[7,16,128]{2,1,0:T(8,128)S(1)}, u32[]{:S(2)}, u32[]{:S(2)}) %collective-permute-start) | collective-permute-done | bytes 57376 | tf_op jit(solution)/shard_map/ppermute | solution.py:346
  28.2 0.7 %shard_map.79 = f32[4,64,128]{2,1,0:T(8,128)} custom-call(f32[4,64,128]{2,1,0:T(8,128)S(1)} %shard_map.78.base, f32[7,16,128]{2,1,0:T(8,128)S(1)} %collective-permute-done.early, f32[7,16,128]{2,1,0:T(8,128)S(1)} %collective-permute-done.1.late, f32[7,16,128]{2,1,0:T(8,128)S(1)} %collective-permute-done.2.odd), custom_call_target="tpu_custom_call" | custom-call | tf_op jit(solution)/shard_map/pallas_call | solution.py:371
  28.9 5.4 %all-to-all-start = ((f32[4,64,128]{2,1,0:T(8,128)}), f32[4,64,128]{2,1,0:T(8,128)S(1)}, u32[]{:S(2)}, u32[]{:S(2)}) async-start(f32[4,64,128]{2,1,0:T(8,128)} %shard_map.79), calls=%async_computation | async-start | bytes 262144 | tf_op jit(solution)/shard_map/all_to_all | solution.py:372
  34.3 0.1 shard_map.80.zpart
  34.4 3.4 %all-to-all-done.yrecv = f32[4,64,128]{2,1,0:T(8,128)S(1)} async-done(((f32[4,64,128]{2,1,0:T(8,128)}), f32[4,64,128]{2,1,0:T(8,128)S(1)}, u32[]{:S(2)}, u32[]{:S(2)}) %all-to-all-start) | async-done | bytes 131104 | tf_op jit(solution)/shard_map/all_to_all | solution.py:372
  37.9 0.1 shard_map.81
  38.0 5.9 %collective-permute-start.4 = (f32[24,128]{1,0:T(8,128)S(1)}, f32[24,128]{1,0:T(8,128)S(1)}, u32[]{:S(2)}, u32[]{:S(2)}) collective-permute-start(f32[24,128]{1,0:T(8,128)S(1)} %get-tuple-element.15), channel_id=1, source_target_pairs={{4,8},{12,16},{20,24},{28,0},{8,4},{16,12},{24,20},{0,28},{5,9},{1... | collective-permute-start | bytes 36872 | tf_op jit(solution)/shard_map/ppermute | solution.py:346
  43.9 1.9 %collective-permute-start.3 = (f32[24,128]{1,0:T(8,128)S(1)}, f32[24,128]{1,0:T(8,128)S(1)}, u32[]{:S(2)}, u32[]{:S(2)}) collective-permute-start(f32[24,128]{1,0:T(8,128)S(1)} %get-tuple-element.15), channel_id=1, source_target_pairs={{0,4},{8,12},{16,20},{24,28},{4,0},{12,8},{20,16},{28,24},{1,5},{9... | collective-permute-start | bytes 36872 | tf_op jit(solution)/shard_map/ppermute | solution.py:346
  45.8 1.7 %shard_map.82 = (f32[3,4,16,128]{3,2,1,0:T(8,128)S(1)}, f32[3,8,128]{2,1,0:T(8,128)S(1)}, f32[4,24,128]{2,1,0:T(8,128)S(1)}) custom-call(f32[16,16,128]{2,1,0:T(8,128)S(1)} %pad_maximum_fusion.own, f32[7,16,128]{2,1,0:T(8,128)S(1)} %collective-permute-done.early, f32[7,16,128]{2,1,0:T(8,128)S(1)} %collective-permute-done.1.late, ...), custom_call_target="tpu_custom_call" | custom-call | flops 4194304 | bytes 8388608 | tf_op jit(solution)/shard_map/pallas_call | solution.py:378
  47.5 0.0 collective-permute-done.4.from_odd_pair
  47.5 0.8 %collective-permute-done.3.from_even_pair = f32[24,128]{1,0:T(8,128)S(1)} collective-permute-done((f32[24,128]{1,0:T(8,128)S(1)}, f32[24,128]{1,0:T(8,128)S(1)}, u32[]{:S(2)}, u32[]{:S(2)}) %collective-permute-start.3) | collective-permute-done | bytes 12320 | tf_op jit(solution)/shard_map/ppermute | solution.py:346
  48.3 1.3 %shard_map.83 = (f32[3,4,16,128]{3,2,1,0:T(8,128)}, f32[3,8,128]{2,1,0:T(8,128)}) custom-call(f32[4,24,128]{2,1,0:T(8,128)S(1)} %get-tuple-element.14.strip, f32[24,128]{1,0:T(8,128)S(1)} %collective-permute-done.3.from_even_pair, f32[24,128]{1,0:T(8,128)S(1)} %collective-permute-done.4.from_odd_pair, f32[4,64,128]{2,1,0:T(8,128)S(1)} %all-to-all-done.yrecv, ...), custom_call_target="tpu_custom_call" | custom-call | tf_op jit(solution)/shard_map/pallas_call | solution.py:390
  (2 shorter events, 0.0 us)
Async XLA Ops:
  1.6 24.3 %copy-start = (s32[1,1,1,4,3,128]{5,3,4,2,1,0:T(4,128)S(1)}, s32[1,1,1,4,3,128]{5,3,4,2,1,0:T(4,128)}, u32[]{:S(2)}) copy-start(s32[1,1,1,4,3,128]{5,3,4,2,1,0:T(4,128)} %param.10) | copy-start | bytes 18436
  1.6 25.6 %collective-permute-start.2 = (f32[7,16,128]{2,1,0:T(8,128)S(1)}, f32[7,16,128]{2,1,0:T(8,128)S(1)}, u32[]{:S(2)}, u32[]{:S(2)}) collective-permute-start(f32[7,16,128]{2,1,0:T(8,128)S(1)} %get-tuple-element.12), channel_id=1, source_target_pairs={{32,64},{96,128},{160,192},{224,256},{288,320},{352,384},{416,448}... | collective-permute-start | bytes 172040 | tf_op jit(solution)/shard_map/ppermute | solution.py:346
  22.6 4.6 %collective-permute-start.1 = (f32[7,16,128]{2,1,0:T(8,128)S(1)}, f32[7,16,128]{2,1,0:T(8,128)S(1)}, u32[]{:S(2)}, u32[]{:S(2)}) collective-permute-start(f32[7,16,128]{2,1,0:T(8,128)S(1)} %get-tuple-element.11), channel_id=1, source_target_pairs={{128,160},{192,224},{384,416},{448,480},{640,672},{704,736},{896,9... | collective-permute-start | bytes 172040 | tf_op jit(solution)/shard_map/ppermute | solution.py:346
  23.3 4.9 %collective-permute-start = (f32[7,16,128]{2,1,0:T(8,128)S(1)}, f32[7,16,128]{2,1,0:T(8,128)S(1)}, u32[]{:S(2)}, u32[]{:S(2)}) collective-permute-start(f32[7,16,128]{2,1,0:T(8,128)S(1)} %get-tuple-element.11), channel_id=1, source_target_pairs={{0,32},{64,96},{256,288},{320,352},{512,544},{576,608},{768,800},{... | collective-permute-start | bytes 172040 | tf_op jit(solution)/shard_map/ppermute | solution.py:346
  25.9 0.7 %copy-start.1 = (s32[1,1,1,4,128]{4,3,2,1,0:T(4,128)S(1)}, s32[1,1,1,4,128]{4,3,2,1,0:T(4,128)}, u32[]{:S(2)}) copy-start(s32[1,1,1,4,128]{4,3,2,1,0:T(4,128)} %param.11) | copy-start | bytes 6148
  25.9 0.7 %copy-start.2 = (s32[1,1,1,4]{3,2,1,0:T(1,128)S(1)}, s32[1,1,1,4]{3,2,1,0:T(1,128)}, u32[]{:S(2)}) copy-start(s32[1,1,1,4]{3,2,1,0:T(1,128)} %param.9) | copy-start | bytes 52
  28.9 9.0 %all-to-all-start = ((f32[4,64,128]{2,1,0:T(8,128)}), f32[4,64,128]{2,1,0:T(8,128)S(1)}, u32[]{:S(2)}, u32[]{:S(2)}) async-start(f32[4,64,128]{2,1,0:T(8,128)} %shard_map.79), calls=%async_computation | async-start | bytes 262144 | tf_op jit(solution)/shard_map/all_to_all | solution.py:372
  38.0 9.5 %collective-permute-start.4 = (f32[24,128]{1,0:T(8,128)S(1)}, f32[24,128]{1,0:T(8,128)S(1)}, u32[]{:S(2)}, u32[]{:S(2)}) collective-permute-start(f32[24,128]{1,0:T(8,128)S(1)} %get-tuple-element.15), channel_id=1, source_target_pairs={{4,8},{12,16},{20,24},{28,0},{8,4},{16,12},{24,20},{0,28},{5,9},{1... | collective-permute-start | bytes 36872 | tf_op jit(solution)/shard_map/ppermute | solution.py:346
  43.9 4.4 %collective-permute-start.3 = (f32[24,128]{1,0:T(8,128)S(1)}, f32[24,128]{1,0:T(8,128)S(1)}, u32[]{:S(2)}, u32[]{:S(2)}) collective-permute-start(f32[24,128]{1,0:T(8,128)S(1)} %get-tuple-element.15), channel_id=1, source_target_pairs={{0,4},{8,12},{16,20},{24,28},{4,0},{12,8},{20,16},{28,24},{1,5},{9... | collective-permute-start | bytes 36872 | tf_op jit(solution)/shard_map/ppermute | solution.py:346

commit v7 on v5

--- a/solution.py
+++ b/solution.py
@@ -151,7 +151,7 @@
     out[...] = acc
 
 
-def edge_rows_kernel(yrecv, zpart, edges, zmsg):
+def edge_rows_kernel(yrecv, zpart, edges, z_even, z_odd):
     tile = lax.axis_index("tile")
     below = jnp.maximum(tile - 1, 0)
     above = jnp.minimum(tile + 1, TILES - 1)
@@ -164,8 +164,9 @@
         edge = jnp.concatenate([high, jnp.zeros((8 - 2 * n, CZ), f32), low], 0)
         edges[g] = edge
         acc = columns(edge, g, lane, acc)
-    zmsg[0:CY, :] = zpart[...]
-    zmsg[CY:LY, :] = acc
+    for message in (z_even, z_odd):
+        message[0:CY, :] = zpart[...]
+        message[CY:LY, :] = acc
 
 
 def outside_walls():
@@ -367,10 +368,10 @@
     ymsg = call(y_kernel, shape(TILES, ROWS, CZ), [VMEM] * 4)(base, *from_x)
     yrecv = lax.all_to_all(ymsg, "tile", split_axis=0, concat_axis=0, tiled=True)
     zpart = call(z_kernel, shape(CY, CZ), [VMEM] * 4, flops=1 << 20, moved=1 << 20)(own, *from_x)
-    edges, zmsg = call(
-        edge_rows_kernel, (shape(N_ALL, 8, CZ), shape(LY, CZ)), [VMEM] * 2
+    edges, z_even, z_odd = call(
+        edge_rows_kernel, (shape(N_ALL, 8, CZ), shape(LY, CZ), shape(LY, CZ)), [VMEM] * 2
     )(yrecv, zpart)
-    from_z = exchange(zmsg, zmsg, "sec")
+    from_z = exchange(z_even, z_odd, "sec")
     fresh, traced, strip = call(
         main_kernel,
         (shape(3, CX, CY, CZ), shape(3, SLOTS, CZ), shape(4, LY, CZ)),

time: 50.8 us -> 50.8 us (level)
  no operation moved by 1% of the time
where the time goes in v7:
time: 50.8 us; the launch traced here: 50.3 us
  starting transfers between devices  37.5 us (74%)
  waiting for transfers between devices  5.21 us (10%)
  Pallas kernels  4.64 us (9%)
  between operations  1.42 us (3%)
  other arithmetic  0.92 us (2%)
  local copies, waits for them, and re-layouts  0.67 us (1%)
    ppermute x6, starting transfers between devices, swap(): return lax.ppermute(value, axis, pairs + [(b, a) for a, b in pairs])  32.1 us
    all_to_all x1, starting transfers between devices, shards(): lax.all_to_all(ymsg, 'tile', split_axis=0, concat_axis=0, tiled=True)  5.39 us
    all_to_all x1, waiting for transfers between devices, shards(): lax.all_to_all(ymsg, 'tile', split_axis=0, concat_axis=0, tiled=True)  3.43 us
    ppermute x6, waiting for transfers between devices, swap(): return lax.ppermute(value, axis, pairs + [(b, a) for a, b in pairs])  1.78 us
    pallas_call x1, Pallas kernels, shards(): call(main_kernel, (shape(3, CX, CY, CZ), shape(3, SLOTS, CZ), shape(4, LY...  1.71 us
    pallas_call x1, Pallas kernels, shards(): call(strip_kernel, (shape(3, CX, CY, CZ), shape(3, SLOTS, CZ)), [VMEM] * 7)  1.34 us
  transfers between devices with their start and end apart: 7, of which 3 were waited for; matrix products, arithmetic and copies ran while one was open for 0% of the time, Pallas kernels for 5%

profile of v7, /device:TPU:1, one launch (start us, length us, event | category | flops | bytes accessed | tf_op | source)
XLA Modules:
  0.0 50.3 jit_solution(8915002293822407190)
XLA Ops:
  0.6 0.9 %pad_maximum_fusion.own = f32[16,16,128]{2,1,0:T(8,128)S(1)} fusion(f32[4,16,128]{2,1,0:T(8,128)} %param.7, f32[12,16,128]{2,1,0:T(8,128)} %bitcast.12), kind=kLoop, calls=%fused_computation | loop fusion | flops 32768 | bytes 262144 | tf_op jit(solution)/shard_map/concatenate | solution.py:356
  1.6 0.0 copy-start
  1.6 21.0 %collective-permute-start.2 = (f32[7,16,128]{2,1,0:T(8,128)S(1)}, f32[7,16,128]{2,1,0:T(8,128)S(1)}, u32[]{:S(2)}, u32[]{:S(2)}) collective-permute-start(f32[7,16,128]{2,1,0:T(8,128)S(1)} %get-tuple-element.13), channel_id=1, source_target_pairs={{32,64},{96,128},{160,192},{224,256},{288,320},{352,384},{416,448}... | collective-permute-start | bytes 172040 | tf_op jit(solution)/shard_map/ppermute | solution.py:347
  22.6 0.7 %collective-permute-start.1 = (f32[7,16,128]{2,1,0:T(8,128)S(1)}, f32[7,16,128]{2,1,0:T(8,128)S(1)}, u32[]{:S(2)}, u32[]{:S(2)}) collective-permute-start(f32[7,16,128]{2,1,0:T(8,128)S(1)} %get-tuple-element.12), channel_id=1, source_target_pairs={{128,160},{192,224},{384,416},{448,480},{640,672},{704,736},{896,9... | collective-permute-start | bytes 172040 | tf_op jit(solution)/shard_map/ppermute | solution.py:347
  23.3 1.9 %collective-permute-start = (f32[7,16,128]{2,1,0:T(8,128)S(1)}, f32[7,16,128]{2,1,0:T(8,128)S(1)}, u32[]{:S(2)}, u32[]{:S(2)}) collective-permute-start(f32[7,16,128]{2,1,0:T(8,128)S(1)} %get-tuple-element.12), channel_id=1, source_target_pairs={{0,32},{64,96},{256,288},{320,352},{512,544},{576,608},{768,800},{... | collective-permute-start | bytes 172040 | tf_op jit(solution)/shard_map/ppermute | solution.py:347
  25.9 0.0 copy-start.1
  25.9 0.0 copy-start.2
  25.9 0.7 %copy-done.1 = s32[1,1,1,4,128]{4,3,2,1,0:T(4,128)S(1)} copy-done((s32[1,1,1,4,128]{4,3,2,1,0:T(4,128)S(1)}, s32[1,1,1,4,128]{4,3,2,1,0:T(4,128)}, u32[]{:S(2)}) %copy-start.1) | copy-done | bytes 2072
  26.6 0.6 %shard_map.78.base = f32[4,64,128]{2,1,0:T(8,128)S(1)} custom-call(s32[4]{0:T(128)S(1)} %bitcast.11, s32[1,1,1]{2,1,0:T(1,128)S(6)} %copy.8.counts, s32[3,4,128]{2,1,0:T(4,128)S(1)} %bitcast.9, s32[4,128]{1,0:T(4,128)S(1)} %bitcast.10, f32[16,16,128]{2,1,0:T(8,128)S(1)} %pad_maximum_fusion.own), custom_call_target="tpu_custom_call" | custom-call | flops 1048576 | bytes 1048576 | tf_op jit(solution)/shard_map/pallas_call | solution.py:359
  27.2 0.0 collective-permute-done.2.odd
  27.2 0.0 collective-permute-done.1.late
  27.2 1.0 %collective-permute-done.early = f32[7,16,128]{2,1,0:T(8,128)S(1)} collective-permute-done((f32[7,16,128]{2,1,0:T(8,128)S(1)}, f32[7,16,128]{2,1,0:T(8,128)S(1)}, u32[]{:S(2)}, u32[]{:S(2)}) %collective-permute-start) | collective-permute-done | bytes 57376 | tf_op jit(solution)/shard_map/ppermute | solution.py:347
  28.2 0.7 %shard_map.79 = f32[4,64,128]{2,1,0:T(8,128)} custom-call(f32[4,64,128]{2,1,0:T(8,128)S(1)} %shard_map.78.base, f32[7,16,128]{2,1,0:T(8,128)S(1)} %collective-permute-done.early, f32[7,16,128]{2,1,0:T(8,128)S(1)} %collective-permute-done.1.late, f32[7,16,128]{2,1,0:T(8,128)S(1)} %collective-permute-done.2.odd), custom_call_target="tpu_custom_call" | custom-call | tf_op jit(solution)/shard_map/pallas_call | solution.py:368
  28.9 5.4 %all-to-all-start = ((f32[4,64,128]{2,1,0:T(8,128)}), f32[4,64,128]{2,1,0:T(8,128)S(1)}, u32[]{:S(2)}, u32[]{:S(2)}) async-start(f32[4,64,128]{2,1,0:T(8,128)} %shard_map.79), calls=%async_computation | async-start | bytes 262144 | tf_op jit(solution)/shard_map/all_to_all | solution.py:369
  34.3 0.1 shard_map.80.zpart
  34.4 3.4 %all-to-all-done.yrecv = f32[4,64,128]{2,1,0:T(8,128)S(1)} async-done(((f32[4,64,128]{2,1,0:T(8,128)}), f32[4,64,128]{2,1,0:T(8,128)S(1)}, u32[]{:S(2)}, u32[]{:S(2)}) %all-to-all-start) | async-done | bytes 131104 | tf_op jit(solution)/shard_map/all_to_all | solution.py:369
  37.9 0.1 shard_map.81
  38.0 5.9 %collective-permute-start.5 = (f32[24,128]{1,0:T(8,128)S(1)}, f32[24,128]{1,0:T(8,128)S(1)}, u32[]{:S(2)}, u32[]{:S(2)}) collective-permute-start(f32[24,128]{1,0:T(8,128)S(1)} %get-tuple-element.17), channel_id=1, source_target_pairs={{4,8},{12,16},{20,24},{28,0},{8,4},{16,12},{24,20},{0,28},{5,9},{1... | collective-permute-start | bytes 36872 | tf_op jit(solution)/shard_map/ppermute | solution.py:347
  43.9 0.7 %collective-permute-start.4 = (f32[24,128]{1,0:T(8,128)S(1)}, f32[24,128]{1,0:T(8,128)S(1)}, u32[]{:S(2)}, u32[]{:S(2)}) collective-permute-start(f32[24,128]{1,0:T(8,128)S(1)} %get-tuple-element.16), channel_id=1, source_target_pairs={{16,20},{24,28},{20,16},{28,24},{17,21},{25,29},{21,17},{29,25},{1... | collective-permute-start | bytes 36872 | tf_op jit(solution)/shard_map/ppermute | solution.py:347
  44.6 1.9 %collective-permute-start.3 = (f32[24,128]{1,0:T(8,128)S(1)}, f32[24,128]{1,0:T(8,128)S(1)}, u32[]{:S(2)}, u32[]{:S(2)}) collective-permute-start(f32[24,128]{1,0:T(8,128)S(1)} %get-tuple-element.16), channel_id=1, source_target_pairs={{0,4},{8,12},{4,0},{12,8},{1,5},{9,13},{5,1},{13,9},{2,6},{10,14},... | collective-permute-start | bytes 36872 | tf_op jit(solution)/shard_map/ppermute | solution.py:347
  46.5 1.7 %shard_map.82 = (f32[3,4,16,128]{3,2,1,0:T(8,128)S(1)}, f32[3,8,128]{2,1,0:T(8,128)S(1)}, f32[4,24,128]{2,1,0:T(8,128)S(1)}) custom-call(f32[16,16,128]{2,1,0:T(8,128)S(1)} %pad_maximum_fusion.own, f32[7,16,128]{2,1,0:T(8,128)S(1)} %collective-permute-done.early, f32[7,16,128]{2,1,0:T(8,128)S(1)} %collective-permute-done.1.late, ...), custom_call_target="tpu_custom_call" | custom-call | flops 4194304 | bytes 8388608 | tf_op jit(solution)/shard_map/pallas_call | solution.py:375
  48.2 0.0 collective-permute-done.4.late
  48.2 0.8 %collective-permute-done.3.early = f32[24,128]{1,0:T(8,128)S(1)} collective-permute-done((f32[24,128]{1,0:T(8,128)S(1)}, f32[24,128]{1,0:T(8,128)S(1)}, u32[]{:S(2)}, u32[]{:S(2)}) %collective-permute-start.3) | collective-permute-done | bytes 12320 | tf_op jit(solution)/shard_map/ppermute | solution.py:347
  49.0 1.3 %shard_map.83 = (f32[3,4,16,128]{3,2,1,0:T(8,128)}, f32[3,8,128]{2,1,0:T(8,128)}) custom-call(f32[4,24,128]{2,1,0:T(8,128)S(1)} %get-tuple-element.15.strip, f32[24,128]{1,0:T(8,128)S(1)} %collective-permute-done.3.early, f32[24,128]{1,0:T(8,128)S(1)} %collective-permute-done.4.late, f32[24,128]{1,0:T(8,128)S(1)} %collective-permute-done.5.odd, ...), custom_call_target="tpu_custom_call" | custom-call | tf_op jit(solution)/shard_map/pallas_call | solution.py:387
  (4 shorter events, 0.0 us)
Async XLA Ops:
  1.6 24.3 %copy-start = (s32[1,1,1,4,3,128]{5,3,4,2,1,0:T(4,128)S(1)}, s32[1,1,1,4,3,128]{5,3,4,2,1,0:T(4,128)}, u32[]{:S(2)}) copy-start(s32[1,1,1,4,3,128]{5,3,4,2,1,0:T(4,128)} %param.10) | copy-start | bytes 18436
  1.6 25.6 %collective-permute-start.2 = (f32[7,16,128]{2,1,0:T(8,128)S(1)}, f32[7,16,128]{2,1,0:T(8,128)S(1)}, u32[]{:S(2)}, u32[]{:S(2)}) collective-permute-start(f32[7,16,128]{2,1,0:T(8,128)S(1)} %get-tuple-element.13), channel_id=1, source_target_pairs={{32,64},{96,128},{160,192},{224,256},{288,320},{352,384},{416,448}... | collective-permute-start | bytes 172040 | tf_op jit(solution)/shard_map/ppermute | solution.py:347
  22.6 4.6 %collective-permute-start.1 = (f32[7,16,128]{2,1,0:T(8,128)S(1)}, f32[7,16,128]{2,1,0:T(8,128)S(1)}, u32[]{:S(2)}, u32[]{:S(2)}) collective-permute-start(f32[7,16,128]{2,1,0:T(8,128)S(1)} %get-tuple-element.12), channel_id=1, source_target_pairs={{128,160},{192,224},{384,416},{448,480},{640,672},{704,736},{896,9... | collective-permute-start | bytes 172040 | tf_op jit(solution)/shard_map/ppermute | solution.py:347
  23.3 4.9 %collective-permute-start = (f32[7,16,128]{2,1,0:T(8,128)S(1)}, f32[7,16,128]{2,1,0:T(8,128)S(1)}, u32[]{:S(2)}, u32[]{:S(2)}) collective-permute-start(f32[7,16,128]{2,1,0:T(8,128)S(1)} %get-tuple-element.12), channel_id=1, source_target_pairs={{0,32},{64,96},{256,288},{320,352},{512,544},{576,608},{768,800},{... | collective-permute-start | bytes 172040 | tf_op jit(solution)/shard_map/ppermute | solution.py:347
  25.9 0.7 %copy-start.1 = (s32[1,1,1,4,128]{4,3,2,1,0:T(4,128)S(1)}, s32[1,1,1,4,128]{4,3,2,1,0:T(4,128)}, u32[]{:S(2)}) copy-start(s32[1,1,1,4,128]{4,3,2,1,0:T(4,128)} %param.11) | copy-start | bytes 6148
  25.9 0.7 %copy-start.2 = (s32[1,1,1,4]{3,2,1,0:T(1,128)S(1)}, s32[1,1,1,4]{3,2,1,0:T(1,128)}, u32[]{:S(2)}) copy-start(s32[1,1,1,4]{3,2,1,0:T(1,128)} %param.9) | copy-start | bytes 52
  28.9 9.0 %all-to-all-start = ((f32[4,64,128]{2,1,0:T(8,128)}), f32[4,64,128]{2,1,0:T(8,128)S(1)}, u32[]{:S(2)}, u32[]{:S(2)}) async-start(f32[4,64,128]{2,1,0:T(8,128)} %shard_map.79), calls=%async_computation | async-start | bytes 262144 | tf_op jit(solution)/shard_map/all_to_all | solution.py:369
  38.0 10.2 %collective-permute-start.5 = (f32[24,128]{1,0:T(8,128)S(1)}, f32[24,128]{1,0:T(8,128)S(1)}, u32[]{:S(2)}, u32[]{:S(2)}) collective-permute-start(f32[24,128]{1,0:T(8,128)S(1)} %get-tuple-element.17), channel_id=1, source_target_pairs={{4,8},{12,16},{20,24},{28,0},{8,4},{16,12},{24,20},{0,28},{5,9},{1... | collective-permute-start | bytes 36872 | tf_op jit(solution)/shard_map/ppermute | solution.py:347
  43.9 4.3 %collective-permute-start.4 = (f32[24,128]{1,0:T(8,128)S(1)}, f32[24,128]{1,0:T(8,128)S(1)}, u32[]{:S(2)}, u32[]{:S(2)}) collective-permute-start(f32[24,128]{1,0:T(8,128)S(1)} %get-tuple-element.16), channel_id=1, source_target_pairs={{16,20},{24,28},{20,16},{28,24},{17,21},{25,29},{21,17},{29,25},{1... | collective-permute-start | bytes 36872 | tf_op jit(solution)/shard_map/ppermute | solution.py:347
  44.6 4.4 %collective-permute-start.3 = (f32[24,128]{1,0:T(8,128)S(1)}, f32[24,128]{1,0:T(8,128)S(1)}, u32[]{:S(2)}, u32[]{:S(2)}) collective-permute-start(f32[24,128]{1,0:T(8,128)S(1)} %get-tuple-element.16), channel_id=1, source_target_pairs={{0,4},{8,12},{4,0},{12,8},{1,5},{9,13},{5,1},{13,9},{2,6},{10,14},... | collective-permute-start | bytes 36872 | tf_op jit(solution)/shard_map/ppermute | solution.py:347

commit v8 on v7

--- a/solution.py
+++ b/solution.py
@@ -126,7 +126,7 @@
             out[down, row : row + n, :] = plane_rows(g, 0, n, own, None, None, None)
 
 
-def y_kernel(base, early, late, odd, out):
+def y_kernel(base, early, late, odd, by_3, by_1, by_2, mine, out):
     out[...] = base[...]
     up, down = next_tiles()
     for g in range(N_ALL):
@@ -134,6 +134,11 @@
             row, n = halo_rows(g)
             out[up, row : row + n, :] = plane_rows(g, CY - n, n, None, early, late, odd)
             out[down, row : row + n, :] = plane_rows(g, 0, n, None, early, late, odd)
+    tile = lax.axis_index("tile")
+    by_3[...] = out[TILES - 1 - tile]
+    by_1[...] = out[tile + 1 - 2 * (tile % 2)]
+    by_2[...] = out[(tile + 2) % TILES, PT_ROW:ROWS, :]
+    mine[...] = out[tile, PT_ROW:ROWS, :]
 
 
 def columns(part, group, lane, acc):
@@ -151,16 +156,16 @@
     out[...] = acc
 
 
-def edge_rows_kernel(yrecv, zpart, edges, z_even, z_odd):
+def edge_rows_kernel(by_3, by_1, zpart, edges, z_even, z_odd):
     tile = lax.axis_index("tile")
-    below = jnp.maximum(tile - 1, 0)
-    above = jnp.minimum(tile + 1, TILES - 1)
+    even = is_even("tile")
     lane = lax.broadcasted_iota(jnp.int32, (8, CZ), 1)
     acc = jnp.zeros((8, CZ), f32)
     for g in range(N_ALL):
         row, n = halo_rows(g)
-        high = jnp.where(tile < TILES - 1, yrecv[above, row : row + n, :], 0.0)
-        low = jnp.where(tile > 0, yrecv[below, row : row + n, :], 0.0)
+        near, far = by_1[row : row + n, :], by_3[row : row + n, :]
+        high = jnp.where(tile < TILES - 1, jnp.where(even, near, far), 0.0)
+        low = jnp.where(tile > 0, jnp.where(even, far, near), 0.0)
         edge = jnp.concatenate([high, jnp.zeros((8 - 2 * n, CZ), f32), low], 0)
         edges[g] = edge
         acc = columns(edge, g, lane, acc)
@@ -222,9 +227,9 @@
     ]
 
 
-def points_of(yrecv, slot):
+def points_of(points, slot):
     s, r = divmod(slot, CAP)
-    rows = yrecv[s, PT_ROW + 4 * r : PT_ROW + 4 * r + 4, :].astype(jnp.int32)
+    rows = points[s, 4 * r : 4 * r + 4, :].astype(jnp.int32)
     return [rows[k : k + 1] for k in range(4)]
 
 
@@ -236,7 +241,14 @@
     return jnp.take_along_axis(table, index, axis=1, mode="promise_in_bounds")
 
 
-def main_kernel(own, early, late, odd, edges, yrecv, fresh, traced, strip, whole, near, table):
+def main_kernel(
+    own, early, late, odd, edges, by_3, by_1, by_2, mine, fresh, traced, strip, points, whole, near, table
+):
+    tile = lax.axis_index("tile")
+    for s in range(TILES):
+        part = jnp.where(tile == TILES - 1 - s, by_3[PT_ROW:ROWS, :], mine[...])
+        part = jnp.where(tile == s + 1 - 2 * (s % 2), by_1[PT_ROW:ROWS, :], part)
+        points[s] = jnp.where(tile == (s + 2) % TILES, by_2[...], part)
     lane = lax.broadcasted_iota(jnp.int32, (LY, CZ), 1)
     strips = [jnp.zeros((LY, CZ), f32) for _ in range(4)]
     for g in range(N_ALL):
@@ -277,7 +289,7 @@
 
     rows = lax.broadcasted_iota(jnp.int32, (CX * CY, CZ), 0)
     for slot in range(SLOTS):
-        sx, sy, sz, steps = points_of(yrecv, slot)
+        sx, sy, sz, steps = points_of(points, slot)
         here = (rows == sx * CY + sy) & (steps > 0) & ~at_edge(sz)
         index = jnp.broadcast_to(sz, (8, CZ))
         for i in range(3):
@@ -287,7 +299,7 @@
             traced[i, slot : slot + 1, :] = jnp.sum(jnp.where(here, got, 0.0), 0, keepdims=True)
 
 
-def strip_kernel(strip, early, late, odd, yrecv, fresh_in, traced_in, fresh, traced):
+def strip_kernel(strip, early, late, odd, points, fresh_in, traced_in, fresh, traced):
     lane = lax.broadcasted_iota(jnp.int32, (LY, CZ), 1)
     place = lane % WIDTH
     even = is_even("sec")
@@ -329,7 +341,7 @@
 
     rows = lax.broadcasted_iota(jnp.int32, (CY, CZ), 0)
     for slot in range(SLOTS):
-        sx, sy, sz, steps = points_of(yrecv, slot)
+        sx, sy, sz, steps = points_of(points, slot)
         here = (rows == sy) & (steps > 0) & at_edge(sz)
         offset = jnp.where(sz < 2, sz + 2, sz - (CZ - 2) + 10)
         index = jnp.where(at_edge(sz), WIDTH * (sx + 2) + offset, 0)
@@ -345,6 +357,9 @@
         n = lax.axis_size(axis)
         pairs = [(i, (i + 1) % n) for i in range(n) if kept(i)]
         return lax.ppermute(value, axis, pairs + [(b, a) for a, b in pairs])
+
+    def swap_tiles(value, k):
+        return lax.ppermute(value, "tile", [(i, i ^ k) for i in range(TILES)])
 
     def exchange(even, odd, axis):
         early = swap(even, axis, lambda i: i % 2 == 0 and i % RUN < RUN // 2)
@@ -365,17 +380,27 @@
         substeps.reshape(BLOCKS, CZ),
         own,
     )
-    ymsg = call(y_kernel, shape(TILES, ROWS, CZ), [VMEM] * 4)(base, *from_x)
-    yrecv = lax.all_to_all(ymsg, "tile", split_axis=0, concat_axis=0, tiled=True)
+    messages = (shape(ROWS, CZ), shape(ROWS, CZ), shape(ROWS - PT_ROW, CZ), shape(ROWS - PT_ROW, CZ))
+    to_3, to_1, to_2, mine = call(
+        y_kernel, messages, [VMEM] * 4, [pltpu.VMEM((TILES, ROWS, CZ), f32)]
+    )(base, *from_x)
+    by_3, by_1, by_2 = (
+        swap_tiles(value, k) for value, k in ((to_3, 3), (to_1, 1), (to_2, 2))
+    )
     zpart = call(z_kernel, shape(CY, CZ), [VMEM] * 4, flops=1 << 20, moved=1 << 20)(own, *from_x)
     edges, z_even, z_odd = call(
-        edge_rows_kernel, (shape(N_ALL, 8, CZ), shape(LY, CZ), shape(LY, CZ)), [VMEM] * 2
-    )(yrecv, zpart)
+        edge_rows_kernel, (shape(N_ALL, 8, CZ), shape(LY, CZ), shape(LY, CZ)), [VMEM] * 3
+    )(by_3, by_1, zpart)
     from_z = exchange(z_even, z_odd, "sec")
-    fresh, traced, strip = call(
+    fresh, traced, strip, points = call(
         main_kernel,
-        (shape(3, CX, CY, CZ), shape(3, SLOTS, CZ), shape(4, LY, CZ)),
-        [VMEM] * 6,
+        (
+            shape(3, CX, CY, CZ),
+            shape(3, SLOTS, CZ),
+            shape(4, LY, CZ),
+            shape(TILES, ROWS - PT_ROW, CZ),
+        ),
+        [VMEM] * 9,
         [
             pltpu.VMEM((N_ALL, LY, CZ), f32),
             pltpu.VMEM((CX + 2, 3, 3, 3, CY, CZ), f32),
@@ -383,10 +408,10 @@
         ],
         flops=1 << 22,
         moved=1 << 23,
-    )(own, *from_x, edges, yrecv)
+    )(own, *from_x, edges, by_3, by_1, by_2, mine)
     fresh, traced = call(
         strip_kernel, (shape(3, CX, CY, CZ), shape(3, SLOTS, CZ)), [VMEM] * 7
-    )(strip, *from_z, yrecv, fresh, traced)
+    )(strip, *from_z, points, fresh, traced)
     return fresh, jnp.swapaxes(traced, 0, 1)[None, None, None]
 
 

time: 50.8 us -> 52.5 us (1.033)
  starting transfers between devices: 37.5 us -> 41.3 us
  waiting for transfers between devices: 5.21 us -> 3.31 us
  Pallas kernels: 4.64 us -> 4.05 us
    ppermute x0 -> x3, starting transfers between devices: none -> 9.19 us  [swap_tiles(): return lax.ppermute(value, 'tile', [(i, i ^ k) for i in range(TILES)])]
    all_to_all x1 -> x0, starting transfers between devices: 5.39 us -> none  [shards(): lax.all_to_all(ymsg, 'tile', split_axis=0, concat_axis=0, tiled=True)]
    all_to_all x1 -> x0, waiting for transfers between devices: 3.43 us -> none  [shards(): lax.all_to_all(ymsg, 'tile', split_axis=0, concat_axis=0, tiled=True)]
    ppermute x0 -> x3, waiting for transfers between devices: none -> 2.31 us  [swap_tiles(): return lax.ppermute(value, 'tile', [(i, i ^ k) for i in range(TILES)])]
    ppermute x6, waiting for transfers between devices: 1.78 us -> 1.01 us  [swap(): return lax.ppermute(value, axis, pairs + [(b, a) for a, b in pairs])]
    pallas_call x1, Pallas kernels: 0.68 us -> 0.05 us  [shards(): call(y_kernel, messages, [VMEM] * 4, [pltpu.VMEM((TILES, ROWS, CZ), f32)])]
  transfers between devices with their start and end apart: 7 -> 9, of which waited for: 3 -> 3; matrix products, arithmetic and copies ran while one was open for 0% -> 0% of each run, Pallas kernels for 5% -> 5%
where the time goes in v8:
time: 52.5 us; the launch traced here: 51.7 us
  starting transfers between devices  41.3 us (79%)
  Pallas kernels  4.05 us (8%)
  waiting for transfers between devices  3.31 us (6%)
  between operations  1.45 us (3%)
  other arithmetic  0.92 us (2%)
  local copies, waits for them, and re-layouts  0.67 us (1%)
    ppermute x6, starting transfers between devices, swap(): return lax.ppermute(value, axis, pairs + [(b, a) for a, b in pairs])  32.1 us
    ppermute x3, starting transfers between devices, swap_tiles(): return lax.ppermute(value, 'tile', [(i, i ^ k) for i in range(TILES)])  9.19 us
    ppermute x3, waiting for transfers between devices, swap_tiles(): return lax.ppermute(value, 'tile', [(i, i ^ k) for i in range(TILES)])  2.31 us
    pallas_call x1, Pallas kernels, shards(): call(main_kernel, (shape(3, CX, CY, CZ), shape(3, SLOTS, CZ), shape(4, LY...  1.73 us
    pallas_call x1, Pallas kernels, shards(): call(strip_kernel, (shape(3, CX, CY, CZ), shape(3, SLOTS, CZ)), [VMEM] * 7)  1.36 us
  transfers between devices with their start and end apart: 9, of which 3 were waited for; matrix products, arithmetic and copies ran while one was open for 0% of the time, Pallas kernels for 5%

profile of v8, /device:TPU:1, one launch (start us, length us, event | category | flops | bytes accessed | tf_op | source)
XLA Modules:
  0.0 51.7 jit_solution(11125189499204465751)
XLA Ops:
  0.6 0.9 %pad_maximum_fusion.own = f32[16,16,128]{2,1,0:T(8,128)S(1)} fusion(f32[4,16,128]{2,1,0:T(8,128)} %param.7, f32[12,16,128]{2,1,0:T(8,128)} %bitcast.12), kind=kLoop, calls=%fused_computation | loop fusion | flops 32768 | bytes 262144 | tf_op jit(solution)/shard_map/concatenate | solution.py:371
  1.6 0.0 copy-start
  1.6 21.0 %collective-permute-start.2 = (f32[7,16,128]{2,1,0:T(8,128)S(1)}, f32[7,16,128]{2,1,0:T(8,128)S(1)}, u32[]{:S(2)}, u32[]{:S(2)}) collective-permute-start(f32[7,16,128]{2,1,0:T(8,128)S(1)} %get-tuple-element.18), channel_id=1, source_target_pairs={{32,64},{96,128},{160,192},{224,256},{288,320},{352,384},{416,448}... | collective-permute-start | bytes 172040 | tf_op jit(solution)/shard_map/ppermute | solution.py:359
  22.6 0.7 %collective-permute-start.1 = (f32[7,16,128]{2,1,0:T(8,128)S(1)}, f32[7,16,128]{2,1,0:T(8,128)S(1)}, u32[]{:S(2)}, u32[]{:S(2)}) collective-permute-start(f32[7,16,128]{2,1,0:T(8,128)S(1)} %get-tuple-element.17), channel_id=1, source_target_pairs={{128,160},{192,224},{384,416},{448,480},{640,672},{704,736},{896,9... | collective-permute-start | bytes 172040 | tf_op jit(solution)/shard_map/ppermute | solution.py:359
  23.3 1.9 %collective-permute-start = (f32[7,16,128]{2,1,0:T(8,128)S(1)}, f32[7,16,128]{2,1,0:T(8,128)S(1)}, u32[]{:S(2)}, u32[]{:S(2)}) collective-permute-start(f32[7,16,128]{2,1,0:T(8,128)S(1)} %get-tuple-element.17), channel_id=1, source_target_pairs={{0,32},{64,96},{256,288},{320,352},{512,544},{576,608},{768,800},{... | collective-permute-start | bytes 172040 | tf_op jit(solution)/shard_map/ppermute | solution.py:359
  25.9 0.0 copy-start.1
  25.9 0.0 copy-start.2
  25.9 0.7 %copy-done.1 = s32[1,1,1,4,128]{4,3,2,1,0:T(4,128)S(1)} copy-done((s32[1,1,1,4,128]{4,3,2,1,0:T(4,128)S(1)}, s32[1,1,1,4,128]{4,3,2,1,0:T(4,128)}, u32[]{:S(2)}) %copy-start.1) | copy-done | bytes 2072
  26.6 0.6 %shard_map.78.base = f32[4,64,128]{2,1,0:T(8,128)S(1)} custom-call(s32[4]{0:T(128)S(1)} %bitcast.11, s32[1,1,1]{2,1,0:T(1,128)S(6)} %copy.8.counts, s32[3,4,128]{2,1,0:T(4,128)S(1)} %bitcast.9, s32[4,128]{1,0:T(4,128)S(1)} %bitcast.10, f32[16,16,128]{2,1,0:T(8,128)S(1)} %pad_maximum_fusion.own), custom_call_target="tpu_custom_call" | custom-call | flops 1048576 | bytes 1048576 | tf_op jit(solution)/shard_map/pallas_call | solution.py:374
  27.2 0.0 collective-permute-done.1.late
  27.2 1.0 %collective-permute-done.early = f32[7,16,128]{2,1,0:T(8,128)S(1)} collective-permute-done((f32[7,16,128]{2,1,0:T(8,128)S(1)}, f32[7,16,128]{2,1,0:T(8,128)S(1)}, u32[]{:S(2)}, u32[]{:S(2)}) %collective-permute-start) | collective-permute-done | bytes 57376 | tf_op jit(solution)/shard_map/ppermute | solution.py:359
  28.3 4.2 %collective-permute-start.3 = (f32[64,128]{1,0:T(8,128)S(1)}, f32[64,128]{1,0:T(8,128)S(1)}, u32[]{:S(2)}, u32[]{:S(2)}) collective-permute-start(f32[64,128]{1,0:T(8,128)S(1)} %get-tuple-element.19), channel_id=1, source_target_pairs={{0,3},{1,2},{2,1},{3,0},{4,7},{5,6},{6,5},{7,4},{8,11},{9,10},{10,... | collective-permute-start | bytes 98312 | tf_op jit(solution)/shard_map/ppermute | solution.py:362
  32.5 1.9 %collective-permute-start.4 = (f32[64,128]{1,0:T(8,128)S(1)}, f32[64,128]{1,0:T(8,128)S(1)}, u32[]{:S(2)}, u32[]{:S(2)}) collective-permute-start(f32[64,128]{1,0:T(8,128)S(1)} %get-tuple-element.20), channel_id=1, source_target_pairs={{0,1},{1,0},{2,3},{3,2},{4,5},{5,4},{6,7},{7,6},{8,9},{9,8},{10,11... | collective-permute-start | bytes 98312 | tf_op jit(solution)/shard_map/ppermute | solution.py:362
  34.4 0.1 shard_map.80.zpart
  34.6 0.0 collective-permute-done.3.by_3
  34.6 1.0 %collective-permute-done.4.by_1 = f32[64,128]{1,0:T(8,128)S(1)} collective-permute-done((f32[64,128]{1,0:T(8,128)S(1)}, f32[64,128]{1,0:T(8,128)S(1)}, u32[]{:S(2)}, u32[]{:S(2)}) %collective-permute-start.4) | collective-permute-done | bytes 32800 | tf_op jit(solution)/shard_map/ppermute | solution.py:362
  35.6 0.1 shard_map.81
  35.7 5.9 %collective-permute-start.8 = (f32[24,128]{1,0:T(8,128)S(1)}, f32[24,128]{1,0:T(8,128)S(1)}, u32[]{:S(2)}, u32[]{:S(2)}) collective-permute-start(f32[24,128]{1,0:T(8,128)S(1)} %get-tuple-element.26), channel_id=1, source_target_pairs={{4,8},{12,16},{20,24},{28,0},{8,4},{16,12},{24,20},{0,28},{5,9},{1... | collective-permute-start | bytes 36872 | tf_op jit(solution)/shard_map/ppermute | solution.py:359
  41.6 0.7 %collective-permute-start.7 = (f32[24,128]{1,0:T(8,128)S(1)}, f32[24,128]{1,0:T(8,128)S(1)}, u32[]{:S(2)}, u32[]{:S(2)}) collective-permute-start(f32[24,128]{1,0:T(8,128)S(1)} %get-tuple-element.25), channel_id=1, source_target_pairs={{16,20},{24,28},{20,16},{28,24},{17,21},{25,29},{21,17},{29,25},{1... | collective-permute-start | bytes 36872 | tf_op jit(solution)/shard_map/ppermute | solution.py:359
  42.3 1.9 %collective-permute-start.6 = (f32[24,128]{1,0:T(8,128)S(1)}, f32[24,128]{1,0:T(8,128)S(1)}, u32[]{:S(2)}, u32[]{:S(2)}) collective-permute-start(f32[24,128]{1,0:T(8,128)S(1)} %get-tuple-element.25), channel_id=1, source_target_pairs={{0,4},{8,12},{4,0},{12,8},{1,5},{9,13},{5,1},{13,9},{2,6},{10,14},... | collective-permute-start | bytes 36872 | tf_op jit(solution)/shard_map/ppermute | solution.py:359
  44.2 3.1 %collective-permute-start.5 = (f32[8,128]{1,0:T(8,128)S(1)}, f32[8,128]{1,0:T(8,128)S(1)}, u32[]{:S(2)}, u32[]{:S(2)}) collective-permute-start(f32[8,128]{1,0:T(8,128)S(1)} %get-tuple-element.22), channel_id=1, source_target_pairs={{0,2},{1,3},{2,0},{3,1},{4,6},{5,7},{6,4},{7,5},{8,10},{9,11},{10,... | collective-permute-start | bytes 12296 | tf_op jit(solution)/shard_map/ppermute | solution.py:362
  47.3 1.3 %collective-permute-done.5.by_2 = f32[8,128]{1,0:T(8,128)S(1)} collective-permute-done((f32[8,128]{1,0:T(8,128)S(1)}, f32[8,128]{1,0:T(8,128)S(1)}, u32[]{:S(2)}, u32[]{:S(2)}) %collective-permute-start.5) | collective-permute-done | bytes 4128 | tf_op jit(solution)/shard_map/ppermute | solution.py:362
  48.6 1.7 %shard_map.82 = (f32[3,4,16,128]{3,2,1,0:T(8,128)S(1)}, f32[3,8,128]{2,1,0:T(8,128)S(1)}, f32[4,24,128]{2,1,0:T(8,128)S(1)}, f32[4,8,128]{2,1,0:T(8,128)S(1)}) custom-call(f32[16,16,128]{2,1,0:T(8,128)S(1)} %pad_maximum_fusion.own, f32[7,16,128]{2,1,0:T(8,128)S(1)} %collective-permute-done.early, f32[7,16,128]{2,1,0:T(8,128)S(1)} %collective-permute-done.1.late, ...), custom_call_target="tpu_custom_call" | custom-call | flops 4194304 | bytes 8388608 | tf_op jit(solution)/shard_map/pallas_call | solution.py:395
  50.3 1.4 %shard_map.83 = (f32[3,4,16,128]{3,2,1,0:T(8,128)}, f32[3,8,128]{2,1,0:T(8,128)}) custom-call(f32[4,24,128]{2,1,0:T(8,128)S(1)} %get-tuple-element.24.strip, f32[24,128]{1,0:T(8,128)S(1)} %collective-permute-done.6.early, f32[24,128]{1,0:T(8,128)S(1)} %collective-permute-done.7.late, f32[24,128]{1,0:T(8,128)S(1)} %collective-permute-done.8.odd, ...), custom_call_target="tpu_custom_call" | custom-call | tf_op jit(solution)/shard_map/pallas_call | solution.py:412
  (8 shorter events, 0.1 us)
Async XLA Ops:
  1.6 24.3 %copy-start = (s32[1,1,1,4,3,128]{5,3,4,2,1,0:T(4,128)S(1)}, s32[1,1,1,4,3,128]{5,3,4,2,1,0:T(4,128)}, u32[]{:S(2)}) copy-start(s32[1,1,1,4,3,128]{5,3,4,2,1,0:T(4,128)} %param.10) | copy-start | bytes 18436
  1.6 25.6 %collective-permute-start.2 = (f32[7,16,128]{2,1,0:T(8,128)S(1)}, f32[7,16,128]{2,1,0:T(8,128)S(1)}, u32[]{:S(2)}, u32[]{:S(2)}) collective-permute-start(f32[7,16,128]{2,1,0:T(8,128)S(1)} %get-tuple-element.18), channel_id=1, source_target_pairs={{32,64},{96,128},{160,192},{224,256},{288,320},{352,384},{416,448}... | collective-permute-start | bytes 172040 | tf_op jit(solution)/shard_map/ppermute | solution.py:359
  22.6 4.6 %collective-permute-start.1 = (f32[7,16,128]{2,1,0:T(8,128)S(1)}, f32[7,16,128]{2,1,0:T(8,128)S(1)}, u32[]{:S(2)}, u32[]{:S(2)}) collective-permute-start(f32[7,16,128]{2,1,0:T(8,128)S(1)} %get-tuple-element.17), channel_id=1, source_target_pairs={{128,160},{192,224},{384,416},{448,480},{640,672},{704,736},{896,9... | collective-permute-start | bytes 172040 | tf_op jit(solution)/shard_map/ppermute | solution.py:359
  23.3 4.9 %collective-permute-start = (f32[7,16,128]{2,1,0:T(8,128)S(1)}, f32[7,16,128]{2,1,0:T(8,128)S(1)}, u32[]{:S(2)}, u32[]{:S(2)}) collective-permute-start(f32[7,16,128]{2,1,0:T(8,128)S(1)} %get-tuple-element.17), channel_id=1, source_target_pairs={{0,32},{64,96},{256,288},{320,352},{512,544},{576,608},{768,800},{... | collective-permute-start | bytes 172040 | tf_op jit(solution)/shard_map/ppermute | solution.py:359
  25.9 0.7 %copy-start.1 = (s32[1,1,1,4,128]{4,3,2,1,0:T(4,128)S(1)}, s32[1,1,1,4,128]{4,3,2,1,0:T(4,128)}, u32[]{:S(2)}) copy-start(s32[1,1,1,4,128]{4,3,2,1,0:T(4,128)} %param.11) | copy-start | bytes 6148
  25.9 0.7 %copy-start.2 = (s32[1,1,1,4]{3,2,1,0:T(1,128)S(1)}, s32[1,1,1,4]{3,2,1,0:T(1,128)}, u32[]{:S(2)}) copy-start(s32[1,1,1,4]{3,2,1,0:T(1,128)} %param.9) | copy-start | bytes 52
  28.3 6.3 %collective-permute-start.3 = (f32[64,128]{1,0:T(8,128)S(1)}, f32[64,128]{1,0:T(8,128)S(1)}, u32[]{:S(2)}, u32[]{:S(2)}) collective-permute-start(f32[64,128]{1,0:T(8,128)S(1)} %get-tuple-element.19), channel_id=1, source_target_pairs={{0,3},{1,2},{2,1},{3,0},{4,7},{5,6},{6,5},{7,4},{8,11},{9,10},{10,... | collective-permute-start | bytes 98312 | tf_op jit(solution)/shard_map/ppermute | solution.py:362
  32.5 3.1 %collective-permute-start.4 = (f32[64,128]{1,0:T(8,128)S(1)}, f32[64,128]{1,0:T(8,128)S(1)}, u32[]{:S(2)}, u32[]{:S(2)}) collective-permute-start(f32[64,128]{1,0:T(8,128)S(1)} %get-tuple-element.20), channel_id=1, source_target_pairs={{0,1},{1,0},{2,3},{3,2},{4,5},{5,4},{6,7},{7,6},{8,9},{9,8},{10,11... | collective-permute-start | bytes 98312 | tf_op jit(solution)/shard_map/ppermute | solution.py:362
  35.7 14.6 %collective-permute-start.8 = (f32[24,128]{1,0:T(8,128)S(1)}, f32[24,128]{1,0:T(8,128)S(1)}, u32[]{:S(2)}, u32[]{:S(2)}) collective-permute-start(f32[24,128]{1,0:T(8,128)S(1)} %get-tuple-element.26), channel_id=1, source_target_pairs={{4,8},{12,16},{20,24},{28,0},{8,4},{16,12},{24,20},{0,28},{5,9},{1... | collective-permute-start | bytes 36872 | tf_op jit(solution)/shard_map/ppermute | solution.py:359
  41.6 8.7 %collective-permute-start.7 = (f32[24,128]{1,0:T(8,128)S(1)}, f32[24,128]{1,0:T(8,128)S(1)}, u32[]{:S(2)}, u32[]{:S(2)}) collective-permute-start(f32[24,128]{1,0:T(8,128)S(1)} %get-tuple-element.25), channel_id=1, source_target_pairs={{16,20},{24,28},{20,16},{28,24},{17,21},{25,29},{21,17},{29,25},{1... | collective-permute-start | bytes 36872 | tf_op jit(solution)/shard_map/ppermute | solution.py:359
  42.3 8.0 %collective-permute-start.6 = (f32[24,128]{1,0:T(8,128)S(1)}, f32[24,128]{1,0:T(8,128)S(1)}, u32[]{:S(2)}, u32[]{:S(2)}) collective-permute-start(f32[24,128]{1,0:T(8,128)S(1)} %get-tuple-element.25), channel_id=1, source_target_pairs={{0,4},{8,12},{4,0},{12,8},{1,5},{9,13},{5,1},{13,9},{2,6},{10,14},... | collective-permute-start | bytes 36872 | tf_op jit(solution)/shard_map/ppermute | solution.py:359
  44.2 4.4 %collective-permute-start.5 = (f32[8,128]{1,0:T(8,128)S(1)}, f32[8,128]{1,0:T(8,128)S(1)}, u32[]{:S(2)}, u32[]{:S(2)}) collective-permute-start(f32[8,128]{1,0:T(8,128)S(1)} %get-tuple-element.22), channel_id=1, source_target_pairs={{0,2},{1,3},{2,0},{3,1},{4,6},{5,7},{6,4},{7,5},{8,10},{9,11},{10,... | collective-permute-start | bytes 12296 | tf_op jit(solution)/shard_map/ppermute | solution.py:362

commit v9 on v8

--- a/solution.py
+++ b/solution.py
@@ -55,8 +55,8 @@
     return lax.axis_index(axis) % 2 == 0
 
 
-def of_even_pair(axis, early, late):
-    return jnp.where(lax.axis_index(axis) % RUN < RUN // 2, early, late)
+def of_even_pair(axis, early, late, span=RUN // 2):
+    return jnp.where(lax.axis_index(axis) % RUN < span, early, late)
 
 
 def plane_rows(group, first, size, own, early, late, odd):
@@ -303,7 +303,7 @@
     lane = lax.broadcasted_iota(jnp.int32, (LY, CZ), 1)
     place = lane % WIDTH
     even = is_even("sec")
-    from_odd, from_even = odd[...], of_even_pair("sec", early[...], late[...])
+    from_odd, from_even = odd[...], of_even_pair("sec", early[...], late[...], 2)
     low = jnp.where(even, from_odd, from_even)
     high = jnp.where(even, from_even, from_odd)
     fields = []
@@ -361,10 +361,10 @@
     def swap_tiles(value, k):
         return lax.ppermute(value, "tile", [(i, i ^ k) for i in range(TILES)])
 
-    def exchange(even, odd, axis):
-        early = swap(even, axis, lambda i: i % 2 == 0 and i % RUN < RUN // 2)
+    def exchange(even, odd, axis, span=RUN // 2):
+        early = swap(even, axis, lambda i: i % 2 == 0 and i % RUN < span)
         odd = swap(odd, axis, lambda i: i % 2 == 1)
-        late = swap(even, axis, lambda i: i % 2 == 0 and i % RUN >= RUN // 2)
+        late = swap(even, axis, lambda i: i % 2 == 0 and i % RUN >= span)
         return early, late, odd
 
     message = shape(7, CY, CZ)
@@ -391,7 +391,7 @@
     edges, z_even, z_odd = call(
         edge_rows_kernel, (shape(N_ALL, 8, CZ), shape(LY, CZ), shape(LY, CZ)), [VMEM] * 3
     )(by_3, by_1, zpart)
-    from_z = exchange(z_even, z_odd, "sec")
+    from_z = exchange(z_even, z_odd, "sec", 2)
     fresh, traced, strip, points = call(
         main_kernel,
         (

time: 52.5 us -> 52.5 us (level)
  no operation moved by 1% of the time
where the time goes in v9:
time: 52.5 us; the launch traced here: 51.7 us
  starting transfers between devices  41.3 us (79%)
  Pallas kernels  4.05 us (8%)
  waiting for transfers between devices  3.31 us (6%)
  between operations  1.45 us (3%)
  other arithmetic  0.92 us (2%)
  local copies, waits for them, and re-layouts  0.67 us (1%)
    ppermute x6, starting transfers between devices, swap(): return lax.ppermute(value, axis, pairs + [(b, a) for a, b in pairs])  32.1 us
    ppermute x3, starting transfers between devices, swap_tiles(): return lax.ppermute(value, 'tile', [(i, i ^ k) for i in range(TILES)])  9.19 us
    ppermute x3, waiting for transfers between devices, swap_tiles(): return lax.ppermute(value, 'tile', [(i, i ^ k) for i in range(TILES)])  2.31 us
    pallas_call x1, Pallas kernels, shards(): call(main_kernel, (shape(3, CX, CY, CZ), shape(3, SLOTS, CZ), shape(4, LY...  1.73 us
    pallas_call x1, Pallas kernels, shards(): call(strip_kernel, (shape(3, CX, CY, CZ), shape(3, SLOTS, CZ)), [VMEM] * 7)  1.36 us
  transfers between devices with their start and end apart: 9, of which 3 were waited for; matrix products, arithmetic and copies ran while one was open for 0% of the time, Pallas kernels for 5%

profile of v9, /device:TPU:1, one launch (start us, length us, event | category | flops | bytes accessed | tf_op | source)
XLA Modules:
  0.0 51.7 jit_solution(17382071288208218470)
XLA Ops:
  0.6 0.9 %pad_maximum_fusion.own = f32[16,16,128]{2,1,0:T(8,128)S(1)} fusion(f32[4,16,128]{2,1,0:T(8,128)} %param.7, f32[12,16,128]{2,1,0:T(8,128)} %bitcast.12), kind=kLoop, calls=%fused_computation | loop fusion | flops 32768 | bytes 262144 | tf_op jit(solution)/shard_map/concatenate | solution.py:371
  1.6 0.0 copy-start
  1.6 21.0 %collective-permute-start.2 = (f32[7,16,128]{2,1,0:T(8,128)S(1)}, f32[7,16,128]{2,1,0:T(8,128)S(1)}, u32[]{:S(2)}, u32[]{:S(2)}) collective-permute-start(f32[7,16,128]{2,1,0:T(8,128)S(1)} %get-tuple-element.18), channel_id=1, source_target_pairs={{32,64},{96,128},{160,192},{224,256},{288,320},{352,384},{416,448}... | collective-permute-start | bytes 172040 | tf_op jit(solution)/shard_map/ppermute | solution.py:359
  22.6 0.7 %collective-permute-start.1 = (f32[7,16,128]{2,1,0:T(8,128)S(1)}, f32[7,16,128]{2,1,0:T(8,128)S(1)}, u32[]{:S(2)}, u32[]{:S(2)}) collective-permute-start(f32[7,16,128]{2,1,0:T(8,128)S(1)} %get-tuple-element.17), channel_id=1, source_target_pairs={{128,160},{192,224},{384,416},{448,480},{640,672},{704,736},{896,9... | collective-permute-start | bytes 172040 | tf_op jit(solution)/shard_map/ppermute | solution.py:359
  23.3 1.9 %collective-permute-start = (f32[7,16,128]{2,1,0:T(8,128)S(1)}, f32[7,16,128]{2,1,0:T(8,128)S(1)}, u32[]{:S(2)}, u32[]{:S(2)}) collective-permute-start(f32[7,16,128]{2,1,0:T(8,128)S(1)} %get-tuple-element.17), channel_id=1, source_target_pairs={{0,32},{64,96},{256,288},{320,352},{512,544},{576,608},{768,800},{... | collective-permute-start | bytes 172040 | tf_op jit(solution)/shard_map/ppermute | solution.py:359
  25.9 0.0 copy-start.1
  25.9 0.0 copy-start.2
  25.9 0.7 %copy-done.1 = s32[1,1,1,4,128]{4,3,2,1,0:T(4,128)S(1)} copy-done((s32[1,1,1,4,128]{4,3,2,1,0:T(4,128)S(1)}, s32[1,1,1,4,128]{4,3,2,1,0:T(4,128)}, u32[]{:S(2)}) %copy-start.1) | copy-done | bytes 2072
  26.6 0.6 %shard_map.78.base = f32[4,64,128]{2,1,0:T(8,128)S(1)} custom-call(s32[4]{0:T(128)S(1)} %bitcast.11, s32[1,1,1]{2,1,0:T(1,128)S(6)} %copy.8.counts, s32[3,4,128]{2,1,0:T(4,128)S(1)} %bitcast.9, s32[4,128]{1,0:T(4,128)S(1)} %bitcast.10, f32[16,16,128]{2,1,0:T(8,128)S(1)} %pad_maximum_fusion.own), custom_call_target="tpu_custom_call" | custom-call | flops 1048576 | bytes 1048576 | tf_op jit(solution)/shard_map/pallas_call | solution.py:374
  27.2 0.0 collective-permute-done.1.late
  27.2 1.0 %collective-permute-done.early = f32[7,16,128]{2,1,0:T(8,128)S(1)} collective-permute-done((f32[7,16,128]{2,1,0:T(8,128)S(1)}, f32[7,16,128]{2,1,0:T(8,128)S(1)}, u32[]{:S(2)}, u32[]{:S(2)}) %collective-permute-start) | collective-permute-done | bytes 57376 | tf_op jit(solution)/shard_map/ppermute | solution.py:359
  28.3 4.2 %collective-permute-start.3 = (f32[64,128]{1,0:T(8,128)S(1)}, f32[64,128]{1,0:T(8,128)S(1)}, u32[]{:S(2)}, u32[]{:S(2)}) collective-permute-start(f32[64,128]{1,0:T(8,128)S(1)} %get-tuple-element.19), channel_id=1, source_target_pairs={{0,3},{1,2},{2,1},{3,0},{4,7},{5,6},{6,5},{7,4},{8,11},{9,10},{10,... | collective-permute-start | bytes 98312 | tf_op jit(solution)/shard_map/ppermute | solution.py:362
  32.5 1.9 %collective-permute-start.4 = (f32[64,128]{1,0:T(8,128)S(1)}, f32[64,128]{1,0:T(8,128)S(1)}, u32[]{:S(2)}, u32[]{:S(2)}) collective-permute-start(f32[64,128]{1,0:T(8,128)S(1)} %get-tuple-element.20), channel_id=1, source_target_pairs={{0,1},{1,0},{2,3},{3,2},{4,5},{5,4},{6,7},{7,6},{8,9},{9,8},{10,11... | collective-permute-start | bytes 98312 | tf_op jit(solution)/shard_map/ppermute | solution.py:362
  34.4 0.1 shard_map.80.zpart
  34.6 0.0 collective-permute-done.3.by_3
  34.6 1.0 %collective-permute-done.4.by_1 = f32[64,128]{1,0:T(8,128)S(1)} collective-permute-done((f32[64,128]{1,0:T(8,128)S(1)}, f32[64,128]{1,0:T(8,128)S(1)}, u32[]{:S(2)}, u32[]{:S(2)}) %collective-permute-start.4) | collective-permute-done | bytes 32800 | tf_op jit(solution)/shard_map/ppermute | solution.py:362
  35.6 0.1 shard_map.81
  35.7 5.9 %collective-permute-start.8 = (f32[24,128]{1,0:T(8,128)S(1)}, f32[24,128]{1,0:T(8,128)S(1)}, u32[]{:S(2)}, u32[]{:S(2)}) collective-permute-start(f32[24,128]{1,0:T(8,128)S(1)} %get-tuple-element.26), channel_id=1, source_target_pairs={{4,8},{12,16},{20,24},{28,0},{8,4},{16,12},{24,20},{0,28},{5,9},{1... | collective-permute-start | bytes 36872 | tf_op jit(solution)/shard_map/ppermute | solution.py:359
  41.6 0.7 %collective-permute-start.7 = (f32[24,128]{1,0:T(8,128)S(1)}, f32[24,128]{1,0:T(8,128)S(1)}, u32[]{:S(2)}, u32[]{:S(2)}) collective-permute-start(f32[24,128]{1,0:T(8,128)S(1)} %get-tuple-element.25), channel_id=1, source_target_pairs={{8,12},{16,20},{24,28},{12,8},{20,16},{28,24},{9,13},{17,21},{25,2... | collective-permute-start | bytes 36872 | tf_op jit(solution)/shard_map/ppermute | solution.py:359
  42.3 1.9 %collective-permute-start.6 = (f32[24,128]{1,0:T(8,128)S(1)}, f32[24,128]{1,0:T(8,128)S(1)}, u32[]{:S(2)}, u32[]{:S(2)}) collective-permute-start(f32[24,128]{1,0:T(8,128)S(1)} %get-tuple-element.25), channel_id=1, source_target_pairs={{0,4},{4,0},{1,5},{5,1},{2,6},{6,2},{3,7},{7,3},{32,36},{36,32},{3... | collective-permute-start | bytes 36872 | tf_op jit(solution)/shard_map/ppermute | solution.py:359
  44.2 3.1 %collective-permute-start.5 = (f32[8,128]{1,0:T(8,128)S(1)}, f32[8,128]{1,0:T(8,128)S(1)}, u32[]{:S(2)}, u32[]{:S(2)}) collective-permute-start(f32[8,128]{1,0:T(8,128)S(1)} %get-tuple-element.22), channel_id=1, source_target_pairs={{0,2},{1,3},{2,0},{3,1},{4,6},{5,7},{6,4},{7,5},{8,10},{9,11},{10,... | collective-permute-start | bytes 12296 | tf_op jit(solution)/shard_map/ppermute | solution.py:362
  47.3 1.3 %collective-permute-done.5.by_2 = f32[8,128]{1,0:T(8,128)S(1)} collective-permute-done((f32[8,128]{1,0:T(8,128)S(1)}, f32[8,128]{1,0:T(8,128)S(1)}, u32[]{:S(2)}, u32[]{:S(2)}) %collective-permute-start.5) | collective-permute-done | bytes 4128 | tf_op jit(solution)/shard_map/ppermute | solution.py:362
  48.6 1.7 %shard_map.82 = (f32[3,4,16,128]{3,2,1,0:T(8,128)S(1)}, f32[3,8,128]{2,1,0:T(8,128)S(1)}, f32[4,24,128]{2,1,0:T(8,128)S(1)}, f32[4,8,128]{2,1,0:T(8,128)S(1)}) custom-call(f32[16,16,128]{2,1,0:T(8,128)S(1)} %pad_maximum_fusion.own, f32[7,16,128]{2,1,0:T(8,128)S(1)} %collective-permute-done.early, f32[7,16,128]{2,1,0:T(8,128)S(1)} %collective-permute-done.1.late, ...), custom_call_target="tpu_custom_call" | custom-call | flops 4194304 | bytes 8388608 | tf_op jit(solution)/shard_map/pallas_call | solution.py:395
  50.3 1.4 %shard_map.83 = (f32[3,4,16,128]{3,2,1,0:T(8,128)}, f32[3,8,128]{2,1,0:T(8,128)}) custom-call(f32[4,24,128]{2,1,0:T(8,128)S(1)} %get-tuple-element.24.strip, f32[24,128]{1,0:T(8,128)S(1)} %collective-permute-done.6.early, f32[24,128]{1,0:T(8,128)S(1)} %collective-permute-done.7.late, f32[24,128]{1,0:T(8,128)S(1)} %collective-permute-done.8.odd, ...), custom_call_target="tpu_custom_call" | custom-call | tf_op jit(solution)/shard_map/pallas_call | solution.py:412
  (8 shorter events, 0.1 us)
Async XLA Ops:
  1.6 24.3 %copy-start = (s32[1,1,1,4,3,128]{5,3,4,2,1,0:T(4,128)S(1)}, s32[1,1,1,4,3,128]{5,3,4,2,1,0:T(4,128)}, u32[]{:S(2)}) copy-start(s32[1,1,1,4,3,128]{5,3,4,2,1,0:T(4,128)} %param.10) | copy-start | bytes 18436
  1.6 25.6 %collective-permute-start.2 = (f32[7,16,128]{2,1,0:T(8,128)S(1)}, f32[7,16,128]{2,1,0:T(8,128)S(1)}, u32[]{:S(2)}, u32[]{:S(2)}) collective-permute-start(f32[7,16,128]{2,1,0:T(8,128)S(1)} %get-tuple-element.18), channel_id=1, source_target_pairs={{32,64},{96,128},{160,192},{224,256},{288,320},{352,384},{416,448}... | collective-permute-start | bytes 172040 | tf_op jit(solution)/shard_map/ppermute | solution.py:359
  22.6 4.6 %collective-permute-start.1 = (f32[7,16,128]{2,1,0:T(8,128)S(1)}, f32[7,16,128]{2,1,0:T(8,128)S(1)}, u32[]{:S(2)}, u32[]{:S(2)}) collective-permute-start(f32[7,16,128]{2,1,0:T(8,128)S(1)} %get-tuple-element.17), channel_id=1, source_target_pairs={{128,160},{192,224},{384,416},{448,480},{640,672},{704,736},{896,9... | collective-permute-start | bytes 172040 | tf_op jit(solution)/shard_map/ppermute | solution.py:359
  23.3 4.9 %collective-permute-start = (f32[7,16,128]{2,1,0:T(8,128)S(1)}, f32[7,16,128]{2,1,0:T(8,128)S(1)}, u32[]{:S(2)}, u32[]{:S(2)}) collective-permute-start(f32[7,16,128]{2,1,0:T(8,128)S(1)} %get-tuple-element.17), channel_id=1, source_target_pairs={{0,32},{64,96},{256,288},{320,352},{512,544},{576,608},{768,800},{... | collective-permute-start | bytes 172040 | tf_op jit(solution)/shard_map/ppermute | solution.py:359
  25.9 0.7 %copy-start.1 = (s32[1,1,1,4,128]{4,3,2,1,0:T(4,128)S(1)}, s32[1,1,1,4,128]{4,3,2,1,0:T(4,128)}, u32[]{:S(2)}) copy-start(s32[1,1,1,4,128]{4,3,2,1,0:T(4,128)} %param.11) | copy-start | bytes 6148
  25.9 0.7 %copy-start.2 = (s32[1,1,1,4]{3,2,1,0:T(1,128)S(1)}, s32[1,1,1,4]{3,2,1,0:T(1,128)}, u32[]{:S(2)}) copy-start(s32[1,1,1,4]{3,2,1,0:T(1,128)} %param.9) | copy-start | bytes 52
  28.3 6.3 %collective-permute-start.3 = (f32[64,128]{1,0:T(8,128)S(1)}, f32[64,128]{1,0:T(8,128)S(1)}, u32[]{:S(2)}, u32[]{:S(2)}) collective-permute-start(f32[64,128]{1,0:T(8,128)S(1)} %get-tuple-element.19), channel_id=1, source_target_pairs={{0,3},{1,2},{2,1},{3,0},{4,7},{5,6},{6,5},{7,4},{8,11},{9,10},{10,... | collective-permute-start | bytes 98312 | tf_op jit(solution)/shard_map/ppermute | solution.py:362
  32.5 3.1 %collective-permute-start.4 = (f32[64,128]{1,0:T(8,128)S(1)}, f32[64,128]{1,0:T(8,128)S(1)}, u32[]{:S(2)}, u32[]{:S(2)}) collective-permute-start(f32[64,128]{1,0:T(8,128)S(1)} %get-tuple-element.20), channel_id=1, source_target_pairs={{0,1},{1,0},{2,3},{3,2},{4,5},{5,4},{6,7},{7,6},{8,9},{9,8},{10,11... | collective-permute-start | bytes 98312 | tf_op jit(solution)/shard_map/ppermute | solution.py:362
  35.7 14.6 %collective-permute-start.8 = (f32[24,128]{1,0:T(8,128)S(1)}, f32[24,128]{1,0:T(8,128)S(1)}, u32[]{:S(2)}, u32[]{:S(2)}) collective-permute-start(f32[24,128]{1,0:T(8,128)S(1)} %get-tuple-element.26), channel_id=1, source_target_pairs={{4,8},{12,16},{20,24},{28,0},{8,4},{16,12},{24,20},{0,28},{5,9},{1... | collective-permute-start | bytes 36872 | tf_op jit(solution)/shard_map/ppermute | solution.py:359
  41.6 8.7 %collective-permute-start.7 = (f32[24,128]{1,0:T(8,128)S(1)}, f32[24,128]{1,0:T(8,128)S(1)}, u32[]{:S(2)}, u32[]{:S(2)}) collective-permute-start(f32[24,128]{1,0:T(8,128)S(1)} %get-tuple-element.25), channel_id=1, source_target_pairs={{8,12},{16,20},{24,28},{12,8},{20,16},{28,24},{9,13},{17,21},{25,2... | collective-permute-start | bytes 36872 | tf_op jit(solution)/shard_map/ppermute | solution.py:359
  42.3 8.0 %collective-permute-start.6 = (f32[24,128]{1,0:T(8,128)S(1)}, f32[24,128]{1,0:T(8,128)S(1)}, u32[]{:S(2)}, u32[]{:S(2)}) collective-permute-start(f32[24,128]{1,0:T(8,128)S(1)} %get-tuple-element.25), channel_id=1, source_target_pairs={{0,4},{4,0},{1,5},{5,1},{2,6},{6,2},{3,7},{7,3},{32,36},{36,32},{3... | collective-permute-start | bytes 36872 | tf_op jit(solution)/shard_map/ppermute | solution.py:359
  44.2 4.4 %collective-permute-start.5 = (f32[8,128]{1,0:T(8,128)S(1)}, f32[8,128]{1,0:T(8,128)S(1)}, u32[]{:S(2)}, u32[]{:S(2)}) collective-permute-start(f32[8,128]{1,0:T(8,128)S(1)} %get-tuple-element.22), channel_id=1, source_target_pairs={{0,2},{1,3},{2,0},{3,1},{4,6},{5,7},{6,4},{7,5},{8,10},{9,11},{10,... | collective-permute-start | bytes 12296 | tf_op jit(solution)/shard_map/ppermute | solution.py:362
